TPU v7x, 32 devices: a whole 2x2x4 slice. The times are simulated.
32 devices in a mesh: head: 2 (over core), batch: 16 (over z, y, x).
Axes of the slice: x: 2, y: 2, z: 4, core: 2. Of those that a mesh axis runs over, the one named last changes fastest.
Arguments:
- inputs: bfloat16 [32, 512, 1024], P('batch', 'head'), may hold values from -6 to 6
- prior_scores: bfloat16 [32, 16, 512, 512], P('batch', 'head'), may hold values from -6 to 6
- lengths: int32 [32], P('batch'), may hold values from 65 to 512, as said below
- w_query: bfloat16 [1024, 1024], P(None, 'head'), may hold values from -0.1875 to 0.1875
- w_key: bfloat16 [1024, 1024], P(None, 'head'), may hold values from -0.1875 to 0.1875
- w_value: bfloat16 [1024, 1024], P(None, 'head'), may hold values from -0.1875 to 0.1875
- b_query: bfloat16 [1024], P('head'), may hold values from -3 to 3
- b_value: bfloat16 [1024], P('head'), may hold values from -2 to 2
- w_output: bfloat16 [1024, 1024], P('head'), may hold values from -1.5 to 1.5
- b_output: bfloat16 [1024], replicated, may hold values from -2 to 2
- gain_attn: bfloat16 [1024], replicated, may hold values from 0.5 to 1.5
- shift_attn: bfloat16 [1024], replicated, may hold values from -2 to 2
- w_inner: bfloat16 [1024, 4096], P(None, 'head'), may hold values from -0.1875 to 0.1875
- b_inner: bfloat16 [4096], P('head'), may hold values from -3 to 3
- w_outer: bfloat16 [4096, 1024], P('head'), may hold values from -0.09375 to 0.09375
- b_outer: bfloat16 [1024], replicated, may hold values from -2 to 2
- gain_ffn: bfloat16 [1024], replicated, may hold values from 0.5 to 1.5
- shift_ffn: bfloat16 [1024], replicated, may hold values from -2 to 2
- grad_out: bfloat16 [32, 512, 1024], P('batch', 'head'), may hold values from -6 to 6
- grad_scores: bfloat16 [32, 16, 512, 512], P('batch', 'head'), may hold values from -1.5 to 1.5
Outputs:
- outputs: bfloat16 [32, 512, 1024], P('batch', 'head')
- new_scores: bfloat16 [32, 16, 512, 512], P('batch', 'head')
- grad_inputs: bfloat16 [32, 512, 1024], P('batch', 'head')
- grad_prior: bfloat16 [32, 16, 512, 512], P('batch', 'head')
- grad_w_query: float32 [1024, 1024], P(None, 'head')
- grad_w_key: float32 [1024, 1024], P(None, 'head')
- grad_w_value: float32 [1024, 1024], P(None, 'head')
- grad_b_query: float32 [1024], P('head')
- grad_b_value: float32 [1024], P('head')
- grad_w_output: float32 [1024, 1024], P('head')
- grad_b_output: float32 [1024], replicated
- grad_gain_attn: float32 [1024], replicated
- grad_shift_attn: float32 [1024], replicated
- grad_w_inner: float32 [1024, 4096], P(None, 'head')
- grad_b_inner: float32 [4096], P('head')
- grad_w_outer: float32 [4096, 1024], P('head')
- grad_b_outer: float32 [1024], replicated
- grad_gain_ffn: float32 [1024], replicated
- grad_shift_ffn: float32 [1024], replicated
Inputs may be any that keep to these rules, and one draw needn't show every extreme that they name: The 2 sequences of one index of batch all lie in one bucket B, one of 128, 256 and 512, with lengths from B/2 + 1 to B; some sequence has length 512.
All inputs are finite; a program needn't handle non-finite values.
Results may differ from a plain program's by a relative error of at most 0.018.
Values may be sent and summed in bfloat16 or wider, within the bound.
A program may use at most 256 MiB of HBM per device.

v0:
```python
import jax
import jax.numpy as jnp
from jax import lax
from jax.sharding import PartitionSpec as P

MB = 2


EPS = 1e-12
NEG = -1e30


def layer_norm(values, norm_gain, norm_shift):
    row_mean = jnp.mean(values, axis=-1, keepdims=True)
    centred = values - row_mean
    row_var = jnp.mean(centred * centred, axis=-1, keepdims=True)
    return centred * lax.rsqrt(row_var + EPS) * norm_gain + norm_shift


def project(left_side, right_side):
    return jnp.dot(left_side, right_side, preferred_element_type=jnp.float32)


def project_back(left_side, right_side):
    return jnp.einsum("sla,ba->slb", left_side, right_side, preferred_element_type=jnp.float32)


def outer_sum(left_side, right_side):
    return jnp.einsum("sla,slb->ab", left_side, right_side, preferred_element_type=jnp.float32)


def gelu_slope(inner_pre):
    cdf_part = 0.5 * (1.0 + lax.erf(inner_pre * 0.7071067811865476))
    density = jnp.exp(-0.5 * inner_pre * inner_pre) * 0.3989422804014327
    return cdf_part + inner_pre * density


def masked_scores(query_heads, key_heads, prior_block, live_keys, score_scale):
    raw_scores = jnp.einsum(
        "sqhe,skhe->shqk", query_heads, key_heads, preferred_element_type=jnp.float32
    )
    scores = raw_scores * score_scale + prior_block.astype(jnp.float32)
    masked = jnp.where(live_keys[:, None, None, :], scores, NEG)
    return (scores, masked)


def on_device(
    inputs,
    prior_scores,
    lengths,
    w_query,
    w_key,
    w_value,
    b_query,
    b_value,
    w_output,
    b_output,
    gain_attn,
    shift_attn,
    w_inner,
    b_inner,
    w_outer,
    b_outer,
    gain_ffn,
    shift_ffn,
    grad_out,
    grad_scores,
):
    micro_seqs = inputs.shape[0] // MB
    full_len = prior_scores.shape[-1]
    heads_local = prior_scores.shape[1]
    head_size = w_query.shape[1] // heads_local
    score_scale = head_size ** (-0.5)
    positions = jnp.arange(full_len)
    head_shape = (micro_seqs, full_len, heads_local, head_size)
    bias_query = b_query.astype(jnp.float32)
    bias_value = b_value.astype(jnp.float32)
    bias_output = b_output.astype(jnp.float32)
    bias_inner = b_inner.astype(jnp.float32)
    bias_outer = b_outer.astype(jnp.float32)
    norm_gain_a = gain_attn.astype(jnp.float32)
    norm_shift_a = shift_attn.astype(jnp.float32)
    norm_gain_f = gain_ffn.astype(jnp.float32)
    norm_shift_f = shift_ffn.astype(jnp.float32)
    weight_totals = tuple(
        (
            jnp.zeros(weight.shape, jnp.float32)
            for weight in (
                w_query,
                w_key,
                w_value,
                b_query,
                b_value,
                w_output,
                w_inner,
                b_inner,
                w_outer,
            )
        )
    )
    small_totals = tuple(
        (
            jnp.zeros(weight.shape, jnp.float32)
            for weight in (b_output, gain_attn, shift_attn, b_outer, gain_ffn, shift_ffn)
        )
    )
    out_list, score_list, grad_in_list, grad_prior_list = ([], [], [], [])
    for micro_index in range(MB):
        first_seq = micro_index * micro_seqs
        inputs_mb = inputs[first_seq : first_seq + micro_seqs]
        prior_mb = prior_scores[first_seq : first_seq + micro_seqs]
        live_keys = positions[None, :] < lengths[first_seq : first_seq + micro_seqs][:, None]
        gathered = lax.all_gather(inputs_mb, "head", axis=1, tiled=True)
        query_rows = (project(gathered, w_query) + bias_query).astype(jnp.bfloat16)
        key_rows = project(gathered, w_key).astype(jnp.bfloat16)
        value_rows = (project(gathered, w_value) + bias_value).astype(jnp.bfloat16)
        query_heads = query_rows.reshape(head_shape)
        key_heads = key_rows.reshape(head_shape)
        value_heads = value_rows.reshape(head_shape)
        scores, masked = masked_scores(query_heads, key_heads, prior_mb, live_keys, score_scale)
        row_max = jnp.max(masked, axis=-1, keepdims=True)
        exp_terms = jnp.exp(masked - row_max)
        row_total = jnp.sum(exp_terms, axis=-1, keepdims=True)
        attn_probs = (exp_terms / row_total).astype(jnp.bfloat16)
        log_total = row_max + jnp.log(row_total)
        context = jnp.einsum(
            "shqk,skhe->sqhe", attn_probs, value_heads, preferred_element_type=jnp.float32
        ).astype(jnp.bfloat16)
        context = context.reshape(micro_seqs, full_len, heads_local * head_size)
        attn_sum = lax.psum_scatter(
            project(context, w_output).astype(jnp.bfloat16), "head", scatter_dimension=1, tiled=True
        ).astype(jnp.float32)
        pre_attn = attn_sum + bias_output + inputs_mb.astype(jnp.float32)
        hidden = layer_norm(pre_attn, norm_gain_a, norm_shift_a)
        hidden_rows = lax.all_gather(hidden.astype(jnp.bfloat16), "head", axis=1, tiled=True)
        inner_pre = project(hidden_rows, w_inner) + bias_inner
        inner_act = jax.nn.gelu(inner_pre, approximate=False).astype(jnp.bfloat16)
        ffn_sum = lax.psum_scatter(
            project(inner_act, w_outer).astype(jnp.bfloat16),
            "head",
            scatter_dimension=1,
            tiled=True,
        ).astype(jnp.float32)
        pre_ffn = ffn_sum + bias_outer + hidden
        out_list.append(layer_norm(pre_ffn, norm_gain_f, norm_shift_f).astype(jnp.bfloat16))
        score_list.append(scores.astype(jnp.bfloat16))
        grad_mb = grad_out[first_seq : first_seq + micro_seqs].astype(jnp.float32)
        unused_ffn, pull_ffn = jax.vjp(layer_norm, pre_ffn, norm_gain_f, norm_shift_f)
        grad_pre_ffn, grad_gain_f, grad_shift_f = pull_ffn(grad_mb)
        grad_ffn_rows = lax.all_gather(
            grad_pre_ffn.astype(jnp.bfloat16), "head", axis=1, tiled=True
        )
        grad_act = project_back(grad_ffn_rows, w_outer).astype(jnp.bfloat16)
        grad_inner = (grad_act.astype(jnp.float32) * gelu_slope(inner_pre)).astype(jnp.bfloat16)
        grad_hidden = grad_pre_ffn + lax.psum_scatter(
            project_back(grad_inner, w_inner).astype(jnp.bfloat16),
            "head",
            scatter_dimension=1,
            tiled=True,
        ).astype(jnp.float32)
        unused_attn, pull_attn = jax.vjp(layer_norm, pre_attn, norm_gain_a, norm_shift_a)
        grad_pre_attn, grad_gain_a, grad_shift_a = pull_attn(grad_hidden)
        grad_attn_rows = lax.all_gather(
            grad_pre_attn.astype(jnp.bfloat16), "head", axis=1, tiled=True
        )
        grad_context = (
            project_back(grad_attn_rows, w_output).astype(jnp.bfloat16).reshape(head_shape)
        )
        unused_scores, masked_again = masked_scores(
            query_heads, key_heads, prior_mb, live_keys, score_scale
        )
        probs_again = jnp.exp(masked_again - log_total)
        grad_probs = jnp.einsum(
            "sqhe,skhe->shqk", grad_context, value_heads, preferred_element_type=jnp.float32
        )
        row_delta = jnp.sum(probs_again * grad_probs, axis=-1, keepdims=True)
        grad_raw = probs_again * (grad_probs - row_delta) + grad_scores[
            first_seq : first_seq + micro_seqs
        ].astype(jnp.float32)
        grad_raw_low = grad_raw.astype(jnp.bfloat16)
        grad_prior_list.append(grad_raw_low)
        grad_query = (
            jnp.einsum(
                "shqk,skhe->sqhe", grad_raw_low, key_heads, preferred_element_type=jnp.float32
            )
            * score_scale
        ).astype(jnp.bfloat16)
        grad_key = (
            jnp.einsum(
                "shqk,sqhe->skhe", grad_raw_low, query_heads, preferred_element_type=jnp.float32
            )
            * score_scale
        ).astype(jnp.bfloat16)
        grad_value = jnp.einsum(
            "shqk,sqhe->skhe", attn_probs, grad_context, preferred_element_type=jnp.float32
        ).astype(jnp.bfloat16)
        flat_shape = (micro_seqs, full_len, heads_local * head_size)
        grad_query = grad_query.reshape(flat_shape)
        grad_key = grad_key.reshape(flat_shape)
        grad_value = grad_value.reshape(flat_shape)
        grad_gathered = (
            project_back(grad_query, w_query)
            + project_back(grad_key, w_key)
            + project_back(grad_value, w_value)
        )
        grad_rows = grad_pre_attn + lax.psum_scatter(
            grad_gathered.astype(jnp.bfloat16), "head", scatter_dimension=1, tiled=True
        ).astype(jnp.float32)
        grad_in_list.append(grad_rows.astype(jnp.bfloat16))
        micro_grads = (
            outer_sum(gathered, grad_query),
            outer_sum(gathered, grad_key),
            outer_sum(gathered, grad_value),
            jnp.sum(grad_query.astype(jnp.float32), axis=(0, 1)),
            jnp.sum(grad_value.astype(jnp.float32), axis=(0, 1)),
            outer_sum(context, grad_attn_rows),
            outer_sum(hidden_rows, grad_inner),
            jnp.sum(grad_inner.astype(jnp.float32), axis=(0, 1)),
            outer_sum(inner_act, grad_ffn_rows),
        )
        micro_small = (
            jnp.sum(grad_pre_attn, axis=(0, 1)),
            grad_gain_a,
            grad_shift_a,
            jnp.sum(grad_pre_ffn, axis=(0, 1)),
            grad_gain_f,
            grad_shift_f,
        )
        weight_totals = jax.tree.map(jnp.add, weight_totals, micro_grads)
        small_totals = jax.tree.map(jnp.add, small_totals, micro_small)
    final_grads = lax.psum(weight_totals, "batch")
    final_small = lax.psum(small_totals, ("head", "batch"))
    (
        grad_w_query,
        grad_w_key,
        grad_w_value,
        grad_b_query,
        grad_b_value,
        grad_w_output,
        grad_w_inner,
        grad_b_inner,
        grad_w_outer,
    ) = final_grads
    grad_b_output, grad_gain_attn, grad_shift_attn, grad_b_outer, grad_gain_ffn, grad_shift_ffn = (
        final_small
    )
    return (
        jnp.concatenate(out_list, axis=0),
        jnp.concatenate(score_list, axis=0),
        jnp.concatenate(grad_in_list, axis=0),
        jnp.concatenate(grad_prior_list, axis=0),
        grad_w_query,
        grad_w_key,
        grad_w_value,
        grad_b_query,
        grad_b_value,
        grad_w_output,
        grad_b_output,
        grad_gain_attn,
        grad_shift_attn,
        grad_w_inner,
        grad_b_inner,
        grad_w_outer,
        grad_b_outer,
        grad_gain_ffn,
        grad_shift_ffn,
    )


def solution(mesh):
    in_specs = (
        P("batch", "head", None),
        P("batch", "head", None, None),
        P("batch"),
        P(None, "head"),
        P(None, "head"),
        P(None, "head"),
        P("head"),
        P("head"),
        P("head", None),
        P(),
        P(),
        P(),
        P(None, "head"),
        P("head"),
        P("head", None),
        P(),
        P(),
        P(),
        P("batch", "head", None),
        P("batch", "head", None, None),
    )
    out_specs = (
        P("batch", "head", None),
        P("batch", "head", None, None),
        P("batch", "head", None),
        P("batch", "head", None, None),
        P(None, "head"),
        P(None, "head"),
        P(None, "head"),
        P("head"),
        P("head"),
        P("head", None),
        P(),
        P(),
        P(),
        P(None, "head"),
        P("head"),
        P("head", None),
        P(),
        P(),
        P(),
    )
    return jax.shard_map(
        on_device, mesh=mesh, in_specs=in_specs, out_specs=out_specs, check_vma=False
    )
```

profile of v0, /device:TPU:0, one launch (start us, length us, event | category | flops | bytes accessed | tf_op | source)
XLA Modules:
  0.0 1013.3 jit_solution(7105312229337089757)
XLA Ops:
  13.1 5.8 fusion.163
  18.9 6.5 copy.64
  26.1 6.6 copy.65
  68.5 9.6 reduce-scatter.13.cloned.1.call-done
  84.8 9.5 all-gather.15.cloned.1.call-done
  94.3 6.9 fusion.123
  101.2 5.3 all-gather.11.cloned.1.call-done
  106.5 23.2 %fusion.10 = (bf16[512,2048]{1,0:T(8,128)(2,1)S(1)}, bf16[512,2048]{1,0:T(8,128)(2,1)}, f32[512,2048]{1,0:T(8,128)}) fusion(f32[2048]{0:T(1024)S(1)} %convert_element_type.359, f32[512,2048]{1,0:T(8,128)} %fusion.123, bf16[1024,2048]{1,0:T(8,128)(2,1)} %param.32, bf16[1,512,1024]{2,1,0:T(8,128)(2,1)} %all-gather.11.cloned.1.call-done), kind=kOutput, calls=%fused_computation.30 | convolution fusion | flops 2285895680 | bytes 17833984 | tf_op jit(solution)/shard_map/dot_general | solution.py:21
  134.5 6.2 fusion.57
  144.1 12.4 %reduce-scatter.15.cloned.1.call-done = bf16[1,256,1024]{2,1,0:T(8,128)(2,1)} async-done(((bf16[1,512,1024]{2,1,0:T(8,128)(2,1)}), bf16[1,256,1024]{2,1,0:T(8,128)(2,1)}) %reduce-scatter.15.cloned.1.call-update) | async-done | bytes 524304 | tf_op jit(solution)/shard_map/reduce_scatter | solution.py:138
  167.0 8.1 all-gather.17.cloned.1.call-done
  175.1 7.1 convert_reduce_fusion.1
  186.9 5.9 fusion.162
  192.9 6.5 copy.67
  199.4 6.5 copy.66
  205.9 7.1 convert_reduce_fusion
  218.0 4.5 fusion.131
  222.5 5.8 fusion.119
  228.3 6.0 convolution_add_fusion.1
  243.7 10.1 convolution_add_fusion
  257.6 5.4 fusion.2
  263.8 6.7 fusion.1
  282.4 5.3 fusion.5
  288.8 6.5 fusion.4
  318.3 45.4 %all-reduce = (f32[1024]{0:T(1024)}, f32[1024]{0:T(1024)}, f32[1024]{0:T(1024)}, f32[1024]{0:T(1024)}, f32[1024]{0:T(1024)}, /*index=5*/f32[1024]{0:T(1024)}) all-reduce(f32[1024]{0:T(1024)S(1)} %add.402, f32[1024]{0:T(1024)S(1)} %add.403, f32[1024]{0:T(1024)S(1)} %add.404, ...), channel_id=1, replica_groups=mesh['head'=2,'batch'=16] {'head','batch'}, use_global_device_ids=true, to_apply=%region_42.43 | all-reduce | flops 6144 | bytes 49152 | tf_op jit(solution)/shard_map/psum | solution.py:232
  363.7 8.0 pad_maximum_fusion
  371.7 11.8 %copy.51 = bf16[2,8,512,512]{3,2,1,0:T(8,128)(2,1)} copy(bf16[2,8,512,512]{2,3,1,0:T(8,128)(2,1)} %pad_maximum_fusion) | data formatting | bytes 16777216
  383.5 7.7 pad_maximum_fusion.1
  391.1 11.9 %copy.52 = bf16[2,8,512,512]{3,2,1,0:T(8,128)(2,1)} copy(bf16[2,8,512,512]{2,3,1,0:T(8,128)(2,1)} %pad_maximum_fusion.1) | data formatting | bytes 16777216
  403.2 79.4 %all-reduce.1 = (f32[512]{0:T(512)}, f32[512]{0:T(512)}, f32[2048]{0:T(1024)}) all-reduce(f32[512]{0:T(512)S(1)} %add.398, f32[512]{0:T(512)S(1)} %add.400, f32[2048]{0:T(1024)S(1)} %add.406), channel_id=1, replica_groups=mesh['head'=2,'batch'=16] {'batch'}, use_global_device_ids=true, to_apply=%region_35.36 | all-reduce | flops 3072 | bytes 24576 | tf_op jit(solution)/shard_map/psum | solution.py:231
  488.0 496.4 %all-reduce.5.cloned.1.call-done = (f32[1024,512]{0,1:T(8,128)}, f32[1024,512]{0,1:T(8,128)}, f32[1024,512]{0,1:T(8,128)}, f32[512,1024]{1,0:T(8,128)}, f32[1024,2048]{1,0:T(8,128)}, /*index=5*/f32[2048,1024]{1,0:T(8,128)}) async-done(((f32[1024,512]{0,1:T(8,128)}, f32[1024,512]{0,1:T(8,128)}, f32[1024,512]{0,1:T(8,128)}, f32[512,1024]{1,0:T(8,128)}, f32[1024,2048]{1,0:T(8,128)}, ...) | async-done | bytes 25165840 | tf_op jit(solution)/shard_map/psum | solution.py:231
  994.6 8.6 copy.75
  (384 shorter events, 144.9 us)
Async XLA Ops:
  7.2 40.1 %copy-start = (bf16[512,1024]{1,0:T(8,128)(2,1)S(1)}, bf16[512,1024]{1,0:T(8,128)(2,1)}, u32[]{:S(2)}) copy-start(bf16[512,1024]{1,0:T(8,128)(2,1)} %param.28) | copy-start | bytes 3145732
  7.2 25.5 %all-gather.9.cloned.1.call-start = ((), (), s32[]{:S(2)}) async-start(), calls=%async_computation.8 | async-start | bytes 1572864 | tf_op jit(solution)/shard_map/all_gather | solution.py:113
  9.6 39.7 %all-gather.13.cloned.1.call-start = ((), (), s32[]{:S(2)}) async-start(), calls=%async_computation.12 | async-start | bytes 1572864 | tf_op jit(solution)/shard_map/all_gather | solution.py:113
  10.3 56.8 %reduce-scatter.9.cloned.1.call-start = ((), (), s32[]{:S(2)}) async-start(), calls=%async_computation.9 | async-start | bytes 1572864 | tf_op jit(solution)/shard_map/reduce_scatter | solution.py:130
  13.0 27.9 %copy-start.85 = (pred[512]{0:T(512)(128)(4,1)}, pred[512]{0:T(512)(128)(4,1)S(1)}, u32[]{:S(2)}) copy-start(pred[512]{0:T(512)(128)(4,1)S(1)} %iota_compare_fusion.1) | copy-start | bytes 1540
  26.1 33.7 %copy-start.87 = (pred[512]{0:T(512)(128)(4,1)}, pred[512]{0:T(512)(128)(4,1)S(1)}, u32[]{:S(2)}) copy-start(pred[512]{0:T(512)(128)(4,1)S(1)} %iota_compare_fusion) | copy-start | bytes 1540
  26.1 8.8 copy-start.33
  49.0 29.2 %reduce-scatter.13.cloned.1.call-start = ((), (), s32[]{:S(2)}) async-start(), calls=%async_computation.13 | async-start | bytes 1572864 | tf_op jit(solution)/shard_map/reduce_scatter | solution.py:130
  67.0 27.3 %all-gather.15.cloned.1.call-start = ((), (), s32[]{:S(2)}) async-start(), calls=%async_computation.14 | async-start | bytes 1572864 | tf_op jit(solution)/shard_map/all_gather | solution.py:135
  67.1 17.6 %copy-start.94 = (bf16[2048]{0:T(1024)(128)(2,1)S(1)}, bf16[2048]{0:T(1024)(128)(2,1)}, u32[]{:S(2)}) copy-start(bf16[2048]{0:T(1024)(128)(2,1)} %param.33) | copy-start | bytes 12292
  67.2 14.1 %copy-start.10 = (bf16[1,256,1024]{2,1,0:T(8,128)(2,1)S(1)}, bf16[1,256,1024]{2,1,0:T(8,128)(2,1)}, u32[]{:S(2)}) copy-start(bf16[1,256,1024]{2,1,0:T(8,128)(2,1)} %reduce-scatter.9.cloned.1.call-done) | copy-start | bytes 1572868
  83.9 22.6 %all-gather.11.cloned.1.call-start = ((), (), s32[]{:S(2)}) async-start(), calls=%async_computation.10 | async-start | bytes 1572864 | tf_op jit(solution)/shard_map/all_gather | solution.py:135
  84.5 59.6 %reduce-scatter.11.cloned.1.call-start = ((), (), s32[]{:S(2)}) async-start(), calls=%async_computation.11 | async-start | bytes 1572864 | tf_op jit(solution)/shard_map/reduce_scatter | solution.py:138
  106.5 24.5 %copy-start.102 = (bf16[2048,1024]{1,0:T(8,128)(2,1)S(1)}, bf16[2048,1024]{1,0:T(8,128)(2,1)}, u32[]{:S(2)}) copy-start(bf16[2048,1024]{1,0:T(8,128)(2,1)} %param.34) | copy-start | bytes 12582916
  134.4 22.2 %reduce-scatter.15.cloned.1.call-start = ((), (), s32[]{:S(2)}) async-start(), calls=%async_computation.15 | async-start | bytes 1572864 | tf_op jit(solution)/shard_map/reduce_scatter | solution.py:138
  134.5 22.1 %copy-start.11 = (bf16[1,256,1024]{2,1,0:T(8,128)(2,1)S(1)}, bf16[1,256,1024]{2,1,0:T(8,128)(2,1)}, u32[]{:S(2)}) copy-start(bf16[1,256,1024]{2,1,0:T(8,128)(2,1)} %reduce-scatter.13.cloned.1.call-done) | copy-start | bytes 1572868
  140.7 34.5 %all-gather.17.cloned.1.call-start = ((), (), s32[]{:S(2)}) async-start(), calls=%async_computation.16 | async-start | bytes 1572864 | tf_op jit(solution)/shard_map/all_gather | solution.py:150
  164.8 41.2 %all-gather.21.cloned.1.call-start = ((), (), s32[]{:S(2)}) async-start(), calls=%async_computation.20 | async-start | bytes 1572864 | tf_op jit(solution)/shard_map/all_gather | solution.py:150
  167.0 67.3 %reduce-scatter.17.cloned.1.call-start = ((), (), s32[]{:S(2)}) async-start(), calls=%async_computation.17 | async-start | bytes 1572864 | tf_op jit(solution)/shard_map/reduce_scatter | solution.py:155
  186.9 47.4 %reduce-scatter.21.cloned.1.call-start = ((), (), s32[]{:S(2)}) async-start(), calls=%async_computation.21 | async-start | bytes 1572864 | tf_op jit(solution)/shard_map/reduce_scatter | solution.py:155
  217.7 37.9 %all-gather.23.cloned.1.call-start = ((), (), s32[]{:S(2)}) async-start(), calls=%async_computation.22 | async-start | bytes 1572864 | tf_op jit(solution)/shard_map/all_gather | solution.py:163
  241.1 12.6 %copy-start.88 = (f32[256]{0:T(256)}, f32[256]{0:T(256)S(1)}, u32[]{:S(2)}) copy-start(f32[256]{0:T(256)S(1)} %negate_multiply_fusion.2) | copy-start | bytes 3076
  243.6 10.1 %copy-start.21 = (f32[1,256,1024]{2,1,0:T(8,128)S(1)}, f32[1,256,1024]{2,1,0:T(8,128)}, u32[]{:S(2)}) copy-start(f32[1,256,1024]{2,1,0:T(8,128)} %get-tuple-element.78) | copy-start | bytes 3145732
  243.6 36.8 %all-gather.19.cloned.1.call-start = ((), (), s32[]{:S(2)}) async-start(), calls=%async_computation.18 | async-start | bytes 1572864 | tf_op jit(solution)/shard_map/all_gather | solution.py:163
  255.3 227.3 %reduce-scatter.23.cloned.1.call-start = ((), (), s32[]{:S(2)}) async-start(), calls=%async_computation.23 | async-start | bytes 1572864 | tf_op jit(solution)/shard_map/reduce_scatter | solution.py:206
  279.9 204.7 %reduce-scatter.19.cloned.1.call-start = ((), (), s32[]{:S(2)}) async-start(), calls=%async_computation.19 | async-start | bytes 1572864 | tf_op jit(solution)/shard_map/reduce_scatter | solution.py:206
  304.5 680.0 %all-reduce.5.cloned.1.call-start = ((), (), s32[]{:S(2)}) async-start(), calls=%async_computation.24 | async-start | bytes 50331648 | tf_op jit(solution)/shard_map/psum | solution.py:231
  391.1 91.5 %copy-start.24 = (f32[1,256,1024]{2,1,0:T(8,128)S(1)}, f32[1,256,1024]{2,1,0:T(8,128)}, u32[]{:S(2)}) copy-start(f32[1,256,1024]{2,1,0:T(8,128)} %copy-done.23) | copy-start | bytes 3145732
  391.1 91.5 %copy-start.89 = (f32[256]{0:T(256)S(1)}, f32[256]{0:T(256)}, u32[]{:S(2)}) copy-start(f32[256]{0:T(256)} %copy-done.88) | copy-start | bytes 3076
  391.1 93.5 %copy-start.22 = (f32[1,256,1024]{2,1,0:T(8,128)S(1)}, f32[1,256,1024]{2,1,0:T(8,128)}, u32[]{:S(2)}) copy-start(f32[1,256,1024]{2,1,0:T(8,128)} %get-tuple-element.78) | copy-start | bytes 3145732
  391.1 93.5 %copy-start.91 = (f32[256]{0:T(256)S(1)}, f32[256]{0:T(256)}, u32[]{:S(2)}) copy-start(f32[256]{0:T(256)} %copy-done.90) | copy-start | bytes 3076
  993.2 9.9 slice-start.4
  (100 other events, 324.2 us)
Sparse Core Ops, SparseCore 0:
  10.1 11.7 all-gather.8
  24.0 10.1 all-gather.12
  49.2 11.0 reduce-scatter.8
  67.1 11.0 reduce-scatter.12
  84.0 10.2 all-gather.14
  96.3 10.1 all-gather.10
  134.5 9.5 reduce-scatter.10
  146.9 9.5 reduce-scatter.14
  164.9 10.2 all-gather.16
  177.1 10.1 all-gather.20
  190.2 9.5 reduce-scatter.16
  217.8 9.5 reduce-scatter.20
  243.7 10.1 all-gather.22
  255.9 10.1 all-gather.18
  280.0 9.4 reduce-scatter.22
  304.6 9.4 reduce-scatter.18
  321.5 662.9 all-reduce.4
where the time goes:
time: 1020 us; the launch traced here: 1010 us
  waiting for transfers between devices  546 us (54%)
  matrix products  146 us (14%)
  blocking collectives  125 us (12%)
  local copies, waits for them, and re-layouts  108 us (11%)
  other arithmetic  70.6 us (7%)
  between operations  15.7 us (2%)
    psum x1, waiting for transfers between devices, on_device(): final_grads = lax.psum(weight_totals, 'batch')  496 us
    unnamed x242, local copies, waits for them, and re-layouts  92.6 us
    psum x1, blocking collectives, on_device(): final_grads = lax.psum(weight_totals, 'batch')  79.4 us
    dot_general x12, matrix products, project(): return jnp.dot(left_side, right_side, preferred_element_type=jnp.float32)  53.1 us
    psum x1, blocking collectives, on_device(): final_small = lax.psum(small_totals, ('head', 'batch'))  45.4 us
    dot_general x12, matrix products, outer_sum(): jnp.einsum('sla,slb->ab', left_side, right_side, preferred_element_type=j...  37.3 us
    dot_general x12, matrix products, project_back(): jnp.einsum('sla,ba->slb', left_side, right_side, preferred_element_type=j...  31.3 us
  transfers between devices with their start and end apart: 17, of which 7 were waited for; matrix products, arithmetic and copies ran while one was open for 23% of the time, Pallas kernels for 0%

commit v1 on v0

--- a/solution.py
+++ b/solution.py
@@ -1,9 +1,166 @@
+import functools
+
 import jax
 import jax.numpy as jnp
 from jax import lax
 from jax.sharding import PartitionSpec as P
 
-MB = 2
+from jax.experimental import pallas as pl
+from jax.experimental.pallas import tpu as pltpu
+
+MESH = pl.DeviceIdType.MESH
+F32, BF16 = jnp.float32, jnp.bfloat16
+
+
+def grid_bits(n):
+    bits = n.bit_length() - 1
+    side = bits // 3
+    return (0, side, 2 * side), bits
+
+
+def chunk_plan(n, color):
+    (bx, by, bz), bits = grid_bits(n)
+    order = ((bx, by, bz), (by, bx, bz), (bz, bx, by), (bz, by, bx))[color]
+    rest = [b for b in range(bits) if b not in order]
+    stages = [("scatter", b) for b in order] + [("double", b) for b in rest]
+    stages += [("gather", b) for b in reversed(order)]
+    return stages
+
+
+def event_order(n, colors, rows):
+    (bx, by, bz), bits = grid_bits(n)
+    axis = lambda b: 0 if b < by else 1 if b < bz else 2
+    hop = lambda b: 1 << (b - (bx, by, bz)[axis(b)])
+    free = [0.0, 0.0, 0.0]
+    ready = [0.0] * len(colors)
+    plans = [chunk_plan(n, c) for c in colors]
+    step = [0] * len(colors)
+    length = [1.0] * len(colors)
+    events = []
+    total = sum(len(p) for p in plans)
+    while len(events) < total:
+        best = None
+        for c, plan in enumerate(plans):
+            if step[c] == len(plan):
+                continue
+            kind, b = plan[step[c]]
+            start = max(ready[c], free[axis(b)])
+            key = (start, -step[c], c)
+            if best is None or key < best[0]:
+                best = (key, c)
+        (start, _, _), c = best
+        kind, b = plans[c][step[c]]
+        if kind == "scatter":
+            length[c] /= 2
+        span = length[c] * (min(hop(b), 2))
+        if kind == "gather":
+            length[c] *= 2
+        free[axis(b)] = start + span
+        ready[c] = start + span + 0.08
+        events.append((start, c, step[c]))
+        step[c] += 1
+    events.sort()
+    return [(c, s) for _, c, s in events], max(ready)
+
+
+def flip(index, bit):
+    return index + (1 - 2 * ((index // (1 << bit)) % 2)) * (1 << bit)
+
+
+def reduce_kernel(n, colors, rows, g_hbm, out_hbm, work, got, full, load_sem, save_sem, send_sem, recv_sem):
+    nc = len(colors)
+    me = lax.axis_index("batch")
+    (bx, by, bz), bits = grid_bits(n)
+    for c in range(nc):
+        pltpu.make_async_copy(g_hbm.at[c], work.at[c], load_sem.at[c]).start()
+    barrier = pltpu.get_barrier_semaphore()
+    for b in range(bits):
+        pl.semaphore_signal(barrier, inc=1, device_id={"batch": flip(me, b)}, device_id_type=MESH)
+    pl.semaphore_wait(barrier, bits)
+
+    plans = [chunk_plan(n, c) for c in colors]
+    events, _ = event_order(n, colors, rows)
+    bit_of = [(me // (1 << b)) % 2 for b in range(bits)]
+    spans = []
+    for c in range(nc):
+        off, length, at = 0, rows, 0
+        row = []
+        for kind, b in plans[c]:
+            if kind == "scatter":
+                half = length // 2
+                keep = off + bit_of[b] * half
+                give = off + (1 - bit_of[b]) * half
+                row.append((keep, give, half, at))
+                off, length, at = keep, half, at + half
+            elif kind == "double":
+                row.append((off, off, length, at))
+                at += length
+            else:
+                row.append((off, off, length, None))
+                off = off - bit_of[b] * length
+                length = 2 * length
+        spans.append(row)
+
+    def copy_of(c, s):
+        kind, b = plans[c][s]
+        keep, give, length, at = spans[c][s]
+        place = (c, pl.ds(pl.multiple_of(give, 16), length))
+        if kind == "gather":
+            src, dst = full.at[place], full.at[place]
+        else:
+            src, dst = work.at[place], got.at[c, pl.ds(at, length)]
+        return pltpu.make_async_remote_copy(
+            src_ref=src, dst_ref=dst, send_sem=send_sem.at[c, s], recv_sem=recv_sem.at[c, s],
+            device_id={"batch": flip(me, b)}, device_id_type=MESH)
+
+    def finish(c, s):
+        kind, b = plans[c][s]
+        keep, give, length, at = spans[c][s]
+        copy_of(c, s).wait()
+        if kind != "gather":
+            target = full if plans[c][s + 1][0] == "gather" else work
+
+            def add(i, _):
+                r = pl.multiple_of(keep + i * 16, 16)
+                q = pl.multiple_of(at + i * 16, 16)
+                target[c, pl.ds(r, 16), :] = (work[c, pl.ds(r, 16), :].astype(F32) + got[c, pl.ds(q, 16), :].astype(F32)).astype(BF16)
+                return 0
+            lax.fori_loop(0, length // 16, add, 0)
+
+    for c, s in events:
+        if s == 0:
+            pltpu.make_async_copy(g_hbm.at[c], work.at[c], load_sem.at[c]).wait()
+        else:
+            finish(c, s - 1)
+        copy_of(c, s).start()
+    for c in range(nc):
+        finish(c, len(plans[c]) - 1)
+        pltpu.make_async_copy(full.at[c], out_hbm.at[c], save_sem.at[c]).start()
+    for c in range(nc):
+        pltpu.make_async_copy(full.at[c], out_hbm.at[c], save_sem.at[c]).wait()
+
+
+def all_reduce(g, n, colors):
+    nc, rows, cols = g.shape
+    stages = len(chunk_plan(n, 0))
+    _, bits = grid_bits(n)
+    got_rows = rows - rows // 8 + (bits - 3) * rows // 8
+    return pl.pallas_call(
+        functools.partial(reduce_kernel, n, colors, rows),
+        out_shape=jax.ShapeDtypeStruct(g.shape, g.dtype),
+        in_specs=[pl.BlockSpec(memory_space=pl.ANY)],
+        out_specs=pl.BlockSpec(memory_space=pl.ANY),
+        scratch_shapes=[
+            pltpu.VMEM(g.shape, BF16), pltpu.VMEM((nc, got_rows, cols), BF16), pltpu.VMEM(g.shape, BF16),
+            pltpu.SemaphoreType.DMA((nc,)), pltpu.SemaphoreType.DMA((nc,)),
+            pltpu.SemaphoreType.DMA((nc, stages)), pltpu.SemaphoreType.DMA((nc, stages)),
+        ],
+        compiler_params=pltpu.CompilerParams(collective_id=0, has_side_effects=True, vmem_limit_bytes=60 << 20),
+        name="reduce_gradients",
+    )(g)
+
+
+MB = 1
 
 
 EPS = 1e-12
@@ -45,6 +202,7 @@
 
 
 def on_device(
+    n_batch,
     inputs,
     prior_scores,
     lengths,
@@ -228,7 +386,22 @@
         )
         weight_totals = jax.tree.map(jnp.add, weight_totals, micro_grads)
         small_totals = jax.tree.map(jnp.add, small_totals, micro_small)
-    final_grads = lax.psum(weight_totals, "batch")
+    low = [total.astype(jnp.bfloat16) for total in weight_totals]
+    width = inputs.shape[2]
+    packed = jnp.concatenate([
+        jnp.concatenate([low[0], low[1]], axis=1),
+        low[2].reshape(-1, width), low[5],
+        low[6].reshape(-1, width), low[8]], axis=0)
+    colors = (0, 1) * 12
+    done = all_reduce(packed.reshape(len(colors), -1, width), n_batch, colors)
+    done = done.reshape(-1, width).astype(jnp.float32)
+    sizes = [low[0].shape[0], low[2].size // width, low[5].shape[0], low[6].size // width, low[8].shape[0]]
+    starts = [sum(sizes[:i]) for i in range(6)]
+    part = [done[starts[i]:starts[i + 1]] for i in range(5)]
+    half = low[0].shape[1]
+    final_b = lax.psum((weight_totals[3], weight_totals[4], weight_totals[7]), "batch")
+    final_grads = (part[0][:, :half], part[0][:, half:], part[1].reshape(low[2].shape),
+                   final_b[0], final_b[1], part[2], part[3].reshape(low[6].shape), final_b[2], part[4])
     final_small = lax.psum(small_totals, ("head", "batch"))
     (
         grad_w_query,
@@ -312,5 +485,5 @@
         P(),
     )
     return jax.shard_map(
-        on_device, mesh=mesh, in_specs=in_specs, out_specs=out_specs, check_vma=False
-    )
+        functools.partial(on_device, mesh.shape["batch"]), mesh=mesh, in_specs=in_specs, out_specs=out_specs, check_vma=False
+    )

time: 1020 us -> 717 us (0.70)
  waiting for transfers between devices: 546 us -> 59.3 us
  Pallas kernels: 0 us -> 220 us
  matrix products: 146 us -> 117 us
    psum x1 -> x0, waiting for transfers between devices: 496 us -> none  [on_device(): final_grads = lax.psum(weight_totals, 'batch')]
    pallas_call x0 -> x1, Pallas kernels: none -> 220 us  [all_reduce(): pl.pallas_call(functools.partial(reduce_kernel, n, colors, rows), out_sha...]
    dot_general x12 -> x6, matrix products: 53.1 us -> 24.1 us  [project(): return jnp.dot(left_side, right_side, preferred_element_type=jnp.float32)]
    convert_element_type x2 -> x3, other arithmetic: 13.1 us -> 40.8 us  [the longest x1 19.7 us: on_device(): inner_act = jax.nn.gelu(inner_pre, approximate=False).astype(jnp.bfloat16)]
    unnamed x242 -> x109, local copies, waits for them, and re-layouts: 92.6 us -> 66.3 us
    sub x0 -> x1, matrix products: none -> 20.5 us  [on_device(): grad_probs - row_delta]
    reshape x0 -> x4, local copies, waits for them, and re-layouts: none -> 19.9 us  [the longest x1 9.87 us: on_device(): part[3].reshape(low[6].shape)]
    concatenate x4 -> x1, other arithmetic: 18.8 us -> 1.49 us  [on_device(): jnp.concatenate([low[0], low[1]], axis=1)]
  transfers between devices with their start and end apart: 17 -> 8, of which waited for: 7 -> 6; matrix products, arithmetic and copies ran while one was open for 23% -> 18% of each run, Pallas kernels for 0% -> 31%
where the time goes in v1:
time: 717 us; the launch traced here: 707 us
  Pallas kernels  220 us (31%)
  matrix products  117 us (16%)
  blocking collectives  116 us (16%)
  local copies, waits for them, and re-layouts  111 us (15%)
  other arithmetic  66.8 us (9%)
  waiting for transfers between devices  59.3 us (8%)
  between operations  15.2 us (2%)
    pallas_call x1, Pallas kernels, all_reduce(): pl.pallas_call(functools.partial(reduce_kernel, n, colors, rows), out_sha...  220 us
    psum x1, blocking collectives, on_device(): lax.psum((weight_totals[3], weight_totals[4], weight_totals[7]), 'batch')  74.5 us
    unnamed x109, local copies, waits for them, and re-layouts  66.3 us
    psum x1, blocking collectives, on_device(): final_small = lax.psum(small_totals, ('head', 'batch'))  41.3 us
    dot_general x6, matrix products, project_back(): jnp.einsum('sla,ba->slb', left_side, right_side, preferred_element_type=j...  26.1 us
    dot_general x6, matrix products, outer_sum(): jnp.einsum('sla,slb->ab', left_side, right_side, preferred_element_type=j...  25 us
    dot_general x6, matrix products, project(): return jnp.dot(left_side, right_side, preferred_element_type=jnp.float32)  24.1 us
    sub x1, matrix products, on_device(): grad_probs - row_delta  20.5 us
  transfers between devices with their start and end apart: 8, of which 6 were waited for; matrix products, arithmetic and copies ran while one was open for 18% of the time, Pallas kernels for 31%

profile of v1, /device:TPU:0, one launch (start us, length us, event | category | flops | bytes accessed | tf_op | source)
XLA Modules:
  0.0 706.6 jit_solution(17587926120668489120)
XLA Ops:
  8.7 11.8 %copy.60 = bf16[2,8,512,512]{2,3,1,0:T(8,128)(2,1)} copy(bf16[2,8,512,512]{3,2,1,0:T(8,128)(2,1)} %param.21) | data formatting | bytes 16777216 | tf_op args[1]
  27.3 6.5 select_reduce_fusion
  33.9 7.0 fusion.73
  42.1 3.6 divide_convert_fusion
  53.3 10.9 %reduce-scatter.5.cloned.1.call-done = bf16[2,256,1024]{2,1,0:T(8,128)(2,1)} async-done(((bf16[2,512,1024]{2,1,0:T(8,128)(2,1)}), bf16[2,256,1024]{2,1,0:T(8,128)(2,1)}) %reduce-scatter.5.cloned.1.call-update) | async-done | bytes 1048592 | tf_op jit(solution)/shard_map/reduce_scatter | solution.py:288
  69.6 11.7 %all-gather.7.cloned.1.call-done = bf16[2,512,1024]{2,1,0:T(8,128)(2,1)} async-done(((bf16[2,256,1024]{2,1,0:T(8,128)(2,1)}), bf16[2,512,1024]{2,1,0:T(8,128)(2,1)}) %all-gather.7.cloned.1.call-update) | async-done | bytes 2097168 | tf_op jit(solution)/shard_map/all_gather | solution.py:293
  81.3 10.1 %fusion.39 = (u8[512,2048]{1,0:T(8,128)(4,1)S(1)}, u8[512,2048]{1,0:T(8,128)(4,1)S(1)}, f32[2,512,2048]{2,1,0:T(8,128)S(1)}) fusion(f32[2048]{0:T(1024)S(1)} %convert_element_type.196, bf16[2,512,1024]{2,1,0:T(8,128)(2,1)} %all-gather.7.cloned.1.call-done, bf16[1024,2048]{1,0:T(8,128)(2,1)} %param.32), kind=kOutput, calls=%fused_computation.86 | convolution fusion | flops 4322230272 | bytes 16785408 | tf_op jit(solution)/shard_map/dot_general | solution.py:178
  91.5 19.7 %fusion.7 = bf16[2,512,2048]{2,1,0:T(8,128)(2,1)S(1)} fusion(f32[2,512,2048]{2,1,0:T(8,128)S(1)} %get-tuple-element.94, f32[2048]{0:T(1024)S(1)} %convert_element_type.196, u8[512,2048]{1,0:T(8,128)(4,1)S(1)} %get-tuple-element.58, u8[512,2048]{1,0:T(8,128)(4,1)S(1)} %get-tuple-element.57), kind=kLoop, calls=%fused_computation.14 | loop fusion | flops 148897792 | bytes 14688256 | tf_op jit(solution)/shard_map/convert_element_type | solution.py:295
  113.1 5.7 fusion.43
  118.9 11.0 %reduce-scatter.7.cloned.1.call-done = bf16[2,256,1024]{2,1,0:T(8,128)(2,1)} async-done(((bf16[2,512,1024]{2,1,0:T(8,128)(2,1)}), bf16[2,256,1024]{2,1,0:T(8,128)(2,1)}) %reduce-scatter.7.cloned.1.call-update) | async-done | bytes 1048592 | tf_op jit(solution)/shard_map/reduce_scatter | solution.py:296
  138.4 11.5 %all-gather.9.cloned.1.call-done = bf16[2,512,1024]{2,1,0:T(8,128)(2,1)} async-done(((bf16[2,256,1024]{2,1,0:T(8,128)(2,1)}), bf16[2,512,1024]{2,1,0:T(8,128)(2,1)}) %all-gather.9.cloned.1.call-update) | async-done | bytes 2097168 | tf_op jit(solution)/shard_map/all_gather | solution.py:308
  149.9 10.9 %convert_reduce_fusion = (f32[2048]{0:T(1024)S(1)}, bf16[2,512,2048]{2,1,0:T(8,128)(2,1)S(1)}) fusion(f32[2,512,2048]{2,1,0:T(8,128)} %copy-done.12, f32[2048]{0:T(1024)S(1)} %convert_element_type.196, bf16[2,512,1024]{2,1,0:T(8,128)(2,1)} %all-gather.9.cloned.1.call-done, bf16[2048,1024]{1,0:T(8,128)(2,1)} %param.34), kind=kOutput, calls=%fused_computation.28 | convolution fusion | flops 4326422528 | bytes 18890752 | tf_op jit(solution)/shard_map/sla,ba->slb/dot_general | solution.py:182
  162.7 5.7 fusion.40
  168.5 11.0 %reduce-scatter.9.cloned.1.call-done = bf16[2,256,1024]{2,1,0:T(8,128)(2,1)} async-done(((bf16[2,512,1024]{2,1,0:T(8,128)(2,1)}), bf16[2,256,1024]{2,1,0:T(8,128)(2,1)}) %reduce-scatter.9.cloned.1.call-update) | async-done | bytes 1048592 | tf_op jit(solution)/shard_map/reduce_scatter | solution.py:313
  179.6 3.4 multiply_reduce_fusion.1
  186.9 11.9 %copy.63 = bf16[2,8,512,512]{2,3,1,0:T(8,128)(2,1)} copy(bf16[2,8,512,512]{3,2,1,0:T(8,128)(2,1)} %param.39) | data formatting | bytes 16777216 | tf_op args[19]
  198.8 11.8 %copy.74 = bf16[2,8,512,512]{3,2,1,0:T(8,128)(2,1)} copy(bf16[2,8,512,512]{2,3,1,0:T(8,128)(2,1)} %get-tuple-element.83) | data formatting | bytes 16777216
  210.6 8.3 %bitcast_convert_fusion.1 = bf16[1024,2048]{1,0:T(8,128)(2,1)} fusion(bf16[2,512,1024]{2,1,0:T(8,128)(2,1)S(1)} %copy-done.48, bf16[2,512,2048]{2,1,0:T(8,128)(2,1)} %copy-done.50), kind=kOutput, calls=%fused_computation.27 | convolution fusion | flops 4297064448 | bytes 10485760 | tf_op jit(solution)/shard_map/sla,slb->ab/dot_general | solution.py:186
  218.9 7.2 %reshape.193 = bf16[2048,1024]{1,0:T(8,128)(2,1)} reshape(bf16[1024,2048]{1,0:T(8,128)(2,1)} %bitcast_convert_fusion.1) | data formatting | bytes 8388608 | tf_op jit(solution)/shard_map/reshape | solution.py:394
  226.1 41.3 %all-reduce = (f32[1024]{0:T(1024)}, f32[1024]{0:T(1024)}, f32[1024]{0:T(1024)}, f32[1024]{0:T(1024)}, f32[1024]{0:T(1024)}, /*index=5*/f32[1024]{0:T(1024)}) all-reduce(f32[1024]{0:T(1024)S(1)} %get-tuple-element.90, f32[1024]{0:T(1024)S(1)} %get-tuple-element.59, ...), channel_id=1, replica_groups=mesh['head'=2,'batch'=16] {'head','batch'}, use_global_device_ids=true, to_apply=%region_20.21 | all-reduce | flops 6144 | bytes 49152 | tf_op jit(solution)/shard_map/psum | solution.py:405
  271.3 6.2 convert_reduce_fusion.2
  277.5 20.5 %add_convert_fusion = bf16[2,8,512,512]{2,3,1,0:T(8,128)(2,1)} fusion(bf16[2,8,512,512]{2,3,1,0:T(8,128)(2,1)} %copy.63, f32[2,8,512,512]{2,3,1,0:T(8,128)} %copy-done.2, f32[2,8,512]{2,1,0:T(8,128)S(1)} %log_add_fusion, pred[2,512]{1,0:T(4,128)(4,1)S(1)} %iota_compare_fusion, bf16[2,512,8,64]{1,3,2,0:T(8,128)(2,1)} %bitcast.149, ...), kind=kOutput, calls=%fused_computation.1 | convolution fusion | flops 1115693568 | bytes 35685376 | tf_op jit(solution)/shard_map/sub | solution.py:335
  298.0 5.1 convert_reduce_fusion.3
  306.6 11.8 %copy.75 = bf16[2,8,512,512]{3,2,1,0:T(8,128)(2,1)} copy(bf16[2,8,512,512]{2,3,1,0:T(8,128)(2,1)} %add_convert_fusion) | data formatting | bytes 16777216
  334.1 3.9 fusion.52
  351.2 6.2 fusion.33
  357.4 219.6 %reduce_gradients.1 = bf16[24,256,1024]{2,1,0:T(8,128)(2,1)} custom-call(bf16[24,256,1024]{2,1,0:T(8,128)(2,1)} %bitcast.34.g_hbm), custom_call_target="tpu_custom_call" | custom-call | tf_op jit(solution)/shard_map/reduce_gradients/pallas_call | solution.py:148
  577.0 14.2 %convert_element_type.234 = f32[24,256,1024]{2,1,0:T(8,128)} convert(bf16[24,256,1024]{2,1,0:T(8,128)(2,1)} %reduce_gradients.1) | non-fusion elementwise | flops 6291456 | bytes 37748736 | tf_op jit(solution)/shard_map/convert_element_type | solution.py:397
  591.3 11.6 %fusion.74 = (f32[8,256,1024]{2,1,0:T(8,128)}, f32[8,256,1024]{2,1,0:T(8,128)}) fusion(bf16[24,256,1024]{2,1,0:T(8,128)(2,1)} %reduce_gradients.1), kind=kLoop, calls=%fused_computation.138 | loop fusion | bytes 33554432 | tf_op jit(solution)/shard_map/slice | solution.py:400
  602.8 9.9 %reshape.196 = f32[1024,2048]{1,0:T(8,128)} reshape(f32[8,256,1024]{2,1,0:T(8,128)} %get-tuple-element.86) | data formatting | bytes 16777216 | tf_op jit(solution)/shard_map/reshape | solution.py:404
  617.5 74.5 %all-reduce.1 = (f32[512]{0:T(512)}, f32[512]{0:T(512)}, f32[2048]{0:T(1024)}) all-reduce(f32[512]{0:T(512)S(1)} %reduce_sum.191, f32[512]{0:T(512)S(1)} %reduce_sum.196, f32[2048]{0:T(1024)S(1)} %get-tuple-element.99), channel_id=1, replica_groups=mesh['head'=2,'batch'=16] {'batch'}, use_global_device_ids=true, to_apply=%region_16.17 | all-reduce | flops 3072 | bytes 24576 | tf_op jit(solution)/shard_map/psum | solution.py:402
  692.0 4.8 fusion.72
  (175 shorter events, 81.9 us)
Async XLA Ops:
  7.2 43.3 %copy-start = (bf16[512,1024]{1,0:T(8,128)(2,1)S(1)}, bf16[512,1024]{1,0:T(8,128)(2,1)}, u32[]{:S(2)}) copy-start(bf16[512,1024]{1,0:T(8,128)(2,1)} %param.28) | copy-start | bytes 3145732
  7.2 15.7 %all-gather.5.cloned.1.call-start = ((), (), s32[]{:S(2)}) async-start(), calls=%async_computation.4 | async-start | bytes 3145728 | tf_op jit(solution)/shard_map/all_gather | solution.py:271
  7.9 56.3 %reduce-scatter.5.cloned.1.call-start = ((), (), s32[]{:S(2)}) async-start(), calls=%async_computation.5 | async-start | bytes 3145728 | tf_op jit(solution)/shard_map/reduce_scatter | solution.py:288
  8.7 11.8 %copy-start.40 = (bf16[512]{0:T(512)(128)(2,1)S(1)}, bf16[512]{0:T(512)(128)(2,1)}, u32[]{:S(2)}) copy-start(bf16[512]{0:T(512)(128)(2,1)} %param.27) | copy-start | bytes 3076
  8.7 11.8 %copy-start.41 = (s32[2]{0:T(128)S(1)}, s32[2]{0:T(128)}, u32[]{:S(2)}) copy-start(s32[2]{0:T(128)} %param.22) | copy-start | bytes 28
  8.7 14.2 %copy-start.30 = (bf16[1024,512]{1,0:T(8,128)(2,1)S(1)}, bf16[1024,512]{1,0:T(8,128)(2,1)}, u32[]{:S(2)}) copy-start(bf16[1024,512]{1,0:T(8,128)(2,1)} %param.24) | copy-start | bytes 3145732
  20.5 5.4 copy-start.31
  26.0 7.9 %copy-start.13 = (bf16[2,512,512]{1,2,0:T(8,128)(2,1)}, bf16[2,512,512]{1,2,0:T(8,128)(2,1)S(1)}, u32[]{:S(2)}) copy-start(bf16[2,512,512]{1,2,0:T(8,128)(2,1)S(1)} %convolution_convert_fusion.4) | copy-start | bytes 3145732
  27.3 6.6 copy-start.17
  33.9 8.2 %copy-start.2 = (f32[2,8,512,512]{2,3,1,0:T(8,128)}, f32[2,8,512,512]{2,3,1,0:T(8,128)S(1)}, u32[]{:S(2)}) copy-start(f32[2,8,512,512]{2,3,1,0:T(8,128)S(1)} %get-tuple-element.93) | copy-start | bytes 50331652
  49.5 14.7 %copy-start.5 = (bf16[2,256,1024]{2,1,0:T(8,128)(2,1)S(1)}, bf16[2,256,1024]{2,1,0:T(8,128)(2,1)}, u32[]{:S(2)}) copy-start(bf16[2,256,1024]{2,1,0:T(8,128)(2,1)} %param.20) | copy-start | bytes 3145732
  53.1 28.2 %all-gather.7.cloned.1.call-start = ((), (), s32[]{:S(2)}) async-start(), calls=%async_computation.6 | async-start | bytes 3145728 | tf_op jit(solution)/shard_map/all_gather | solution.py:293
  53.3 16.3 %copy-start.33 = (bf16[2048]{0:T(1024)(128)(2,1)S(1)}, bf16[2048]{0:T(1024)(128)(2,1)}, u32[]{:S(2)}) copy-start(bf16[2048]{0:T(1024)(128)(2,1)} %param.33) | copy-start | bytes 12292
  69.3 60.6 %reduce-scatter.7.cloned.1.call-start = ((), (), s32[]{:S(2)}) async-start(), calls=%async_computation.7 | async-start | bytes 3145728 | tf_op jit(solution)/shard_map/reduce_scatter | solution.py:296
  91.5 19.7 %copy-start.12 = (f32[2,512,2048]{2,1,0:T(8,128)}, f32[2,512,2048]{2,1,0:T(8,128)S(1)}, u32[]{:S(2)}) copy-start(f32[2,512,2048]{2,1,0:T(8,128)S(1)} %get-tuple-element.94) | copy-start | bytes 25165828
  91.5 21.6 %copy-start.42 = (bf16[2048,1024]{1,0:T(8,128)(2,1)S(1)}, bf16[2048,1024]{1,0:T(8,128)(2,1)}, u32[]{:S(2)}) copy-start(bf16[2048,1024]{1,0:T(8,128)(2,1)} %param.34) | copy-start | bytes 12582916
  113.1 5.8 copy-start.37
  113.1 5.8 copy-start.38
  113.1 5.8 copy-start.39
  118.8 31.1 %all-gather.9.cloned.1.call-start = ((), (), s32[]{:S(2)}) async-start(), calls=%async_computation.8 | async-start | bytes 3145728 | tf_op jit(solution)/shard_map/all_gather | solution.py:308
  137.9 41.7 %reduce-scatter.9.cloned.1.call-start = ((), (), s32[]{:S(2)}) async-start(), calls=%async_computation.9 | async-start | bytes 3145728 | tf_op jit(solution)/shard_map/reduce_scatter | solution.py:313
  149.9 12.9 %copy-start.43 = (bf16[1024,2048]{1,0:T(8,128)(2,1)S(1)}, bf16[1024,2048]{1,0:T(8,128)(2,1)}, u32[]{:S(2)}) copy-start(bf16[1024,2048]{1,0:T(8,128)(2,1)} %param.32) | copy-start | bytes 12582916
  168.5 98.9 %all-gather.11.cloned.1.call-start = ((), (), s32[]{:S(2)}) async-start(), calls=%async_computation.10 | async-start | bytes 3145728 | tf_op jit(solution)/shard_map/all_gather | solution.py:321
  186.8 510.0 %reduce-scatter.11.cloned.1.call-start = ((), (), s32[]{:S(2)}) async-start(), calls=%async_computation.11 | async-start | bytes 3145728 | tf_op jit(solution)/shard_map/reduce_scatter | solution.py:364
  198.8 11.8 %copy-start.48 = (bf16[2,512,1024]{2,1,0:T(8,128)(2,1)S(1)}, bf16[2,512,1024]{2,1,0:T(8,128)(2,1)}, u32[]{:S(2)}) copy-start(bf16[2,512,1024]{2,1,0:T(8,128)(2,1)} %all-gather.7.cloned.1.call-done) | copy-start | bytes 6291460
  271.3 6.2 copy-start.26
  277.4 45.1 %copy-start.19 = (bf16[2,8,64,512]{3,2,1,0:T(8,128)(2,1)}, bf16[2,8,64,512]{3,2,1,0:T(8,128)(2,1)S(1)}, u32[]{:S(2)}) copy-start(bf16[2,8,64,512]{3,2,1,0:T(8,128)(2,1)S(1)} %get-tuple-element.98) | copy-start | bytes 3145732
  277.5 20.5 %copy-start.14 = (bf16[2,512,512]{1,2,0:T(8,128)(2,1)S(1)}, bf16[2,512,512]{1,2,0:T(8,128)(2,1)}, u32[]{:S(2)}) copy-start(bf16[2,512,512]{1,2,0:T(8,128)(2,1)} %copy-done.13) | copy-start | bytes 3145732
  298.0 5.8 copy-start.4
  298.0 6.0 copy-start.18
  692.0 4.8 copy-start.10
  692.0 7.3 %copy-start.1 = (bf16[512,1024]{1,0:T(8,128)(2,1)S(1)}, bf16[512,1024]{1,0:T(8,128)(2,1)}, u32[]{:S(2)}) copy-start(bf16[512,1024]{1,0:T(8,128)(2,1)} %param.28) | copy-start | bytes 3145732
  (27 other events, 77.6 us)
Sparse Core Ops, SparseCore 0:
  9.6 13.2 all-gather.4
  53.3 10.8 reduce-scatter.4
  69.5 11.8 all-gather.6
  118.9 10.9 reduce-scatter.6
  138.0 11.8 all-gather.8
  168.6 10.9 reduce-scatter.8
  186.9 11.8 all-gather.10
  325.4 9.9 reduce-scatter.10

commit v2 on v0

v2 whole, which is shorter than its diff:
```python
import functools
import jax, jax.numpy as jnp
from jax import lax
from jax.experimental import pallas as pl
from jax.experimental.pallas import tpu as pltpu
from jax.sharding import PartitionSpec as P

MESH = pl.DeviceIdType.MESH
F32, BF16 = jnp.float32, jnp.bfloat16
EPS = 1e-12
NEG = -1e30
LIMIT = 64 * 1000 * 1000


def dot(a, b):
    return jnp.dot(a, b, preferred_element_type=F32)


def dot_t(a, b):
    return lax.dot_general(a, b, (((1,), (1,)), ((), ())), preferred_element_type=F32)


def t_dot(a, b):
    return lax.dot_general(a, b, (((0,), (0,)), ((), ())), preferred_element_type=F32)


def meet(partner):
    barrier = pltpu.get_barrier_semaphore()
    pl.semaphore_signal(barrier, inc=1, device_id={"head": partner}, device_id_type=MESH)
    pl.semaphore_wait(barrier, 1)


def to_partner(src, dst, sems, i, partner):
    return pltpu.make_async_remote_copy(
        src_ref=src, dst_ref=dst, send_sem=sems.at[0, i], recv_sem=sems.at[1, i],
        device_id={"head": partner}, device_id_type=MESH)


def vmem(count):
    return [pl.BlockSpec(memory_space=pltpu.VMEM)] * count


def project_kernel(seqs, part, x, wq, wk, wv, bias, rows, q, k, v, got, sems):
    me = lax.axis_index("head")
    other = 1 - me
    meet(other)
    for s in range(seqs):
        to_partner(x.at[s], got.at[s], sems, s, other).start()

    def emit(block, s, p):
        at = pl.ds(pl.multiple_of((2 * s + p) * part, part), part)
        rows[at, :] = block
        q[at, :] = (dot(block, wq[...]) + bias[0:1, :]).astype(BF16)
        k[at, :] = dot(block, wk[...]).astype(BF16)
        v[at, :] = (dot(block, wv[...]) + bias[1:2, :]).astype(BF16)

    def own(s, _):
        emit(x[s], s, me)
        return 0

    lax.fori_loop(0, seqs, own, 0)
    for s in range(seqs):
        to_partner(x.at[s], got.at[s], sems, s, other).wait()

    def theirs(s, _):
        emit(got[s], s, other)
        return 0

    lax.fori_loop(0, seqs, theirs, 0)


def project_rows(x, wq, wk, wv, bias):
    seqs, part, width = x.shape
    total, cols = 2 * seqs * part, wq.shape[1]
    out = jax.ShapeDtypeStruct((total, cols), BF16)
    return pl.pallas_call(
        functools.partial(project_kernel, seqs, part),
        out_shape=(jax.ShapeDtypeStruct((total, width), BF16), out, out, out),
        in_specs=vmem(5), out_specs=tuple(vmem(4)),
        scratch_shapes=[pltpu.VMEM(x.shape, BF16), pltpu.SemaphoreType.DMA((2, seqs))],
        compiler_params=pltpu.CompilerParams(collective_id=1, has_side_effects=True, vmem_limit_bytes=LIMIT),
        name="project_rows",
    )(x, wq, wk, wv, bias)


def attend_kernel(block, head, lengths, q, k, v, prior, score, c, norm):
    full = k.shape[0]
    live = lax.broadcasted_iota(jnp.int32, (1, full), 1) < lengths[pl.program_id(0)]
    first = lax.broadcasted_iota(jnp.int32, (1, 2 * head), 1) < head
    scale = head ** -0.5
    for r in range(0, full, block):
        rows = pl.ds(r, block)
        queries = q[rows, :]
        parts, norms = [], []
        for h in range(2):
            mine = jnp.where(first == (h == 0), queries, jnp.zeros_like(queries))
            scores = dot_t(mine, k[...]) * scale + prior[0, h, rows, :].astype(F32)
            score[0, h, rows, :] = scores.astype(BF16)
            masked = jnp.where(live, scores, NEG)
            top = jnp.max(masked, axis=-1, keepdims=True)
            terms = jnp.exp(masked - top)
            total = jnp.sum(terms, axis=-1, keepdims=True)
            probs = (terms * (1.0 / total)).astype(BF16)
            parts.append(dot(probs, v[...]))
            norms.append(top + jnp.log(total))
        c[rows, :] = jnp.where(first, parts[0], parts[1]).astype(BF16)
        norm[0, 0, rows, :] = jnp.where(first, norms[0], norms[1])


def attend(lengths, q, k, v, prior):
    seqs, heads, full, _ = prior.shape
    pair = q.shape[1] // heads * 2
    rows = pl.BlockSpec((full, pair), lambda s, h, n: (s, h))
    big = pl.BlockSpec((1, 2, full, full), lambda s, h, n: (s, h, 0, 0))
    norm = pl.BlockSpec((1, 1, full, pair), lambda s, h, n: (s, h, 0, 0))
    return pl.pallas_call(
        functools.partial(attend_kernel, 256, pair // 2),
        grid_spec=pltpu.PrefetchScalarGridSpec(
            num_scalar_prefetch=1, grid=(seqs, heads // 2),
            in_specs=[rows, rows, rows, big], out_specs=(big, rows, norm)),
        out_shape=(jax.ShapeDtypeStruct(prior.shape, BF16), jax.ShapeDtypeStruct(q.shape, BF16),
                   jax.ShapeDtypeStruct((seqs, heads // 2, full, pair), F32)),
        compiler_params=pltpu.CompilerParams(vmem_limit_bytes=40 << 20),
        name="attend",
    )(lengths, q, k, v, prior)


def attend_back_kernel(block, head, lengths, q, k, v, dc, prior, norm, given, grad, dq, dk, dv):
    full = k.shape[0]
    live = lax.broadcasted_iota(jnp.int32, (1, full), 1) < lengths[pl.program_id(0)]
    first = lax.broadcasted_iota(jnp.int32, (1, 2 * head), 1) < head
    scale = head ** -0.5
    q_t, dc_t = q[...].T, dc[...].T
    dk_t, dv_t = [0.0, 0.0], [0.0, 0.0]
    for r in range(0, full, block):
        rows = pl.ds(r, block)
        queries, cots = q[rows, :], dc[rows, :]
        parts = []
        for h in range(2):
            mine = first == (h == 0)
            scores = dot_t(jnp.where(mine, queries, jnp.zeros_like(queries)), k[...]) * scale
            scores = scores + prior[0, h, rows, :].astype(F32)
            probs = jnp.exp(jnp.where(live, scores, NEG) - norm[0, 0, rows, h * head:h * head + 1])
            dp = dot_t(jnp.where(mine, cots, jnp.zeros_like(cots)), v[...])
            delta = jnp.sum(probs * dp, axis=-1, keepdims=True)
            ds = (probs * (dp - delta) + given[0, h, rows, :].astype(F32)).astype(BF16)
            grad[0, h, rows, :] = ds
            parts.append(dot(ds, k[...]))
            lanes = slice(h * head, (h + 1) * head)
            dk_t[h] = dk_t[h] + dot(q_t[lanes, r:r + block], ds)
            dv_t[h] = dv_t[h] + dot(dc_t[lanes, r:r + block], probs.astype(BF16))
        dq[rows, :] = (jnp.where(first, parts[0], parts[1]) * scale).astype(BF16)
    dk[...] = (jnp.concatenate(dk_t, axis=0) * scale).T.astype(BF16)
    dv[...] = jnp.concatenate(dv_t, axis=0).T.astype(BF16)


def attend_back(lengths, q, k, v, dc, prior, norm, given):
    seqs, heads, full, _ = prior.shape
    pair = q.shape[1] // heads * 2
    rows = pl.BlockSpec((full, pair), lambda s, h, n: (s, h))
    big = pl.BlockSpec((1, 2, full, full), lambda s, h, n: (s, h, 0, 0))
    norms = pl.BlockSpec((1, 1, full, pair), lambda s, h, n: (s, h, 0, 0))
    flat = jax.ShapeDtypeStruct(q.shape, BF16)
    return pl.pallas_call(
        functools.partial(attend_back_kernel, 256, pair // 2),
        grid_spec=pltpu.PrefetchScalarGridSpec(
            num_scalar_prefetch=1, grid=(seqs, heads // 2),
            in_specs=[rows, rows, rows, rows, big, norms, big], out_specs=(big, rows, rows, rows)),
        out_shape=(jax.ShapeDtypeStruct(prior.shape, BF16), flat, flat, flat),
        compiler_params=pltpu.CompilerParams(vmem_limit_bytes=40 << 20),
        name="attend_back",
    )(lengths, q, k, v, dc, prior, norm, given)


def fold(value):
    return jnp.sum(value.reshape(value.shape[0] // 8, 8, value.shape[1]), axis=0)


def norm_stats(z):
    mean = jnp.mean(z, axis=-1, keepdims=True)
    centred = z - mean
    r = lax.rsqrt(jnp.mean(centred * centred, axis=-1, keepdims=True) + EPS)
    return centred * r, r


def norm_back(cot, gain, unit, r):
    e = cot * gain
    return r * (e - jnp.mean(e, axis=-1, keepdims=True) - unit * jnp.mean(e * unit, axis=-1, keepdims=True))


def middle_kernel(seqs, part, c, x, wo, wi, wf, vec, b_inner, gout,
                  out, dz1, dc, g_wo, g_wi, g_wf, small, g_bi,
                  unit1, r1, dz2, hn, act, slope, df, du, da, give, got, own, sums, bsum, sems):
    me = lax.axis_index("head")
    other = 1 - me
    width = x.shape[2]
    hidden = wi.shape[1]
    tile = 512
    sub = 64
    meet(other)
    b_output, gain1, shift1, b_outer, gain2, shift2 = [vec[i:i + 1, :] for i in range(6)]
    sums[...] = jnp.zeros_like(sums)
    bsum[...] = jnp.zeros_like(bsum)

    def rows_of(s, p):
        return pl.ds(pl.multiple_of((2 * s + p) * part, part), part)

    def at(start, size):
        return pl.ds(pl.multiple_of(start, size), size)

    def attn_part(s, _):
        give[s] = dot(c[rows_of(s, other), :], wo[...]).astype(BF16)
        return 0
    for s in range(seqs):
        attn_part(s, 0)
        to_partner(give.at[s], got.at[0, s], sems, s, other).start()

    def attn_own(s, _):
        own[s] = dot(c[rows_of(s, me), :], wo[...]).astype(BF16)
        return 0
    lax.fori_loop(0, seqs, attn_own, 0)
    for s in range(seqs):
        to_partner(give.at[s], got.at[0, s], sems, s, other).wait()

        def first_norm(i, _):
            rows = at(i * sub, sub)
            z = x[s, rows, :].astype(F32) + (own[s, rows, :].astype(F32) + got[0, s, rows, :].astype(F32)) + b_output
            unit, r = norm_stats(z)
            unit1[s, rows, :] = unit
            r1[s, rows, :] = jnp.broadcast_to(r, (sub, 128))
            hn[at((2 * s + me) * part + i * sub, sub), :] = (unit * gain1 + shift1).astype(BF16)
            return 0
        lax.fori_loop(0, part // sub, first_norm, 0)
        block = hn.at[rows_of(s, me)]
        to_partner(block, block, sems, seqs + s, other).start()

    order = [(0, me)] + [(s, other) for s in range(seqs)] + [(s, me) for s in range(1, seqs)]

    def inner(s, p):
        rows = rows_of(s, p)

        def columns(j, _):
            cols = at(j * tile, tile)
            u = dot(hn[rows, :], wi[:, cols]) + b_inner[:, cols]
            cdf = 0.5 * (1.0 + lax.erf(u * 0.7071067811865476))
            act[rows, cols] = (u * cdf).astype(BF16)
            slope[rows, cols] = cdf + u * (jnp.exp(-0.5 * u * u) * 0.3989422804014327)
            return 0
        lax.fori_loop(0, hidden // tile, columns, 0)

    def outer(s, p, place):
        rows = rows_of(s, p)

        def columns(j, _):
            cols = at(j * tile, tile)
            place[s, :, cols] = dot(act[rows, :], wf[:, cols]).astype(BF16)
            return 0
        lax.fori_loop(0, width // tile, columns, 0)

    for n, (s, p) in enumerate(order):
        if n == 1:
            for q in range(seqs):
                block = hn.at[rows_of(q, me)]
                to_partner(block, block, sems, seqs + q, other).wait()
        inner(s, p)
        if p is other:
            outer(s, p, give.at[pl.ds(seqs, seqs)])
            to_partner(give.at[seqs + s], got.at[1, s], sems, 2 * seqs + s, other).start()
        else:
            outer(s, p, own)

    for s in range(seqs):
        to_partner(give.at[seqs + s], got.at[1, s], sems, 2 * seqs + s, other).wait()

        def second_norm(i, _):
            rows = at(i * sub, sub)
            h = unit1[s, rows, :] * gain1 + shift1
            z = (own[s, rows, :].astype(F32) + got[1, s, rows, :].astype(F32)) + b_outer + h
            unit, r = norm_stats(z)
            out[s, rows, :] = (unit * gain2 + shift2).astype(BF16)
            g = gout[s, rows, :].astype(F32)
            d = norm_back(g, gain2, unit, r)
            dz2[s, rows, :] = d
            df[at((2 * s + me) * part + i * sub, sub), :] = d.astype(BF16)
            sums[3] += fold(d)
            sums[4] += fold(g * unit)
            sums[5] += fold(g)
            return 0
        lax.fori_loop(0, part // sub, second_norm, 0)
        block = df.at[rows_of(s, me)]
        to_partner(block, block, sems, 3 * seqs + s, other).start()

    def inner_back(s, p):
        rows = rows_of(s, p)

        def columns(j, _):
            cols = at(j * tile, tile)
            dg = dot_t(df[rows, :], wf[cols, :]).astype(BF16).astype(F32)
            low = (dg * slope[rows, cols]).astype(BF16)
            du[rows, cols] = low
            bsum[:, cols] += fold(low.astype(F32))
            return 0
        lax.fori_loop(0, hidden // tile, columns, 0)

    def outer_back(s, p, place):
        rows = rows_of(s, p)

        def columns(j, _):
            cols = at(j * tile, tile)
            place[s, :, cols] = dot_t(du[rows, :], wi[cols, :]).astype(BF16)
            return 0
        lax.fori_loop(0, width // tile, columns, 0)

    for n, (s, p) in enumerate(order):
        if n == 1:
            for q in range(seqs):
                block = df.at[rows_of(q, me)]
                to_partner(block, block, sems, 3 * seqs + q, other).wait()
        inner_back(s, p)
        if p is other:
            outer_back(s, p, give.at[pl.ds(2 * seqs, seqs)])
            to_partner(give.at[2 * seqs + s], got.at[2, s], sems, 4 * seqs + s, other).start()
        else:
            outer_back(s, p, own)

    for s in range(seqs):
        to_partner(give.at[2 * seqs + s], got.at[2, s], sems, 4 * seqs + s, other).wait()

        def first_back(i, _):
            rows = at(i * sub, sub)
            cot = dz2[s, rows, :] + (own[s, rows, :].astype(F32) + got[2, s, rows, :].astype(F32))
            unit = unit1[s, rows, :]
            d = norm_back(cot, gain1, unit, r1[s, rows, 0:1])
            dz1[s, rows, :] = d
            da[at((2 * s + me) * part + i * sub, sub), :] = d.astype(BF16)
            sums[0] += fold(d)
            sums[1] += fold(cot * unit)
            sums[2] += fold(cot)
            return 0
        lax.fori_loop(0, part // sub, first_back, 0)
        block = da.at[rows_of(s, me)]
        to_partner(block, block, sems, 5 * seqs + s, other).start()

    def grad_inner(j, _):
        cols = at(j * tile, tile)
        g_wi[:, cols] = t_dot(hn[...], du[:, cols]).astype(BF16)
        return 0
    lax.fori_loop(0, hidden // tile, grad_inner, 0)

    def grad_outer(j, _):
        cols = at(j * tile, tile)
        g_wf[cols, :] = t_dot(act[:, cols], df[...]).astype(BF16)
        return 0
    lax.fori_loop(0, hidden // tile, grad_outer, 0)

    for s in range(seqs):
        block = da.at[rows_of(s, me)]
        to_partner(block, block, sems, 5 * seqs + s, other).wait()
    dc[...] = dot_t(da[...], wo[...]).astype(BF16)
    g_wo[...] = t_dot(c[...], da[...]).astype(BF16)
    small[...] = jnp.sum(sums[...], axis=1)
    g_bi[...] = jnp.sum(bsum[...], axis=0, keepdims=True)


def middle(c, x, wo, wi, wf, vec, b_inner, gout):
    seqs, part, width = x.shape
    total, cols = c.shape
    hidden = wi.shape[1]
    sds = jax.ShapeDtypeStruct
    return pl.pallas_call(
        functools.partial(middle_kernel, seqs, part),
        out_shape=(sds(x.shape, BF16), sds(x.shape, F32), sds(c.shape, BF16), sds(wo.shape, BF16),
                   sds(wi.shape, BF16), sds(wf.shape, BF16), sds((6, width), F32), sds((1, hidden), F32)),
        in_specs=vmem(8), out_specs=tuple(vmem(8)),
        scratch_shapes=[
            pltpu.VMEM(x.shape, F32), pltpu.VMEM((seqs, part, 128), F32), pltpu.VMEM(x.shape, F32),
            pltpu.VMEM((total, width), BF16), pltpu.VMEM((total, hidden), BF16), pltpu.VMEM((total, hidden), F32),
            pltpu.VMEM((total, width), BF16), pltpu.VMEM((total, hidden), BF16), pltpu.VMEM((total, width), BF16),
            pltpu.VMEM((3 * seqs, part, width), BF16), pltpu.VMEM((3, seqs, part, width), BF16),
            pltpu.VMEM(x.shape, BF16), pltpu.VMEM((6, 8, width), F32), pltpu.VMEM((8, hidden), F32),
            pltpu.SemaphoreType.DMA((2, 6 * seqs)),
        ],
        compiler_params=pltpu.CompilerParams(collective_id=2, has_side_effects=True, vmem_limit_bytes=LIMIT),
        name="middle",
    )(c, x, wo, wi, wf, vec, b_inner, gout)


def project_back_kernel(seqs, part, rows, dq, dk, dv, wq, wk, wv, dz1,
                        gin, g_q, g_k, g_v, g_b, give, got, sems):
    me = lax.axis_index("head")
    other = 1 - me
    meet(other)

    def total_of(s, p):
        at = pl.ds(pl.multiple_of((2 * s + p) * part, part), part)
        return dot_t(dq[at, :], wq[...]) + dot_t(dk[at, :], wk[...]) + dot_t(dv[at, :], wv[...])

    for s in range(seqs):
        give[s] = total_of(s, other).astype(BF16)
        to_partner(give.at[s], got.at[s], sems, s, other).start()
    g_q[...] = t_dot(rows[...], dq[...]).astype(BF16)
    g_k[...] = t_dot(rows[...], dk[...]).astype(BF16)
    g_v[...] = t_dot(rows[...], dv[...]).astype(BF16)
    g_b[0:1, :] = jnp.sum(fold(dq[...].astype(F32)), axis=0, keepdims=True)
    g_b[1:2, :] = jnp.sum(fold(dv[...].astype(F32)), axis=0, keepdims=True)
    for s in range(seqs):
        own = total_of(s, me).astype(BF16)
        to_partner(give.at[s], got.at[s], sems, s, other).wait()
        gin[s] = (dz1[s] + (own.astype(F32) + got[s].astype(F32))).astype(BF16)


def project_back(rows, dq, dk, dv, wq, wk, wv, dz1):
    seqs, part, width = dz1.shape
    sds = jax.ShapeDtypeStruct
    grad = sds(wq.shape, BF16)
    return pl.pallas_call(
        functools.partial(project_back_kernel, seqs, part),
        out_shape=(sds(dz1.shape, BF16), grad, grad, grad, sds((2, wq.shape[1]), F32)),
        in_specs=vmem(8), out_specs=tuple(vmem(5)),
        scratch_shapes=[pltpu.VMEM(dz1.shape, BF16), pltpu.VMEM(dz1.shape, BF16), pltpu.SemaphoreType.DMA((2, seqs))],
        compiler_params=pltpu.CompilerParams(collective_id=3, has_side_effects=True, vmem_limit_bytes=LIMIT),
        name="project_back",
    )(rows, dq, dk, dv, wq, wk, wv, dz1)
def grid_bits(n):
    bits = n.bit_length() - 1
    side = bits // 3
    return (0, side, 2 * side), bits


def chunk_plan(n, color):
    (bx, by, bz), bits = grid_bits(n)
    order = ((bx, by, bz), (by, bx, bz), (bz, bx, by), (bz, by, bx))[color]
    rest = [b for b in range(bits) if b not in order]
    stages = [("scatter", b) for b in order] + [("double", b) for b in rest]
    return stages + [("gather", b) for b in reversed(order)]


def event_order(n, colors):
    (bx, by, bz), _ = grid_bits(n)
    plans = [chunk_plan(n, c) for c in colors]
    free, ready = [0.0] * 3, [0.0] * len(colors)
    step, length = [0] * len(colors), [1.0] * len(colors)
    events = []
    for _ in range(sum(len(p) for p in plans)):
        best = None
        for c, plan in enumerate(plans):
            if step[c] < len(plan):
                axis = (plan[step[c]][1] >= by) + (plan[step[c]][1] >= bz)
                key = (max(ready[c], free[axis]), -step[c], c, axis)
                best = key if best is None or key < best else best
        start, _, c, axis = best
        kind, b = plans[c][step[c]]
        length[c] *= 0.5 if kind == "scatter" else 1.0
        free[axis] = start + length[c] * (2 if b != (bx, by, bz)[axis] else 1)
        length[c] *= 2.0 if kind == "gather" else 1.0
        ready[c] = free[axis] + 0.08
        events.append((start, c, step[c]))
        step[c] += 1
    return [(c, s) for _, c, s in sorted(events)]


def flip(index, bit):
    return index + (1 - 2 * ((index // (1 << bit)) % 2)) * (1 << bit)


def chunk_pieces(shapes, rows, width):
    chunks = []
    for i, (height, cols) in enumerate(shapes):
        per = max(1, width // cols)
        for r in range(0, height, rows * per):
            for col in range(0, cols, width):
                span = min(cols, width)
                chunks.append([(i, r + j * rows, col, span, j * span) for j in range(per)])
    return chunks


def reduce_kernel(n, colors, rows, pieces, count, *refs):
    grads, tiny = refs[:count], refs[count]
    sums, tiny_out = refs[count + 1:2 * count + 1], refs[2 * count + 1]
    work, got, full, hold, tiny_got, load_sem, save_sem, send_sem, recv_sem, tiny_sem = refs[2 * count + 2:]
    nc = len(colors)
    me, head = lax.axis_index("batch"), lax.axis_index("head")
    _, bits = grid_bits(n)

    def moves(c, out):
        for k, (i, r, col, span, at) in enumerate(pieces[c]):
            outside = (sums if out else grads)[i].at[pl.ds(r, rows), pl.ds(col, span)]
            inside = (full if out else work).at[c, :, pl.ds(at, span)]
            if out:
                yield pltpu.make_async_copy(inside, outside, save_sem.at[c, k])
            else:
                yield pltpu.make_async_copy(outside, inside, load_sem.at[c, k])

    for c in range(nc):
        for move in moves(c, False):
            move.start()
    hold[...] = tiny[...]
    barrier = pltpu.get_barrier_semaphore()
    for b in range(bits):
        pl.semaphore_signal(barrier, inc=1, device_id={"batch": flip(me, b)}, device_id_type=MESH)
    pl.semaphore_signal(barrier, inc=1, device_id={"head": 1 - head}, device_id_type=MESH)
    pl.semaphore_wait(barrier, bits + 1)

    plans = [chunk_plan(n, c) for c in colors]
    bit_of = [(me // (1 << b)) % 2 for b in range(bits)]
    spans = []
    for c in range(nc):
        off, length, at, row = 0, rows, 0, []
        for kind, b in plans[c]:
            if kind == "scatter":
                length //= 2
                row.append((off + bit_of[b] * length, off + (1 - bit_of[b]) * length, length, at))
                off, at = row[-1][0], at + length
            elif kind == "double":
                row.append((off, off, length, at))
                at += length
            else:
                row.append((off, off, length, 0))
                off, length = off - bit_of[b] * length, 2 * length
        spans.append(row)

    def copy_of(c, s):
        kind, b = plans[c][s]
        _, start, length, at = spans[c][s]
        place = (c, pl.ds(pl.multiple_of(start, 16), length))
        if kind == "gather":
            src, dst = full.at[place], full.at[place]
        else:
            src, dst = work.at[place], got.at[c, pl.ds(at, length)]
        return pltpu.make_async_remote_copy(
            src_ref=src, dst_ref=dst, send_sem=send_sem.at[c, s], recv_sem=recv_sem.at[c, s],
            device_id={"batch": flip(me, b)}, device_id_type=MESH)

    def finish(c, s):
        keep, _, length, at = spans[c][s]
        copy_of(c, s).wait()
        if plans[c][s][0] != "gather":
            target = full if plans[c][s + 1][0] == "gather" else work

            def add(i, _):
                here = pl.ds(pl.multiple_of(keep + i * 16, 16), 16)
                there = pl.ds(pl.multiple_of(at + i * 16, 16), 16)
                target[c, here, :] = (work[c, here, :].astype(F32) + got[c, there, :].astype(F32)).astype(BF16)
                return 0
            lax.fori_loop(0, length // 16, add, 0)

    def tiny_copy(k):
        rest = hold.at[pl.ds(0, 8)] if k == 0 else hold
        there = tiny_got.at[k, pl.ds(0, 8)] if k == 0 else tiny_got.at[k]
        target = {"head": 1 - head} if k == 0 else {"batch": flip(me, k - 1)}
        return pltpu.make_async_remote_copy(
            src_ref=rest, dst_ref=there, send_sem=tiny_sem.at[0, k], recv_sem=tiny_sem.at[1, k],
            device_id=target, device_id_type=MESH)

    def tiny_finish(k):
        tiny_copy(k).wait()
        if k == 0:
            hold[0:8, :] += tiny_got[0, 0:8, :]
        else:
            hold[...] += tiny_got[k]

    events = event_order(n, colors)
    gap = len(events) // (bits + 2)
    for e, (c, s) in enumerate(events):
        if s == 0:
            for move in moves(c, False):
                move.wait()
        else:
            finish(c, s - 1)
        copy_of(c, s).start()
        if e % gap == 0 and e // gap <= bits:
            k = e // gap
            if k > 0:
                tiny_finish(k - 1)
            tiny_copy(k).start()
    tiny_finish(bits)
    tiny_out[...] = hold[...]
    for c in range(nc):
        finish(c, len(plans[c]) - 1)
        for move in moves(c, True):
            move.start()
    for c in range(nc):
        for move in moves(c, True):
            move.wait()


def reduce_gradients(grads, tiny, n, rows=256):
    width = tiny.shape[1]
    pieces = chunk_pieces([g.shape for g in grads], rows, width)
    nc = len(pieces)
    colors = [c % 2 for c in range(nc)]
    stages = len(chunk_plan(n, 0))
    _, bits = grid_bits(n)
    got_rows = rows - rows // 8 + (bits - 3) * rows // 8
    hbm = [pl.BlockSpec(memory_space=pl.ANY)] * len(grads)
    done = pl.pallas_call(
        functools.partial(reduce_kernel, n, colors, rows, pieces, len(grads)),
        out_shape=tuple(jax.ShapeDtypeStruct(g.shape, g.dtype) for g in (*grads, tiny)),
        in_specs=hbm + vmem(1), out_specs=tuple(hbm + vmem(1)),
        scratch_shapes=[
            pltpu.VMEM((nc, rows, width), BF16), pltpu.VMEM((nc, got_rows, width), BF16),
            pltpu.VMEM((nc, rows, width), BF16), pltpu.VMEM(tiny.shape, F32),
            pltpu.VMEM((bits + 1,) + tiny.shape, F32),
            pltpu.SemaphoreType.DMA((nc, 2)), pltpu.SemaphoreType.DMA((nc, 2)),
            pltpu.SemaphoreType.DMA((nc, stages)), pltpu.SemaphoreType.DMA((nc, stages)),
            pltpu.SemaphoreType.DMA((2, bits + 1)),
        ],
        compiler_params=pltpu.CompilerParams(collective_id=0, has_side_effects=True, vmem_limit_bytes=LIMIT),
        name="reduce_gradients",
    )(*grads, tiny)
    return done[:-1], done[-1]
def on_device(n_batch, inputs, prior_scores, lengths, w_query, w_key, w_value, b_query, b_value, w_output, b_output,
              gain_attn, shift_attn, w_inner, b_inner, w_outer, b_outer, gain_ffn, shift_ffn, grad_out, grad_scores):
    width = inputs.shape[2]
    bias = jnp.stack([b_query, b_value]).astype(F32)
    vec = jnp.stack([b_output, gain_attn, shift_attn, b_outer, gain_ffn, shift_ffn]).astype(F32)
    rows, q, k, v = project_rows(inputs, w_query, w_key, w_value, bias)
    new_scores, context, norm = attend(lengths, q, k, v, prior_scores)
    outputs, dz1, dc, g_wo, g_wi, g_wf, small, g_bi = middle(
        context, inputs, w_output, w_inner, w_outer, vec, b_inner.astype(F32)[None], grad_out)
    grad_prior, dq, dk, dv = attend_back(lengths, q, k, v, dc, prior_scores, norm, grad_scores)
    grad_inputs, g_wq, g_wk, g_wv, g_b = project_back(rows, dq, dk, dv, w_query, w_key, w_value, dz1)
    pad = lambda a, to: jnp.pad(a, ((0, to - a.shape[0]), (0, 0)))
    mine = jnp.concatenate([g_bi.reshape(-1, width), g_b.reshape(-1, width)])
    tiny = jnp.concatenate([pad(small, 8), pad(mine, 8)])
    grads, tiny = reduce_gradients((g_wi, g_wf, g_wo, g_wq, g_wk, g_wv), tiny, n_batch)
    g_wi, g_wf, g_wo, g_wq, g_wk, g_wv = [g.astype(F32) for g in grads]
    g_bi = tiny[8:8 + g_bi.size // width].reshape(-1)
    g_b = tiny[8 + g_bi.size // width:8 + mine.shape[0]].reshape(g_b.shape)
    return (outputs, new_scores, grad_inputs, grad_prior, g_wq, g_wk, g_wv, g_b[0], g_b[1], g_wo,
            tiny[0], tiny[1], tiny[2], g_wi, g_bi, g_wf, tiny[3], tiny[4], tiny[5])


def solution(mesh):
    seq, scores, whole = P("batch", "head", None), P("batch", "head", None, None), P()
    down, across, vector = P("head", None), P(None, "head"), P("head")
    in_specs = (seq, scores, P("batch"), across, across, across, vector, vector, down, whole, whole, whole,
                across, vector, down, whole, whole, whole, seq, scores)
    out_specs = (seq, scores, seq, scores, across, across, across, vector, vector, down, whole, whole, whole,
                 across, vector, down, whole, whole, whole)
    layer = functools.partial(on_device, mesh.shape["batch"])
    return jax.shard_map(layer, mesh=mesh, in_specs=in_specs, out_specs=out_specs, check_vma=False)
```

time: 1020 us -> 390 us (0.38)
  waiting for transfers between devices: 546 us -> 0 us
  Pallas kernels: 0 us -> 348 us
  matrix products: 146 us -> 0 us
  blocking collectives: 125 us -> 0 us
  local copies, waits for them, and re-layouts: 108 us -> 19.4 us
  other arithmetic: 70.6 us -> 20.8 us
  between operations: 15.7 us -> 0.91 us
    psum x1 -> x0, waiting for transfers between devices: 496 us -> none  [on_device(): final_grads = lax.psum(weight_totals, 'batch')]
    pallas_call x0 -> x6, Pallas kernels: none -> 348 us  [the longest x1 225 us: reduce_gradients(): pl.pallas_call(functools.partial(reduce_kernel, n, colors, rows, pieces,...]
    dot_general x48 -> x0, matrix products: 146 us -> none  [the longest x12 53.1 us: project(): return jnp.dot(left_side, right_side, preferred_element_type=jnp.float32)]
    psum x2 -> x0, blocking collectives: 125 us -> none  [the longest x1 79.4 us: on_device(): final_grads = lax.psum(weight_totals, 'batch')]
    unnamed x242 -> x67, local copies, waits for them, and re-layouts: 92.6 us -> 16.2 us
    reduce_scatter x8 -> x0, waiting for transfers between devices: 25 us -> none  [the longest x2 15.4 us: on_device(): lax.psum_scatter(project(inner_act, w_outer).astype(jnp.bfloat16), 'head'...]
    reduce_sum x14 -> x0, other arithmetic: 23.8 us -> none  [the longest x2 5.32 us: layer_norm(): return centred * lax.rsqrt(row_var + EPS) * norm_gain + norm_shift]
    all_gather x8 -> x0, waiting for transfers between devices: 23.1 us -> none  [the longest x2 14.9 us: on_device(): lax.all_gather(hidden.astype(jnp.bfloat16), 'head', axis=1, tiled=True)]
  transfers between devices with their start and end apart: 17 -> 0, of which waited for: 7 -> 0; matrix products, arithmetic and copies ran while one was open for 23% -> 0% of each run, Pallas kernels for 0% -> 0%
where the time goes in v2:
time: 390 us; the launch traced here: 389 us
  Pallas kernels  348 us (89%)
  other arithmetic  20.8 us (5%)
  local copies, waits for them, and re-layouts  19.4 us (5%)
    pallas_call x1, Pallas kernels, reduce_gradients(): pl.pallas_call(functools.partial(reduce_kernel, n, colors, rows, pieces,...  225 us
    pallas_call x1, Pallas kernels, middle(): pl.pallas_call(functools.partial(middle_kernel, seqs, part), out_shape=(s...  59.1 us
    pallas_call x1, Pallas kernels, attend_back(): pl.pallas_call(functools.partial(attend_back_kernel, 256, pair // 2), gri...  23.3 us
    pallas_call x1, Pallas kernels, attend(): pl.pallas_call(functools.partial(attend_kernel, 256, pair // 2), grid_spe...  18.4 us
    convert_element_type x6, other arithmetic, on_device(): g_wi, g_wf, g_wo, g_wq, g_wk, g_wv = [g.astype(F32) for g in grads]  17.6 us
    unnamed x67, local copies, waits for them, and re-layouts  16.2 us
    pallas_call x1, Pallas kernels, project_back(): pl.pallas_call(functools.partial(project_back_kernel, seqs, part), out_sh...  14 us
    pallas_call x1, Pallas kernels, project_rows(): pl.pallas_call(functools.partial(project_kernel, seqs, part), out_shape=(...  8.48 us

profile of v2, /device:TPU:0, one launch (start us, length us, event | category | flops | bytes accessed | tf_op | source)
XLA Modules:
  0.0 389.4 jit_solution(17859996420034777364)
XLA Ops:
  0.7 0.7 stack.30
  1.4 0.7 stack.31
  2.6 8.5 %project_rows.1 = (bf16[1024,1024]{1,0:T(8,128)(2,1)}, bf16[1024,512]{1,0:T(8,128)(2,1)}, bf16[1024,512]{1,0:T(8,128)(2,1)}, bf16[1024,512]{1,0:T(8,128)(2,1)}) custom-call(bf16[2,256,1024]{2,1,0:T(8,128)(2,1)} %x.7, bf16[1024,512]{1,0:T(8,128)(2,1)} %wq.3, bf16[1024,512]{1,0:T(8,128)(2,1)} %wk.3, bf16[1024,512]{1,0:T(8,128)(2,1)} %wv.3, ...), custom_call_target="tpu_custom_call" | custom-call | tf_op jit(solution)/shard_map/project_rows/pallas_call | solution.py:76
  11.1 1.2 copy-done
  12.4 1.2 copy-done.2
  13.6 1.2 copy-done.4
  14.9 18.4 %attend.1 = (bf16[2,8,512,512]{3,2,1,0:T(8,128)(2,1)}, bf16[1024,512]{1,0:T(8,128)(2,1)S(1)}, f32[2,4,512,128]{3,2,1,0:T(8,128)S(1)}) custom-call(s32[2]{0:T(128)S(1)} %copy-done.13, bf16[1024,512]{1,0:T(8,128)(2,1)S(1)} %copy-done, bf16[1024,512]{1,0:T(8,128)(2,1)S(1)} %copy-done.2, bf16[1024,512]{1,0:T(8,128)(2,1)S(1)} %copy-done.4, ...), custom_call_target="tpu_custom_call" | custom-call | tf_op jit(solution)/shard_map/attend/pallas_call | solution.py:116
  33.2 1.3 copy-done.6
  34.6 1.0 copy-done.12
  35.7 0.6 convert_element_type.30.vec
  36.9 59.1 %middle.1 = (bf16[2,256,1024]{2,1,0:T(8,128)(2,1)}, f32[2,256,1024]{2,1,0:T(8,128)}, bf16[1024,512]{1,0:T(8,128)(2,1)}, bf16[512,1024]{1,0:T(8,128)(2,1)}, bf16[...) custom-call(bf16[1024,512]{1,0:T(8,128)(2,1)} %copy-done.12, ...), custom_call_target="tpu_custom_call" | custom-call | tf_op jit(solution)/shard_map/middle/pallas_call | solution.py:370
  96.0 1.2 copy-done.5
  97.3 1.6 copy-done.7
  98.9 1.2 copy-done.8
  100.1 23.3 %attend_back.1 = (bf16[2,8,512,512]{3,2,1,0:T(8,128)(2,1)}, bf16[1024,512]{1,0:T(8,128)(2,1)S(1)}, bf16[1024,512]{1,0:T(8,128)(2,1)S(1)}, bf16[1024,512]{1,0:T(8,128)(2,1)S(1)}) custom-call(s32[2]{0:T(128)S(1)} %copy-done.13, bf16[1024,512]{1,0:T(8,128)(2,1)S(1)} %copy-done.1, bf16[1024,512]{1,0:T(8,128)(2,1)S(1)} %copy-done.3, ...), custom_call_target="tpu_custom_call" | custom-call | tf_op jit(solution)/shard_map/attend_back/pallas_call | solution.py:164
  123.4 1.0 copy-done.9
  124.3 1.0 copy-done.10
  125.3 1.0 copy-done.11
  126.3 14.0 %project_back.1 = (bf16[2,256,1024]{2,1,0:T(8,128)(2,1)}, bf16[1024,512]{1,0:T(8,128)(2,1)}, bf16[1024,512]{1,0:T(8,128)(2,1)}, bf16[1024,512]{1,0:T(8,128)(2,1)}, f32[2,512]{1,0:T(2,128)}) custom-call(bf16[1024,1024]{1,0:T(8,128)(2,1)} %get-tuple-element.56.rows, bf16[1024,512]{1,0:T(8,128)(2,1)} %copy-done.9, bf16[1024,512]{1,0:T(8,128)(2,1)} %copy-done.10, ...), custom_call_target="tpu_custom_call" | custom-call | tf_op jit(solution)/shard_map/project_back/pallas_call | solution.py:416
  140.3 0.7 copy.39
  141.5 0.7 reduce.3
  142.2 0.6 select_maximum_fusion.refs_6_
  142.8 225.1 %reduce_gradients.1 = (bf16[1024,2048]{1,0:T(8,128)(2,1)}, bf16[2048,1024]{1,0:T(8,128)(2,1)}, bf16[512,1024]{1,0:T(8,128)(2,1)}, bf16[1024,512]{1,0:T(8,128)(2,...) custom-call(bf16[1024,2048]{1,0:T(8,128)(2,1)} %get-tuple-element.65.refs_0_, ...), custom_call_target="tpu_custom_call" | custom-call | tf_op jit(solution)/shard_map/reduce_gradients/pallas_call | solution.py:596
  368.0 6.8 %convert_element_type.35 = f32[1024,2048]{1,0:T(8,128)} convert(bf16[1024,2048]{1,0:T(8,128)(2,1)} %get-tuple-element.79) | non-fusion elementwise | flops 2097152 | bytes 12582912 | tf_op jit(solution)/shard_map/convert_element_type | solution.py:627
  374.8 4.4 %convert_element_type.36 = f32[2048,1024]{1,0:T(8,128)} convert(bf16[2048,1024]{1,0:T(8,128)(2,1)S(1)} %copy-done.14) | non-fusion elementwise | flops 2097152 | bytes 12582912 | tf_op jit(solution)/shard_map/convert_element_type | solution.py:627
  379.2 1.6 convert_element_type.31
  380.8 1.6 convert_element_type.32
  382.5 1.6 convert_element_type.33
  384.1 1.6 convert_element_type.34
  385.6 0.6 fusion
  387.5 1.0 copy.45
  388.4 1.0 copy.46
  (66 shorter events, 3.1 us)
Async XLA Ops:
  0.7 10.5 %copy-start.13 = (s32[2]{0:T(128)S(1)}, s32[2]{0:T(128)}, u32[]{:S(2)}) copy-start(s32[2]{0:T(128)} %lengths.3) | copy-start | bytes 28
  11.1 1.2 copy-start
  12.4 1.2 copy-start.2
  13.6 1.2 copy-start.4
  14.8 20.7 %copy-start.25 = (bf16[1024]{0:T(1024)(128)(2,1)S(1)}, bf16[1024]{0:T(1024)(128)(2,1)}, u32[]{:S(2)}) copy-start(bf16[1024]{0:T(1024)(128)(2,1)} %param.29) | copy-start | bytes 6148
  14.8 20.7 %copy-start.26 = (bf16[1024]{0:T(1024)(128)(2,1)S(1)}, bf16[1024]{0:T(1024)(128)(2,1)}, u32[]{:S(2)}) copy-start(bf16[1024]{0:T(1024)(128)(2,1)} %param.30) | copy-start | bytes 6148
  14.8 20.7 %copy-start.27 = (bf16[1024]{0:T(1024)(128)(2,1)S(1)}, bf16[1024]{0:T(1024)(128)(2,1)}, u32[]{:S(2)}) copy-start(bf16[1024]{0:T(1024)(128)(2,1)} %param.31) | copy-start | bytes 6148
  14.8 20.8 %copy-start.28 = (bf16[1024]{0:T(1024)(128)(2,1)S(1)}, bf16[1024]{0:T(1024)(128)(2,1)}, u32[]{:S(2)}) copy-start(bf16[1024]{0:T(1024)(128)(2,1)} %param.35) | copy-start | bytes 6148
  14.8 20.8 %copy-start.29 = (bf16[1024]{0:T(1024)(128)(2,1)S(1)}, bf16[1024]{0:T(1024)(128)(2,1)}, u32[]{:S(2)}) copy-start(bf16[1024]{0:T(1024)(128)(2,1)} %param.36) | copy-start | bytes 6148
  14.8 20.8 %copy-start.30 = (bf16[1024]{0:T(1024)(128)(2,1)S(1)}, bf16[1024]{0:T(1024)(128)(2,1)}, u32[]{:S(2)}) copy-start(bf16[1024]{0:T(1024)(128)(2,1)} %param.37) | copy-start | bytes 6148
  14.9 21.5 %copy-start.24 = (bf16[2048]{0:T(1024)(128)(2,1)S(1)}, bf16[2048]{0:T(1024)(128)(2,1)}, u32[]{:S(2)}) copy-start(bf16[2048]{0:T(1024)(128)(2,1)} %param.33) | copy-start | bytes 12292
  33.2 1.3 copy-start.6
  34.6 1.0 copy-start.12
  36.9 59.1 %copy-start.1 = (bf16[1024,512]{1,0:T(8,128)(2,1)S(1)}, bf16[1024,512]{1,0:T(8,128)(2,1)}, u32[]{:S(2)}) copy-start(bf16[1024,512]{1,0:T(8,128)(2,1)} %get-tuple-element.50.q) | copy-start | bytes 3145732
  36.9 59.1 %copy-start.3 = (bf16[1024,512]{1,0:T(8,128)(2,1)S(1)}, bf16[1024,512]{1,0:T(8,128)(2,1)}, u32[]{:S(2)}) copy-start(bf16[1024,512]{1,0:T(8,128)(2,1)} %get-tuple-element.51.k) | copy-start | bytes 3145732
  96.0 1.2 copy-start.5
  97.3 1.6 copy-start.7
  98.9 1.2 copy-start.8
  123.4 1.0 copy-start.9
  124.3 1.0 copy-start.10
  125.3 1.0 copy-start.11
  126.3 15.2 %copy-start.23 = (f32[1,2048]{1,0:T(1,128)S(1)}, f32[1,2048]{1,0:T(1,128)}, u32[]{:S(2)}) copy-start(f32[1,2048]{1,0:T(1,128)} %get-tuple-element.72) | copy-start | bytes 24580
  126.3 15.9 %copy-start.21 = (f32[6,1024]{1,0:T(8,128)S(1)}, f32[6,1024]{1,0:T(8,128)}, u32[]{:S(2)}) copy-start(f32[6,1024]{1,0:T(8,128)} %get-tuple-element.71) | copy-start | bytes 73732
  367.9 6.8 %copy-start.14 = (bf16[2048,1024]{1,0:T(8,128)(2,1)S(1)}, bf16[2048,1024]{1,0:T(8,128)(2,1)}, u32[]{:S(2)}) copy-start(bf16[2048,1024]{1,0:T(8,128)(2,1)} %get-tuple-element.80) | copy-start | bytes 12582916
  374.8 4.4 %copy-start.18 = (bf16[1024,512]{1,0:T(8,128)(2,1)S(1)}, bf16[1024,512]{1,0:T(8,128)(2,1)}, u32[]{:S(2)}) copy-start(bf16[1024,512]{1,0:T(8,128)(2,1)} %get-tuple-element.74) | copy-start | bytes 3145732
  374.8 6.1 %copy-start.17 = (bf16[1024,512]{1,0:T(8,128)(2,1)S(1)}, bf16[1024,512]{1,0:T(8,128)(2,1)}, u32[]{:S(2)}) copy-start(bf16[1024,512]{1,0:T(8,128)(2,1)} %get-tuple-element.75) | copy-start | bytes 3145732
  379.2 3.2 copy-start.16
  379.2 4.9 %copy-start.15 = (bf16[512,1024]{1,0:T(8,128)(2,1)S(1)}, bf16[512,1024]{1,0:T(8,128)(2,1)}, u32[]{:S(2)}) copy-start(bf16[512,1024]{1,0:T(8,128)(2,1)} %get-tuple-element.78) | copy-start | bytes 3145732
  380.8 4.8 %copy-start.22 = (f32[16,1024]{1,0:T(8,128)S(1)}, f32[16,1024]{1,0:T(8,128)}, u32[]{:S(2)}) copy-start(f32[16,1024]{1,0:T(8,128)} %get-tuple-element.77) | copy-start | bytes 196612
  380.8 6.6 %copy-start.19 = (bf16[2,256,1024]{2,1,0:T(8,128)(2,1)S(1)}, bf16[2,256,1024]{2,1,0:T(8,128)(2,1)}, u32[]{:S(2)}) copy-start(bf16[2,256,1024]{2,1,0:T(8,128)(2,1)} %get-tuple-element.108) | copy-start | bytes 3145732
  382.5 6.0 %copy-start.20 = (bf16[2,256,1024]{2,1,0:T(8,128)(2,1)S(1)}, bf16[2,256,1024]{2,1,0:T(8,128)(2,1)}, u32[]{:S(2)}) copy-start(bf16[2,256,1024]{2,1,0:T(8,128)(2,1)} %get-tuple-element.110) | copy-start | bytes 3145732

commit v3 on v2

--- a/solution.py
+++ b/solution.py
@@ -168,6 +168,8 @@
             in_specs=[rows, rows, rows, rows, big, norms, big], out_specs=(big, rows, rows, rows)),
         out_shape=(jax.ShapeDtypeStruct(prior.shape, BF16), flat, flat, flat),
         compiler_params=pltpu.CompilerParams(vmem_limit_bytes=40 << 20),
+        cost_estimate=pl.CostEstimate(flops=40 * full * full * seqs * heads * pair // 2, transcendentals=prior.size,
+                                      bytes_accessed=6 * prior.size),
         name="attend_back",
     )(lengths, q, k, v, dc, prior, norm, given)
 
@@ -188,8 +190,8 @@
     return r * (e - jnp.mean(e, axis=-1, keepdims=True) - unit * jnp.mean(e * unit, axis=-1, keepdims=True))
 
 
-def middle_kernel(seqs, part, c, x, wo, wi, wf, vec, b_inner, gout,
-                  out, dz1, dc, g_wo, g_wi, g_wf, small, g_bi,
+def middle_kernel(seqs, part, firsts, c, x, wo, wi, wf, vec, b_inner, gout,
+                  out, dz1, dc, g_wo, keep, give_x, give_y, give_z, small, g_bi,
                   unit1, r1, dz2, hn, act, slope, df, du, da, give, got, own, sums, bsum, sems):
     me = lax.axis_index("head")
     other = 1 - me
@@ -341,17 +343,43 @@
         block = da.at[rows_of(s, me)]
         to_partner(block, block, sems, 5 * seqs + s, other).start()
 
-    def grad_inner(j, _):
-        cols = at(j * tile, tile)
-        g_wi[:, cols] = t_dot(hn[...], du[:, cols]).astype(BF16)
-        return 0
-    lax.fori_loop(0, hidden // tile, grad_inner, 0)
-
-    def grad_outer(j, _):
-        cols = at(j * tile, tile)
-        g_wf[cols, :] = t_dot(act[:, cols], df[...]).astype(BF16)
-        return 0
-    lax.fori_loop(0, hidden // tile, grad_outer, 0)
+    mine = lax.axis_index("batch")
+    gives = (give_x, give_y, give_z)
+    half = keep.shape[1]
+    per = hidden // width
+
+    def put(value, kept, axis, given):
+        bit = (mine // (1 << firsts[axis])) % 2
+
+        @pl.when(bit == 0)
+        def _():
+            keep[kept] = value[:half].astype(BF16)
+            gives[axis][given] = value[half:].astype(BF16)
+
+        @pl.when(bit == 1)
+        def _():
+            keep[kept] = value[half:].astype(BF16)
+            gives[axis][given] = value[:half].astype(BF16)
+
+    def grads_of(axis, start, count):
+        def grad_outer(i, _):
+            at_act = at((start + i) * 2 * half, 2 * half)
+            put(t_dot(act[:, at_act], df[...]), early + start + i, axis, count + i)
+            return 0
+
+        def grad_inner(i, _):
+            at_hn, at_du = at((start + i) // per * 2 * half, 2 * half), at((start + i) % per * width, width)
+            put(t_dot(hn[:, at_hn], du[:, at_du]), start + i, axis, i)
+            return 0
+
+        lax.fori_loop(0, count, grad_inner, 0)
+        lax.fori_loop(0, count, grad_outer, 0)
+
+    early = keep.shape[0] // 2
+    begin = 0
+    for axis in range(3):
+        grads_of(axis, begin, gives[axis].shape[0] // 2)
+        begin += gives[axis].shape[0] // 2
 
     for s in range(seqs):
         block = da.at[rows_of(s, me)]
@@ -362,16 +390,17 @@
     g_bi[...] = jnp.sum(bsum[...], axis=0, keepdims=True)
 
 
-def middle(c, x, wo, wi, wf, vec, b_inner, gout):
+def middle(c, x, wo, wi, wf, vec, b_inner, gout, firsts, counts, rows):
     seqs, part, width = x.shape
     total, cols = c.shape
     hidden = wi.shape[1]
     sds = jax.ShapeDtypeStruct
+    halves = [sds((2 * count, rows // 2, width), BF16) for count in (sum(counts), *counts)]
     return pl.pallas_call(
-        functools.partial(middle_kernel, seqs, part),
+        functools.partial(middle_kernel, seqs, part, firsts),
         out_shape=(sds(x.shape, BF16), sds(x.shape, F32), sds(c.shape, BF16), sds(wo.shape, BF16),
-                   sds(wi.shape, BF16), sds(wf.shape, BF16), sds((6, width), F32), sds((1, hidden), F32)),
-        in_specs=vmem(8), out_specs=tuple(vmem(8)),
+                   *halves, sds((6, width), F32), sds((1, hidden), F32)),
+        in_specs=vmem(8), out_specs=tuple(vmem(10)),
         scratch_shapes=[
             pltpu.VMEM(x.shape, F32), pltpu.VMEM((seqs, part, 128), F32), pltpu.VMEM(x.shape, F32),
             pltpu.VMEM((total, width), BF16), pltpu.VMEM((total, hidden), BF16), pltpu.VMEM((total, hidden), F32),
@@ -381,6 +410,8 @@
             pltpu.SemaphoreType.DMA((2, 6 * seqs)),
         ],
         compiler_params=pltpu.CompilerParams(collective_id=2, has_side_effects=True, vmem_limit_bytes=LIMIT),
+        cost_estimate=pl.CostEstimate(flops=14 * total * width * hidden, transcendentals=total * hidden,
+                                      bytes_accessed=30 << 20),
         name="middle",
     )(c, x, wo, wi, wf, vec, b_inner, gout)
 
@@ -419,6 +450,7 @@
         in_specs=vmem(8), out_specs=tuple(vmem(5)),
         scratch_shapes=[pltpu.VMEM(dz1.shape, BF16), pltpu.VMEM(dz1.shape, BF16), pltpu.SemaphoreType.DMA((2, seqs))],
         compiler_params=pltpu.CompilerParams(collective_id=3, has_side_effects=True, vmem_limit_bytes=LIMIT),
+        cost_estimate=pl.CostEstimate(flops=12 * rows.size * wq.shape[1], transcendentals=0, bytes_accessed=16 << 20),
         name="project_back",
     )(rows, dq, dk, dv, wq, wk, wv, dz1)
 def grid_bits(n):
@@ -435,25 +467,37 @@
     return stages + [("gather", b) for b in reversed(order)]
 
 
-def event_order(n, colors):
-    (bx, by, bz), _ = grid_bits(n)
-    plans = [chunk_plan(n, c) for c in colors]
-    free, ready = [0.0] * 3, [0.0] * len(colors)
-    step, length = [0] * len(colors), [1.0] * len(colors)
-    events = []
+def event_order(n, plans, halved):
+    first, _ = grid_bits(n)
+    lag = 0.1
+
+    def path(b):
+        axis = (b >= first[1]) + (b >= first[2])
+        return ((axis, 1),) if b == first[axis] else ((axis, 1), (axis + 3, 2))
+
+    work = []
+    for plan, half in zip(plans, halved):
+        length, row = 0.5 if half else 1.0, []
+        for kind, b in plan:
+            length *= 0.5 if kind == "scatter" else 1.0
+            row.append((path(b), length))
+            length *= 2.0 if kind == "gather" else 1.0
+        work.append(row)
+    left = [sum(w * p[-1][1] + lag for p, w in row) for row in work]
+    free, ready, step, events = [0.0] * 6, [0.0] * len(plans), [0] * len(plans), []
     for _ in range(sum(len(p) for p in plans)):
         best = None
-        for c, plan in enumerate(plans):
-            if step[c] < len(plan):
-                axis = (plan[step[c]][1] >= by) + (plan[step[c]][1] >= bz)
-                key = (max(ready[c], free[axis]), -step[c], c, axis)
+        for c, row in enumerate(work):
+            if step[c] < len(row):
+                start = max([ready[c]] + [free[link] for link, _ in row[step[c]][0]])
+                key = (start, left[c] + step[c], c)
                 best = key if best is None or key < best else best
-        start, _, c, axis = best
-        kind, b = plans[c][step[c]]
-        length[c] *= 0.5 if kind == "scatter" else 1.0
-        free[axis] = start + length[c] * (2 if b != (bx, by, bz)[axis] else 1)
-        length[c] *= 2.0 if kind == "gather" else 1.0
-        ready[c] = free[axis] + 0.08
+        start, _, c = best
+        links, span = work[c][step[c]]
+        for link, times in links:
+            free[link] = start + times * span
+        ready[c] = start + links[-1][1] * span + lag
+        left[c] -= links[-1][1] * span + lag
         events.append((start, c, step[c]))
         step[c] += 1
     return [(c, s) for _, c, s in sorted(events)]
@@ -474,32 +518,29 @@
     return chunks
 
 
-def reduce_kernel(n, colors, rows, pieces, count, *refs):
+def reduce_kernel(n, colors, rows, loads, saves, count, results, *refs):
     grads, tiny = refs[:count], refs[count]
-    sums, tiny_out = refs[count + 1:2 * count + 1], refs[2 * count + 1]
-    work, got, full, hold, tiny_got, load_sem, save_sem, send_sem, recv_sem, tiny_sem = refs[2 * count + 2:]
+    sums, tiny_out = refs[count + 1:count + results + 1], refs[count + results + 1]
+    work, got, full, hold, tiny_got, load_sem, save_sem, send_sem, recv_sem, tiny_sem = refs[count + results + 2:]
     nc = len(colors)
     me, head = lax.axis_index("batch"), lax.axis_index("head")
     _, bits = grid_bits(n)
 
     def moves(c, out):
-        for k, (i, r, col, span, at) in enumerate(pieces[c]):
-            outside = (sums if out else grads)[i].at[pl.ds(r, rows), pl.ds(col, span)]
-            inside = (full if out else work).at[c, :, pl.ds(at, span)]
-            if out:
-                yield pltpu.make_async_copy(inside, outside, save_sem.at[c, k])
-            else:
-                yield pltpu.make_async_copy(outside, inside, load_sem.at[c, k])
-
-    for c in range(nc):
-        for move in moves(c, False):
-            move.start()
-    hold[...] = tiny[...]
-    barrier = pltpu.get_barrier_semaphore()
-    for b in range(bits):
-        pl.semaphore_signal(barrier, inc=1, device_id={"batch": flip(me, b)}, device_id_type=MESH)
-    pl.semaphore_signal(barrier, inc=1, device_id={"head": 1 - head}, device_id_type=MESH)
-    pl.semaphore_wait(barrier, bits + 1)
+        if out:
+            for k, (i, r, col, span, at) in enumerate(saves[c]):
+                outside = sums[i].at[pl.ds(r, rows), pl.ds(col, span)]
+                yield pltpu.make_async_copy(full.at[c, :, pl.ds(at, span)], outside, save_sem.at[c, k])
+        elif loads[c] is None:
+            for k, (i, r, col, span, at) in enumerate(saves[c]):
+                outside = grads[i + count - results].at[pl.ds(r, rows), pl.ds(col, span)]
+                yield pltpu.make_async_copy(outside, work.at[c, :, pl.ds(at, span)], load_sem.at[c, k])
+        else:
+            kept, kept_at, given, given_at = loads[c]
+            keep, _, length, at = spans[c][0]
+            inside = work.at[c, pl.ds(pl.multiple_of(keep, 16), length)]
+            yield pltpu.make_async_copy(grads[kept].at[kept_at], inside, load_sem.at[c, 0])
+            yield pltpu.make_async_copy(grads[given].at[given_at], got.at[c, pl.ds(at, length)], load_sem.at[c, 1])
 
     plans = [chunk_plan(n, c) for c in colors]
     bit_of = [(me // (1 << b)) % 2 for b in range(bits)]
@@ -519,6 +560,16 @@
                 off, length = off - bit_of[b] * length, 2 * length
         spans.append(row)
 
+    for c in range(nc):
+        for move in moves(c, False):
+            move.start()
+    hold[...] = tiny[...]
+    barrier = pltpu.get_barrier_semaphore()
+    for b in range(bits):
+        pl.semaphore_signal(barrier, inc=1, device_id={"batch": flip(me, b)}, device_id_type=MESH)
+    pl.semaphore_signal(barrier, inc=1, device_id={"head": 1 - head}, device_id_type=MESH)
+    pl.semaphore_wait(barrier, bits + 1)
+
     def copy_of(c, s):
         kind, b = plans[c][s]
         _, start, length, at = spans[c][s]
@@ -533,7 +584,11 @@
 
     def finish(c, s):
         keep, _, length, at = spans[c][s]
-        copy_of(c, s).wait()
+        if s == 0 and loads[c] is not None:
+            for move in moves(c, False):
+                move.wait()
+        else:
+            copy_of(c, s).wait()
         if plans[c][s][0] != "gather":
             target = full if plans[c][s + 1][0] == "gather" else work
 
@@ -559,7 +614,8 @@
         else:
             hold[...] += tiny_got[k]
 
-    events = event_order(n, colors)
+    done = [load is not None for load in loads]
+    events = [(c, s + done[c]) for c, s in event_order(n, [p[d:] for p, d in zip(plans, done)], done)]
     gap = len(events) // (bits + 2)
     for e, (c, s) in enumerate(events):
         if s == 0:
@@ -584,22 +640,42 @@
             move.wait()
 
 
-def reduce_gradients(grads, tiny, n, rows=256):
+EARLY_MIX = (0, 0, 0, 1, 1, 1, 2, 3)
+LATE_MIX = (0, 1, 2, 0, 1, 3, 0, 1)
+ROWS = 256
+
+
+def reduce_gradients(early, late, shapes, tiny, n):
     width = tiny.shape[1]
-    pieces = chunk_pieces([g.shape for g in grads], rows, width)
-    nc = len(pieces)
-    colors = [c % 2 for c in range(nc)]
+    saves = chunk_pieces(shapes, ROWS, width)
+    count = early[0].shape[0] // 2
+    slots, colors, loads = [0, 0, 0], [], []
+    for which in range(2):
+        for c in range(count):
+            color = EARLY_MIX[c * len(EARLY_MIX) // count]
+            axis = min(color, 2)
+            loads.append((0, which * count + c, 1 + axis, slots[axis]))
+            slots[axis] += 1
+            colors.append(color)
+    for c in range(len(saves) - 2 * count):
+        colors.append(LATE_MIX[c % len(LATE_MIX)])
+        loads.append(None)
+    rank = [(c % count, c // count) if c < 2 * count else (c - 2 * count, 2) for c in range(len(saves))]
+    order = sorted(range(len(saves)), key=lambda c: rank[c])
+    saves, colors, loads = ([array[c] for c in order] for array in (saves, colors, loads))
+    nc = len(saves)
     stages = len(chunk_plan(n, 0))
     _, bits = grid_bits(n)
-    got_rows = rows - rows // 8 + (bits - 3) * rows // 8
-    hbm = [pl.BlockSpec(memory_space=pl.ANY)] * len(grads)
+    got_rows = ROWS - ROWS // 8 + (bits - 3) * ROWS // 8
+    grads = (*early, *late)
+    hbm = lambda k: [pl.BlockSpec(memory_space=pl.ANY)] * k
     done = pl.pallas_call(
-        functools.partial(reduce_kernel, n, colors, rows, pieces, len(grads)),
-        out_shape=tuple(jax.ShapeDtypeStruct(g.shape, g.dtype) for g in (*grads, tiny)),
-        in_specs=hbm + vmem(1), out_specs=tuple(hbm + vmem(1)),
+        functools.partial(reduce_kernel, n, colors, ROWS, loads, saves, len(grads), len(shapes)),
+        out_shape=(*(jax.ShapeDtypeStruct(shape, BF16) for shape in shapes), jax.ShapeDtypeStruct(tiny.shape, F32)),
+        in_specs=hbm(len(grads)) + vmem(1), out_specs=tuple(hbm(len(shapes)) + vmem(1)),
         scratch_shapes=[
-            pltpu.VMEM((nc, rows, width), BF16), pltpu.VMEM((nc, got_rows, width), BF16),
-            pltpu.VMEM((nc, rows, width), BF16), pltpu.VMEM(tiny.shape, F32),
+            pltpu.VMEM((nc, ROWS, width), BF16), pltpu.VMEM((nc, got_rows, width), BF16),
+            pltpu.VMEM((nc, ROWS, width), BF16), pltpu.VMEM(tiny.shape, F32),
             pltpu.VMEM((bits + 1,) + tiny.shape, F32),
             pltpu.SemaphoreType.DMA((nc, 2)), pltpu.SemaphoreType.DMA((nc, 2)),
             pltpu.SemaphoreType.DMA((nc, stages)), pltpu.SemaphoreType.DMA((nc, stages)),
@@ -616,14 +692,21 @@
     vec = jnp.stack([b_output, gain_attn, shift_attn, b_outer, gain_ffn, shift_ffn]).astype(F32)
     rows, q, k, v = project_rows(inputs, w_query, w_key, w_value, bias)
     new_scores, context, norm = attend(lengths, q, k, v, prior_scores)
-    outputs, dz1, dc, g_wo, g_wi, g_wf, small, g_bi = middle(
-        context, inputs, w_output, w_inner, w_outer, vec, b_inner.astype(F32)[None], grad_out)
+    firsts, _ = grid_bits(n_batch)
+    chunks = w_inner.size // (ROWS * width)
+    counts = [chunks * sum(min(color, 2) == axis for color in EARLY_MIX) // len(EARLY_MIX) for axis in range(3)]
+    outputs, dz1, dc, g_wo, keep, *gives, small, g_bi = middle(
+        context, inputs, w_output, w_inner, w_outer, vec, b_inner.astype(F32)[None], grad_out, firsts, counts, ROWS)
+    taken = [lax.ppermute(give, "batch", [(i, flip(i, first)) for i in range(n_batch)])
+             for give, first in zip(gives, firsts)]
     grad_prior, dq, dk, dv = attend_back(lengths, q, k, v, dc, prior_scores, norm, grad_scores)
     grad_inputs, g_wq, g_wk, g_wv, g_b = project_back(rows, dq, dk, dv, w_query, w_key, w_value, dz1)
     pad = lambda a, to: jnp.pad(a, ((0, to - a.shape[0]), (0, 0)))
     mine = jnp.concatenate([g_bi.reshape(-1, width), g_b.reshape(-1, width)])
     tiny = jnp.concatenate([pad(small, 8), pad(mine, 8)])
-    grads, tiny = reduce_gradients((g_wi, g_wf, g_wo, g_wq, g_wk, g_wv), tiny, n_batch)
+    late = (g_wo, g_wq, g_wk, g_wv)
+    shapes = [w_inner.shape, w_outer.shape] + [g.shape for g in late]
+    grads, tiny = reduce_gradients((keep, *taken), late, shapes, tiny, n_batch)
     g_wi, g_wf, g_wo, g_wq, g_wk, g_wv = [g.astype(F32) for g in grads]
     g_bi = tiny[8:8 + g_bi.size // width].reshape(-1)
     g_b = tiny[8 + g_bi.size // width:8 + mine.shape[0]].reshape(g_b.shape)

time: 390 us -> 339 us (0.87)
  Pallas kernels: 348 us -> 284 us
  local copies, waits for them, and re-layouts: 19.4 us -> 25.9 us
  starting transfers between devices: 0 us -> 5.94 us
    pallas_call x2, Pallas kernels: 284 us -> 221 us  [the longest x1 159 us: reduce_gradients(): pl.pallas_call(functools.partial(reduce_kernel, n, colors, ROWS, loads, s...]
    ppermute x0 -> x3, starting transfers between devices: none -> 5.94 us  [on_device(): lax.ppermute(give, 'batch', [(i, flip(i, first)) for i in range(n_batch)])]
    another operation x7, local copies, waits for them, and re-layouts: 0.08 us -> 4.16 us  [on_device(): jnp.stack([b_output, gain_attn, shift_attn, b_outer, gain_ffn, shift_ffn])]
    unnamed x67 -> x51, local copies, waits for them, and re-layouts: 16.2 us -> 16.9 us
  transfers between devices with their start and end apart: 0 -> 3, of which waited for: 0 -> 0; matrix products, arithmetic and copies ran while one was open for 0% -> 1% of each run, Pallas kernels for 0% -> 11%
where the time goes in v3:
time: 339 us
  Pallas kernels  284 us (84%)
  local copies, waits for them, and re-layouts  25.9 us (8%)
  other arithmetic  21.5 us (6%)
  starting transfers between devices  5.94 us (2%)
    pallas_call x1, Pallas kernels, reduce_gradients(): pl.pallas_call(functools.partial(reduce_kernel, n, colors, ROWS, loads, s...  159 us
    pallas_call x1, Pallas kernels, middle(): pl.pallas_call(functools.partial(middle_kernel, seqs, part, firsts), out_...  61.7 us
    pallas_call x1, Pallas kernels, attend_back(): pl.pallas_call(functools.partial(attend_back_kernel, 256, pair // 2), gri...  23.3 us
    pallas_call x1, Pallas kernels, attend(): pl.pallas_call(functools.partial(attend_kernel, 256, pair // 2), grid_spe...  18.4 us
    convert_element_type x6, other arithmetic, on_device(): g_wi, g_wf, g_wo, g_wq, g_wk, g_wv = [g.astype(F32) for g in grads]  17.7 us
    unnamed x51, local copies, waits for them, and re-layouts  16.9 us
    pallas_call x1, Pallas kernels, project_back(): pl.pallas_call(functools.partial(project_back_kernel, seqs, part), out_sh...  13.6 us
    pallas_call x1, Pallas kernels, project_rows(): pl.pallas_call(functools.partial(project_kernel, seqs, part), out_shape=(...  8.52 us
  transfers between devices with their start and end apart: 3, of which 0 were waited for; matrix products, arithmetic and copies ran while one was open for 1% of the time, Pallas kernels for 11%

profile of v3, /device:TPU:0, one launch (start us, length us, event | category | flops | bytes accessed | tf_op | source)
XLA Modules:
  0.0 338.6 jit_solution(11741585849243900791)
XLA Ops:
  6.8 1.3 broadcast_in_dim.7
  8.7 8.5 %project_rows.1 = (bf16[1024,1024]{1,0:T(8,128)(2,1)}, bf16[1024,512]{1,0:T(8,128)(2,1)}, bf16[1024,512]{1,0:T(8,128)(2,1)}, bf16[1024,512]{1,0:T(8,128)(2,1)}) custom-call(bf16[2,256,1024]{2,1,0:T(8,128)(2,1)} %x.7, bf16[1024,512]{1,0:T(8,128)(2,1)} %wq.3, bf16[1024,512]{1,0:T(8,128)(2,1)} %wk.3, bf16[1024,512]{1,0:T(8,128)(2,1)} %wv.3, ...), custom_call_target="tpu_custom_call" | custom-call | tf_op jit(solution)/shard_map/project_rows/pallas_call | solution.py:76
  17.3 1.2 copy-done
  18.5 1.2 copy-done.2
  19.7 1.2 copy-done.4
  20.9 18.4 %attend.1 = (bf16[2,8,512,512]{3,2,1,0:T(8,128)(2,1)}, bf16[1024,512]{1,0:T(8,128)(2,1)S(1)}, f32[2,4,512,128]{3,2,1,0:T(8,128)S(1)}) custom-call(s32[2]{0:T(128)S(1)} %copy-done.6, bf16[1024,512]{1,0:T(8,128)(2,1)S(1)} %copy-done, bf16[1024,512]{1,0:T(8,128)(2,1)S(1)} %copy-done.2, bf16[1024,512]{1,0:T(8,128)(2,1)S(1)} %copy-done.4, ...), custom_call_target="tpu_custom_call" | custom-call | tf_op jit(solution)/shard_map/attend/pallas_call | solution.py:116
  39.3 1.3 copy-done.7
  40.6 1.0 copy-done.9
  41.6 61.7 %middle.1 = (bf16[2,256,1024]{2,1,0:T(8,128)(2,1)}, f32[2,256,1024]{2,1,0:T(8,128)}, bf16[1024,512]{1,0:T(8,128)(2,1)}, bf16[512,1024]{1,0:T(8,128)(2,1)}, bf16[...) custom-call(bf16[1024,512]{1,0:T(8,128)(2,1)} %copy-done.9, ...), custom_call_target="tpu_custom_call" | custom-call | flops 30064771072 | bytes 31457280 | tf_op jit(solution)/shard_map/middle/pallas_call | solution.py:399
  103.2 2.9 collective-permute-start
  106.1 1.5 collective-permute-start.1
  107.6 1.6 collective-permute-start.2
  109.2 1.2 copy-done.5
  110.4 1.6 copy-done.8
  112.0 1.2 copy-done.13
  113.2 23.3 %attend_back.1 = (bf16[2,8,512,512]{3,2,1,0:T(8,128)(2,1)}, bf16[1024,512]{1,0:T(8,128)(2,1)S(1)}, bf16[1024,512]{1,0:T(8,128)(2,1)S(1)}, bf16[1024,512]{1,0:T(8,128)(2,1)S(1)}) custom-call(s32[2]{0:T(128)S(1)} %copy-done.6, bf16[1024,512]{1,0:T(8,128)(2,1)S(1)} %copy-done.1, bf16[1024,512]{1,0:T(8,128)(2,1)S(1)} %copy-done.3, ...), custom_call_target="tpu_custom_call" | custom-call | flops 10737418240 | bytes 25165824 | tf_op jit(solution)/shard_map/attend_back/pallas_call | solution.py:164
  136.5 1.0 copy-done.10
  137.5 1.0 copy-done.11
  138.5 1.0 copy-done.12
  139.4 13.6 %project_back.1 = (bf16[2,256,1024]{2,1,0:T(8,128)(2,1)}, bf16[1024,512]{1,0:T(8,128)(2,1)}, bf16[1024,512]{1,0:T(8,128)(2,1)}, bf16[1024,512]{1,0:T(8,128)(2,1)}, f32[2,512]{1,0:T(2,128)}) custom-call(bf16[1024,1024]{1,0:T(8,128)(2,1)} %get-tuple-element.58.rows, bf16[1024,512]{1,0:T(8,128)(2,1)} %copy-done.10, bf16[1024,512]{1,0:T(8,128)(2,1)} %copy-done.11, ...), custom_call_target="tpu_custom_call" | custom-call | flops 6442450944 | bytes 16777216 | tf_op jit(solution)/shard_map/project_back/pallas_call | solution.py:447
  155.6 159.1 %reduce_gradients.1 = (bf16[1024,2048]{1,0:T(8,128)(2,1)}, bf16[2048,1024]{1,0:T(8,128)(2,1)}, bf16[512,1024]{1,0:T(8,128)(2,1)}, bf16[1024,512]{1,0:T(8,128)(2,...) custom-call(bf16[16,128,1024]{2,1,0:T(8,128)(2,1)} %get-tuple-element.67.refs_0_, ...), custom_call_target="tpu_custom_call" | custom-call | tf_op jit(solution)/shard_map/reduce_gradients/pallas_call | solution.py:672
  314.7 1.6 fusion
  316.3 0.8 slice_bitcast_fusion
  317.0 1.3 fusion.1
  318.4 6.8 %convert_element_type.35 = f32[1024,2048]{1,0:T(8,128)} convert(bf16[1024,2048]{1,0:T(8,128)(2,1)} %get-tuple-element.83) | non-fusion elementwise | flops 2097152 | bytes 12582912 | tf_op jit(solution)/shard_map/convert_element_type | solution.py:710
  325.2 4.5 %convert_element_type.36 = f32[2048,1024]{1,0:T(8,128)} convert(bf16[2048,1024]{1,0:T(8,128)(2,1)S(1)} %copy-done.14) | non-fusion elementwise | flops 2097152 | bytes 12582912 | tf_op jit(solution)/shard_map/convert_element_type | solution.py:710
  329.6 1.6 convert_element_type.31
  331.3 1.6 convert_element_type.32
  332.9 1.6 convert_element_type.33
  334.5 1.6 convert_element_type.34
  336.7 1.0 copy.45
  337.6 1.0 copy.46
  (56 shorter events, 9.9 us)
Async XLA Ops:
  0.7 16.6 %copy-start.6 = (s32[2]{0:T(128)S(1)}, s32[2]{0:T(128)}, u32[]{:S(2)}) copy-start(s32[2]{0:T(128)} %lengths.3) | copy-start | bytes 28
  17.2 1.2 copy-start
  18.5 1.2 copy-start.2
  19.7 1.2 copy-start.4
  39.3 1.3 copy-start.7
  40.6 1.0 copy-start.9
  41.6 67.6 %copy-start.1 = (bf16[1024,512]{1,0:T(8,128)(2,1)S(1)}, bf16[1024,512]{1,0:T(8,128)(2,1)}, u32[]{:S(2)}) copy-start(bf16[1024,512]{1,0:T(8,128)(2,1)} %get-tuple-element.52.q) | copy-start | bytes 3145732
  41.6 67.6 %copy-start.3 = (bf16[1024,512]{1,0:T(8,128)(2,1)S(1)}, bf16[1024,512]{1,0:T(8,128)(2,1)}, u32[]{:S(2)}) copy-start(bf16[1024,512]{1,0:T(8,128)(2,1)} %get-tuple-element.53.k) | copy-start | bytes 3145732
  103.2 52.3 %collective-permute-start = (bf16[6,128,1024]{2,1,0:T(8,128)(2,1)}, bf16[6,128,1024]{2,1,0:T(8,128)(2,1)}, u32[]{:S(2)}, u32[]{:S(2)}) collective-permute-start(bf16[6,128,1024]{2,1,0:T(8,128)(2,1)} %get-tuple-element.68), channel_id=1, source_target_pairs={{0,1},{1,0},{2,3},{3,2},{4,5},{5,4},{6,7},{7,6},{8,9},{9,8},{10,11... | collective-permute-start | bytes 4718600 | tf_op jit(solution)/shard_map/ppermute | solution.py:700
  106.1 49.5 %collective-permute-start.1 = (bf16[6,128,1024]{2,1,0:T(8,128)(2,1)}, bf16[6,128,1024]{2,1,0:T(8,128)(2,1)}, u32[]{:S(2)}, u32[]{:S(2)}) collective-permute-start(bf16[6,128,1024]{2,1,0:T(8,128)(2,1)} %get-tuple-element.69), channel_id=1, source_target_pairs={{0,2},{1,3},{2,0},{3,1},{4,6},{5,7},{6,4},{7,5},{8,10},{9,11},{10,... | collective-permute-start | bytes 4718600 | tf_op jit(solution)/shard_map/ppermute | solution.py:700
  107.6 48.0 %collective-permute-start.2 = (bf16[4,128,1024]{2,1,0:T(8,128)(2,1)}, bf16[4,128,1024]{2,1,0:T(8,128)(2,1)}, u32[]{:S(2)}, u32[]{:S(2)}) collective-permute-start(bf16[4,128,1024]{2,1,0:T(8,128)(2,1)} %get-tuple-element.70), channel_id=1, source_target_pairs={{0,4},{1,5},{2,6},{3,7},{4,0},{5,1},{6,2},{7,3},{8,12},{9,13},{10,... | collective-permute-start | bytes 3145736 | tf_op jit(solution)/shard_map/ppermute | solution.py:700
  109.2 1.2 copy-start.5
  110.4 1.6 copy-start.8
  112.0 1.2 copy-start.13
  136.5 1.0 copy-start.10
  137.5 1.0 copy-start.11
  138.5 1.0 copy-start.12
  139.4 14.8 %copy-start.22 = (f32[1,2048]{1,0:T(1,128)S(1)}, f32[1,2048]{1,0:T(1,128)}, u32[]{:S(2)}) copy-start(f32[1,2048]{1,0:T(1,128)} %get-tuple-element.76) | copy-start | bytes 24580
  139.4 15.5 %copy-start.21 = (f32[6,1024]{1,0:T(8,128)S(1)}, f32[6,1024]{1,0:T(8,128)}, u32[]{:S(2)}) copy-start(f32[6,1024]{1,0:T(8,128)} %get-tuple-element.75) | copy-start | bytes 73732
  318.4 6.8 %copy-start.14 = (bf16[2048,1024]{1,0:T(8,128)(2,1)S(1)}, bf16[2048,1024]{1,0:T(8,128)(2,1)}, u32[]{:S(2)}) copy-start(bf16[2048,1024]{1,0:T(8,128)(2,1)} %get-tuple-element.84) | copy-start | bytes 12582916
  325.2 4.5 %copy-start.18 = (bf16[1024,512]{1,0:T(8,128)(2,1)S(1)}, bf16[1024,512]{1,0:T(8,128)(2,1)}, u32[]{:S(2)}) copy-start(bf16[1024,512]{1,0:T(8,128)(2,1)} %get-tuple-element.78) | copy-start | bytes 3145732
  325.2 6.1 %copy-start.17 = (bf16[1024,512]{1,0:T(8,128)(2,1)S(1)}, bf16[1024,512]{1,0:T(8,128)(2,1)}, u32[]{:S(2)}) copy-start(bf16[1024,512]{1,0:T(8,128)(2,1)} %get-tuple-element.79) | copy-start | bytes 3145732
  329.6 3.2 copy-start.16
  329.6 4.8 %copy-start.15 = (bf16[512,1024]{1,0:T(8,128)(2,1)S(1)}, bf16[512,1024]{1,0:T(8,128)(2,1)}, u32[]{:S(2)}) copy-start(bf16[512,1024]{1,0:T(8,128)(2,1)} %get-tuple-element.82) | copy-start | bytes 3145732
  331.3 5.4 %copy-start.19 = (bf16[2,256,1024]{2,1,0:T(8,128)(2,1)S(1)}, bf16[2,256,1024]{2,1,0:T(8,128)(2,1)}, u32[]{:S(2)}) copy-start(bf16[2,256,1024]{2,1,0:T(8,128)(2,1)} %get-tuple-element.112) | copy-start | bytes 3145732
  332.9 4.8 %copy-start.20 = (bf16[2,256,1024]{2,1,0:T(8,128)(2,1)S(1)}, bf16[2,256,1024]{2,1,0:T(8,128)(2,1)}, u32[]{:S(2)}) copy-start(bf16[2,256,1024]{2,1,0:T(8,128)(2,1)} %get-tuple-element.114) | copy-start | bytes 3145732

commit v4 on v3

--- a/solution.py
+++ b/solution.py
@@ -40,19 +40,25 @@
     return [pl.BlockSpec(memory_space=pltpu.VMEM)] * count
 
 
-def project_kernel(seqs, part, x, wq, wk, wv, bias, rows, q, k, v, got, sems):
+def as_row(vector):
+    return vector[...].astype(F32).reshape(1, vector.shape[0])
+
+
+def project_kernel(seqs, part, x, wq, wk, wv, b_query, b_value, rows, q, k, v, got, sems):
     me = lax.axis_index("head")
     other = 1 - me
     meet(other)
     for s in range(seqs):
         to_partner(x.at[s], got.at[s], sems, s, other).start()
 
+    bias_q, bias_v = as_row(b_query), as_row(b_value)
+
     def emit(block, s, p):
         at = pl.ds(pl.multiple_of((2 * s + p) * part, part), part)
         rows[at, :] = block
-        q[at, :] = (dot(block, wq[...]) + bias[0:1, :]).astype(BF16)
+        q[at, :] = (dot(block, wq[...]) + bias_q).astype(BF16)
         k[at, :] = dot(block, wk[...]).astype(BF16)
-        v[at, :] = (dot(block, wv[...]) + bias[1:2, :]).astype(BF16)
+        v[at, :] = (dot(block, wv[...]) + bias_v).astype(BF16)
 
     def own(s, _):
         emit(x[s], s, me)
@@ -69,18 +75,18 @@
     lax.fori_loop(0, seqs, theirs, 0)
 
 
-def project_rows(x, wq, wk, wv, bias):
+def project_rows(x, wq, wk, wv, b_query, b_value):
     seqs, part, width = x.shape
     total, cols = 2 * seqs * part, wq.shape[1]
     out = jax.ShapeDtypeStruct((total, cols), BF16)
     return pl.pallas_call(
         functools.partial(project_kernel, seqs, part),
         out_shape=(jax.ShapeDtypeStruct((total, width), BF16), out, out, out),
-        in_specs=vmem(5), out_specs=tuple(vmem(4)),
+        in_specs=vmem(6), out_specs=tuple(vmem(4)),
         scratch_shapes=[pltpu.VMEM(x.shape, BF16), pltpu.SemaphoreType.DMA((2, seqs))],
         compiler_params=pltpu.CompilerParams(collective_id=1, has_side_effects=True, vmem_limit_bytes=LIMIT),
         name="project_rows",
-    )(x, wq, wk, wv, bias)
+    )(x, wq, wk, wv, b_query, b_value)
 
 
 def attend_kernel(block, head, lengths, q, k, v, prior, score, c, norm):
@@ -120,7 +126,7 @@
             in_specs=[rows, rows, rows, big], out_specs=(big, rows, norm)),
         out_shape=(jax.ShapeDtypeStruct(prior.shape, BF16), jax.ShapeDtypeStruct(q.shape, BF16),
                    jax.ShapeDtypeStruct((seqs, heads // 2, full, pair), F32)),
-        compiler_params=pltpu.CompilerParams(vmem_limit_bytes=40 << 20),
+        compiler_params=pltpu.CompilerParams(vmem_limit_bytes=LIMIT),
         name="attend",
     )(lengths, q, k, v, prior)
 
@@ -167,7 +173,7 @@
             num_scalar_prefetch=1, grid=(seqs, heads // 2),
             in_specs=[rows, rows, rows, rows, big, norms, big], out_specs=(big, rows, rows, rows)),
         out_shape=(jax.ShapeDtypeStruct(prior.shape, BF16), flat, flat, flat),
-        compiler_params=pltpu.CompilerParams(vmem_limit_bytes=40 << 20),
+        compiler_params=pltpu.CompilerParams(vmem_limit_bytes=LIMIT),
         cost_estimate=pl.CostEstimate(flops=40 * full * full * seqs * heads * pair // 2, transcendentals=prior.size,
                                       bytes_accessed=6 * prior.size),
         name="attend_back",
@@ -190,9 +196,9 @@
     return r * (e - jnp.mean(e, axis=-1, keepdims=True) - unit * jnp.mean(e * unit, axis=-1, keepdims=True))
 
 
-def middle_kernel(seqs, part, firsts, c, x, wo, wi, wf, vec, b_inner, gout,
-                  out, dz1, dc, g_wo, keep, give_x, give_y, give_z, small, g_bi,
-                  unit1, r1, dz2, hn, act, slope, df, du, da, give, got, own, sums, bsum, sems):
+def middle_kernel(seqs, part, firsts, c, x, wo, wi, wf, b_output, gain1, shift1, b_outer, gain2, shift2, b_inner, gout,
+                  out, dz1, dc, g_wo, keep, give_x, give_y, small, g_bi,
+                  unit1, r1, dz2, hn, act, slope, df, du, da, give, got, own, sums, bsum, bi, sems):
     me = lax.axis_index("head")
     other = 1 - me
     width = x.shape[2]
@@ -200,9 +206,10 @@
     tile = 512
     sub = 64
     meet(other)
-    b_output, gain1, shift1, b_outer, gain2, shift2 = [vec[i:i + 1, :] for i in range(6)]
+    b_output, gain1, shift1, b_outer, gain2, shift2 = map(as_row, (b_output, gain1, shift1, b_outer, gain2, shift2))
     sums[...] = jnp.zeros_like(sums)
     bsum[...] = jnp.zeros_like(bsum)
+    bi[...] = as_row(b_inner)
 
     def rows_of(s, p):
         return pl.ds(pl.multiple_of((2 * s + p) * part, part), part)
@@ -243,7 +250,7 @@
 
         def columns(j, _):
             cols = at(j * tile, tile)
-            u = dot(hn[rows, :], wi[:, cols]) + b_inner[:, cols]
+            u = dot(hn[rows, :], wi[:, cols]) + bi[:, cols]
             cdf = 0.5 * (1.0 + lax.erf(u * 0.7071067811865476))
             act[rows, cols] = (u * cdf).astype(BF16)
             slope[rows, cols] = cdf + u * (jnp.exp(-0.5 * u * u) * 0.3989422804014327)
@@ -344,7 +351,7 @@
         to_partner(block, block, sems, 5 * seqs + s, other).start()
 
     mine = lax.axis_index("batch")
-    gives = (give_x, give_y, give_z)
+    gives = (give_x, give_y)
     half = keep.shape[1]
     per = hidden // width
 
@@ -377,7 +384,7 @@
 
     early = keep.shape[0] // 2
     begin = 0
-    for axis in range(3):
+    for axis in range(2):
         grads_of(axis, begin, gives[axis].shape[0] // 2)
         begin += gives[axis].shape[0] // 2
 
@@ -390,7 +397,7 @@
     g_bi[...] = jnp.sum(bsum[...], axis=0, keepdims=True)
 
 
-def middle(c, x, wo, wi, wf, vec, b_inner, gout, firsts, counts, rows):
+def middle(c, x, wo, wi, wf, vectors, gout, firsts, counts, rows):
     seqs, part, width = x.shape
     total, cols = c.shape
     hidden = wi.shape[1]
@@ -400,20 +407,21 @@
         functools.partial(middle_kernel, seqs, part, firsts),
         out_shape=(sds(x.shape, BF16), sds(x.shape, F32), sds(c.shape, BF16), sds(wo.shape, BF16),
                    *halves, sds((6, width), F32), sds((1, hidden), F32)),
-        in_specs=vmem(8), out_specs=tuple(vmem(10)),
+        in_specs=vmem(6 + len(vectors)), out_specs=tuple(vmem(9)),
         scratch_shapes=[
             pltpu.VMEM(x.shape, F32), pltpu.VMEM((seqs, part, 128), F32), pltpu.VMEM(x.shape, F32),
             pltpu.VMEM((total, width), BF16), pltpu.VMEM((total, hidden), BF16), pltpu.VMEM((total, hidden), F32),
             pltpu.VMEM((total, width), BF16), pltpu.VMEM((total, hidden), BF16), pltpu.VMEM((total, width), BF16),
             pltpu.VMEM((3 * seqs, part, width), BF16), pltpu.VMEM((3, seqs, part, width), BF16),
             pltpu.VMEM(x.shape, BF16), pltpu.VMEM((6, 8, width), F32), pltpu.VMEM((8, hidden), F32),
+            pltpu.VMEM((1, hidden), F32),
             pltpu.SemaphoreType.DMA((2, 6 * seqs)),
         ],
         compiler_params=pltpu.CompilerParams(collective_id=2, has_side_effects=True, vmem_limit_bytes=LIMIT),
         cost_estimate=pl.CostEstimate(flops=14 * total * width * hidden, transcendentals=total * hidden,
                                       bytes_accessed=30 << 20),
         name="middle",
-    )(c, x, wo, wi, wf, vec, b_inner, gout)
+    )(c, x, wo, wi, wf, *vectors, gout)
 
 
 def project_back_kernel(seqs, part, rows, dq, dk, dv, wq, wk, wv, dz1,
@@ -453,53 +461,64 @@
         cost_estimate=pl.CostEstimate(flops=12 * rows.size * wq.shape[1], transcendentals=0, bytes_accessed=16 << 20),
         name="project_back",
     )(rows, dq, dk, dv, wq, wk, wv, dz1)
+LINE = 16
+ROWS = 256
+LATE_COLORS = (0, 1, 2, 3, 0, 1, 2, 3)
+PRECEDENCE = (29, 13, 18, 0, 6, 13, 11, 17, 6, 9, 1, 15, 15, 6, 22, 21, 13, 2, 9, 12, 8, 7, 35, 19)
+LANDS = ("gather", "out", "back_in", "back_mid", "back_out")
+
+
 def grid_bits(n):
     bits = n.bit_length() - 1
     side = bits // 3
     return (0, side, 2 * side), bits
 
 
-def chunk_plan(n, color):
+def chunk_plan(n, color, rows):
     (bx, by, bz), bits = grid_bits(n)
-    order = ((bx, by, bz), (by, bx, bz), (bz, bx, by), (bz, by, bx))[color]
-    rest = [b for b in range(bits) if b not in order]
-    stages = [("scatter", b) for b in order] + [("double", b) for b in rest]
-    return stages + [("gather", b) for b in reversed(order)]
-
-
-def event_order(n, plans, halved):
+    order = (by, bx) if color % 2 else (bx, by)
+    line = n == LINE
+    plan, length = [], rows
+    if line and color >= 2:
+        plan = [("far_in", bz, 3 * rows // 4), ("far_mid", bz, rows // 2), ("far_out", bz, rows // 4)]
+        length = rows // 4
+    if not line:
+        order = (*order, bz)
+    for b in order:
+        length //= 2
+        plan.append(("scatter", b, length))
+    if line and color < 2:
+        plan += [(kind, bz, length) for kind in ("in", "mid", "out")]
+    plan += [("double", b, length) for b in range(bits) if not line and b not in order]
+    for b in reversed(order):
+        plan.append(("gather", b, length))
+        length *= 2
+    if line and color >= 2:
+        plan += [("back_in", bz, rows // 4), ("back_mid", bz, rows // 2), ("back_out", bz, 3 * rows // 4)]
+    return plan
+
+
+def event_order(n, plans, rows):
     first, _ = grid_bits(n)
-    lag = 0.1
-
-    def path(b):
-        axis = (b >= first[1]) + (b >= first[2])
-        return ((axis, 1),) if b == first[axis] else ((axis, 1), (axis + 3, 2))
-
-    work = []
-    for plan, half in zip(plans, halved):
-        length, row = 0.5 if half else 1.0, []
-        for kind, b in plan:
-            length *= 0.5 if kind == "scatter" else 1.0
-            row.append((path(b), length))
-            length *= 2.0 if kind == "gather" else 1.0
-        work.append(row)
-    left = [sum(w * p[-1][1] + lag for p, w in row) for row in work]
-    free, ready, step, events = [0.0] * 6, [0.0] * len(plans), [0] * len(plans), []
-    for _ in range(sum(len(p) for p in plans)):
-        best = None
-        for c, row in enumerate(work):
-            if step[c] < len(row):
-                start = max([ready[c]] + [free[link] for link, _ in row[step[c]][0]])
-                key = (start, left[c] + step[c], c)
-                best = key if best is None or key < best else best
-        start, _, c = best
-        links, span = work[c][step[c]]
-        for link, times in links:
-            free[link] = start + times * span
-        ready[c] = start + links[-1][1] * span + lag
-        left[c] -= links[-1][1] * span + lag
+    lag = 0.16
+
+    def path(kind, b):
+        place = kind.split("_")[-1]
+        if place in ("in", "mid", "out"):
+            return ("in", "mid", "out").index(place) + 2
+        return (b >= first[1]) + (b >= first[2])
+
+    work = [[(path(kind, b), size / rows) for kind, b, size in plan] for plan in plans]
+    free, ready, step, events = [0.0] * 5, [0.0] * len(plans), [0] * len(plans), []
+    for _ in range(sum(map(len, work))):
+        start, _, c = min((max(ready[c], free[row[step[c]][0]]), -PRECEDENCE[c % len(PRECEDENCE)], c)
+                          for c, row in enumerate(work) if step[c] < len(row))
+        link, span = work[c][step[c]]
+        free[link] = start + span
+        ready[c] = free[link] + lag
         events.append((start, c, step[c]))
         step[c] += 1
+    events += [(r, c, len(work[c])) for c, r in enumerate(ready)]
     return [(c, s) for _, c, s in sorted(events)]
 
 
@@ -518,13 +537,57 @@
     return chunks
 
 
-def reduce_kernel(n, colors, rows, loads, saves, count, results, *refs):
-    grads, tiny = refs[:count], refs[count]
-    sums, tiny_out = refs[count + 1:count + results + 1], refs[count + results + 1]
-    work, got, full, hold, tiny_got, load_sem, save_sem, send_sem, recv_sem, tiny_sem = refs[count + results + 2:]
-    nc = len(colors)
+def only(cond, body):
+    if cond is None:
+        body()
+    else:
+        pl.when(cond)(body)
+
+
+def reduce_kernel(n, plans, rows, loads, saves, count, results, *refs):
+    grads, (small, g_bi, g_b) = refs[:count], refs[count:count + 3]
+    refs = refs[count + 3:]
+    sums, tiny_out = refs[:results], refs[results]
+    work, got, full, hold, tiny_got, load_sem, save_sem, send_sem, recv_sem, tiny_sem = refs[results + 1:]
+    nc = len(plans)
     me, head = lax.axis_index("batch"), lax.axis_index("head")
-    _, bits = grid_bits(n)
+    first, bits = grid_bits(n)
+    bit_of = [(me // (1 << b)) % 2 for b in range(bits)]
+    z = me // (1 << first[2])
+    side = z // 2
+    end = z % 3 == 0
+    middle = z % 3 != 0
+    mirror = me + (3 - 2 * z) * (1 << first[2])
+
+    spans = []
+    for plan in plans:
+        off, length, at, row = 0, rows, 0, []
+        quarter = rows // 4
+        for kind, b, size in plan:
+            where = None if kind in LANDS else at
+            at += 0 if kind in LANDS else size
+            if kind == "scatter":
+                row.append((off + bit_of[b] * size, off + (1 - bit_of[b]) * size, size, where))
+                off = row[-1][0]
+            elif kind == "gather":
+                row.append((off, off, size, where))
+                off = off - bit_of[b] * size
+            elif kind in ("far_in", "back_out"):
+                row.append(((1 - side) * quarter, (1 - side) * quarter, size, where))
+            elif kind == "far_mid":
+                row.append((side * 2 * quarter, (1 - side) * 2 * quarter, size, where))
+            elif kind == "back_mid":
+                row.append((side * 2 * quarter, side * 2 * quarter, size, where))
+            elif kind in ("far_out", "back_in"):
+                row.append((side * 3 * quarter, side * 3 * quarter, size, where))
+                off = z * quarter
+            else:
+                row.append((off, off, size, where))
+        spans.append(row)
+
+    def roles(kind):
+        place = kind.split("_")[-1]
+        return {"in": (end, middle), "mid": (middle, middle), "out": (middle, end)}.get(place, (None, None))
 
     def moves(c, out):
         if out:
@@ -542,55 +605,51 @@
             yield pltpu.make_async_copy(grads[kept].at[kept_at], inside, load_sem.at[c, 0])
             yield pltpu.make_async_copy(grads[given].at[given_at], got.at[c, pl.ds(at, length)], load_sem.at[c, 1])
 
-    plans = [chunk_plan(n, c) for c in colors]
-    bit_of = [(me // (1 << b)) % 2 for b in range(bits)]
-    spans = []
-    for c in range(nc):
-        off, length, at, row = 0, rows, 0, []
-        for kind, b in plans[c]:
-            if kind == "scatter":
-                length //= 2
-                row.append((off + bit_of[b] * length, off + (1 - bit_of[b]) * length, length, at))
-                off, at = row[-1][0], at + length
-            elif kind == "double":
-                row.append((off, off, length, at))
-                at += length
-            else:
-                row.append((off, off, length, 0))
-                off, length = off - bit_of[b] * length, 2 * length
-        spans.append(row)
-
     for c in range(nc):
         for move in moves(c, False):
             move.start()
-    hold[...] = tiny[...]
+    hold[...] = jnp.zeros_like(hold)
+    hold[0:6, :] = small[...]
+    width, row = hold.shape[1], 8
+    for j in range(g_bi.shape[1] // width):
+        hold[row:row + 1, :] = g_bi[:, j * width:(j + 1) * width]
+        row += 1
+    cols = g_b.shape[1]
+    for j in range(2):
+        hold[row + j * cols // width:row + j * cols // width + 1, pl.ds(j * cols % width, cols)] = g_b[j:j + 1, :]
     barrier = pltpu.get_barrier_semaphore()
-    for b in range(bits):
-        pl.semaphore_signal(barrier, inc=1, device_id={"batch": flip(me, b)}, device_id_type=MESH)
+    friends = [flip(me, b) for b in range(bits)] + ([mirror] if n == LINE else [])
+    for friend in friends:
+        pl.semaphore_signal(barrier, inc=1, device_id={"batch": friend}, device_id_type=MESH)
     pl.semaphore_signal(barrier, inc=1, device_id={"head": 1 - head}, device_id_type=MESH)
-    pl.semaphore_wait(barrier, bits + 1)
+    pl.semaphore_wait(barrier, len(friends) + 1)
 
     def copy_of(c, s):
-        kind, b = plans[c][s]
+        kind, b, _ = plans[c][s]
         _, start, length, at = spans[c][s]
         place = (c, pl.ds(pl.multiple_of(start, 16), length))
-        if kind == "gather":
-            src, dst = full.at[place], full.at[place]
-        else:
-            src, dst = work.at[place], got.at[c, pl.ds(at, length)]
+        src = full.at[place] if kind in LANDS else work.at[place]
+        dst = full.at[place] if kind in LANDS else got.at[c, pl.ds(at, length)]
         return pltpu.make_async_remote_copy(
             src_ref=src, dst_ref=dst, send_sem=send_sem.at[c, s], recv_sem=recv_sem.at[c, s],
-            device_id={"batch": flip(me, b)}, device_id_type=MESH)
+            device_id={"batch": mirror if kind.endswith("mid") else flip(me, b)}, device_id_type=MESH)
 
     def finish(c, s):
+        kind = plans[c][s][0]
         keep, _, length, at = spans[c][s]
+        sender, receiver = roles(kind)
         if s == 0 and loads[c] is not None:
             for move in moves(c, False):
                 move.wait()
         else:
-            copy_of(c, s).wait()
-        if plans[c][s][0] != "gather":
-            target = full if plans[c][s + 1][0] == "gather" else work
+            only(sender, lambda: copy_of(c, s).wait_send())
+
+        def take():
+            if s > 0 or loads[c] is None:
+                copy_of(c, s).wait_recv()
+            if kind in LANDS:
+                return
+            target = full if plans[c][s + 1][0] in LANDS else work
 
             def add(i, _):
                 here = pl.ds(pl.multiple_of(keep + i * 16, 16), 16)
@@ -598,6 +657,7 @@
                 target[c, here, :] = (work[c, here, :].astype(F32) + got[c, there, :].astype(F32)).astype(BF16)
                 return 0
             lax.fori_loop(0, length // 16, add, 0)
+        only(receiver, take)
 
     def tiny_copy(k):
         rest = hold.at[pl.ds(0, 8)] if k == 0 else hold
@@ -615,7 +675,7 @@
             hold[...] += tiny_got[k]
 
     done = [load is not None for load in loads]
-    events = [(c, s + done[c]) for c, s in event_order(n, [p[d:] for p, d in zip(plans, done)], done)]
+    events = [(c, s + done[c]) for c, s in event_order(n, [p[d:] for p, d in zip(plans, done)], rows)]
     gap = len(events) // (bits + 2)
     for e, (c, s) in enumerate(events):
         if s == 0:
@@ -623,7 +683,11 @@
                 move.wait()
         else:
             finish(c, s - 1)
-        copy_of(c, s).start()
+        if s == len(plans[c]):
+            for move in moves(c, True):
+                move.start()
+        else:
+            only(roles(plans[c][s][0])[0], lambda: copy_of(c, s).start())
         if e % gap == 0 and e // gap <= bits:
             k = e // gap
             if k > 0:
@@ -632,84 +696,70 @@
     tiny_finish(bits)
     tiny_out[...] = hold[...]
     for c in range(nc):
-        finish(c, len(plans[c]) - 1)
-        for move in moves(c, True):
-            move.start()
-    for c in range(nc):
         for move in moves(c, True):
             move.wait()
 
 
-EARLY_MIX = (0, 0, 0, 1, 1, 1, 2, 3)
-LATE_MIX = (0, 1, 2, 0, 1, 3, 0, 1)
-ROWS = 256
-
-
 def reduce_gradients(early, late, shapes, tiny, n):
-    width = tiny.shape[1]
+    width = tiny[0].shape[1]
+    tiny_shape = (16, width)
     saves = chunk_pieces(shapes, ROWS, width)
     count = early[0].shape[0] // 2
-    slots, colors, loads = [0, 0, 0], [], []
+    slots, plans, loads = [0, 0], [], []
     for which in range(2):
         for c in range(count):
-            color = EARLY_MIX[c * len(EARLY_MIX) // count]
-            axis = min(color, 2)
-            loads.append((0, which * count + c, 1 + axis, slots[axis]))
-            slots[axis] += 1
-            colors.append(color)
+            color = c * 2 // count
+            loads.append((0, which * count + c, 1 + color, slots[color]))
+            slots[color] += 1
+            plans.append(chunk_plan(n, color, ROWS))
     for c in range(len(saves) - 2 * count):
-        colors.append(LATE_MIX[c % len(LATE_MIX)])
+        plans.append(chunk_plan(n, LATE_COLORS[c % len(LATE_COLORS)], ROWS))
         loads.append(None)
-    rank = [(c % count, c // count) if c < 2 * count else (c - 2 * count, 2) for c in range(len(saves))]
-    order = sorted(range(len(saves)), key=lambda c: rank[c])
-    saves, colors, loads = ([array[c] for c in order] for array in (saves, colors, loads))
     nc = len(saves)
-    stages = len(chunk_plan(n, 0))
+    stages = max(len(plan) for plan in plans)
     _, bits = grid_bits(n)
-    got_rows = ROWS - ROWS // 8 + (bits - 3) * ROWS // 8
+    got_rows = max(sum(size for kind, _, size in plan if kind not in LANDS) for plan in plans)
     grads = (*early, *late)
     hbm = lambda k: [pl.BlockSpec(memory_space=pl.ANY)] * k
     done = pl.pallas_call(
-        functools.partial(reduce_kernel, n, colors, ROWS, loads, saves, len(grads), len(shapes)),
-        out_shape=(*(jax.ShapeDtypeStruct(shape, BF16) for shape in shapes), jax.ShapeDtypeStruct(tiny.shape, F32)),
-        in_specs=hbm(len(grads)) + vmem(1), out_specs=tuple(hbm(len(shapes)) + vmem(1)),
+        functools.partial(reduce_kernel, n, plans, ROWS, loads, saves, len(grads), len(shapes)),
+        out_shape=(*(jax.ShapeDtypeStruct(shape, BF16) for shape in shapes), jax.ShapeDtypeStruct(tiny_shape, F32)),
+        in_specs=hbm(len(grads)) + vmem(3), out_specs=tuple(hbm(len(shapes)) + vmem(1)),
         scratch_shapes=[
             pltpu.VMEM((nc, ROWS, width), BF16), pltpu.VMEM((nc, got_rows, width), BF16),
-            pltpu.VMEM((nc, ROWS, width), BF16), pltpu.VMEM(tiny.shape, F32),
-            pltpu.VMEM((bits + 1,) + tiny.shape, F32),
+            pltpu.VMEM((nc, ROWS, width), BF16), pltpu.VMEM(tiny_shape, F32),
+            pltpu.VMEM((bits + 1,) + tiny_shape, F32),
             pltpu.SemaphoreType.DMA((nc, 2)), pltpu.SemaphoreType.DMA((nc, 2)),
             pltpu.SemaphoreType.DMA((nc, stages)), pltpu.SemaphoreType.DMA((nc, stages)),
             pltpu.SemaphoreType.DMA((2, bits + 1)),
         ],
         compiler_params=pltpu.CompilerParams(collective_id=0, has_side_effects=True, vmem_limit_bytes=LIMIT),
         name="reduce_gradients",
-    )(*grads, tiny)
+    )(*grads, *tiny)
     return done[:-1], done[-1]
+
+
 def on_device(n_batch, inputs, prior_scores, lengths, w_query, w_key, w_value, b_query, b_value, w_output, b_output,
               gain_attn, shift_attn, w_inner, b_inner, w_outer, b_outer, gain_ffn, shift_ffn, grad_out, grad_scores):
     width = inputs.shape[2]
-    bias = jnp.stack([b_query, b_value]).astype(F32)
-    vec = jnp.stack([b_output, gain_attn, shift_attn, b_outer, gain_ffn, shift_ffn]).astype(F32)
-    rows, q, k, v = project_rows(inputs, w_query, w_key, w_value, bias)
+    vectors = (b_output, gain_attn, shift_attn, b_outer, gain_ffn, shift_ffn, b_inner)
+    rows, q, k, v = project_rows(inputs, w_query, w_key, w_value, b_query, b_value)
     new_scores, context, norm = attend(lengths, q, k, v, prior_scores)
-    firsts, _ = grid_bits(n_batch)
+    firsts = grid_bits(n_batch)[0][:2]
     chunks = w_inner.size // (ROWS * width)
-    counts = [chunks * sum(min(color, 2) == axis for color in EARLY_MIX) // len(EARLY_MIX) for axis in range(3)]
+    counts = [chunks // 2] * 2
     outputs, dz1, dc, g_wo, keep, *gives, small, g_bi = middle(
-        context, inputs, w_output, w_inner, w_outer, vec, b_inner.astype(F32)[None], grad_out, firsts, counts, ROWS)
+        context, inputs, w_output, w_inner, w_outer, vectors, grad_out, firsts, counts, ROWS)
     taken = [lax.ppermute(give, "batch", [(i, flip(i, first)) for i in range(n_batch)])
              for give, first in zip(gives, firsts)]
     grad_prior, dq, dk, dv = attend_back(lengths, q, k, v, dc, prior_scores, norm, grad_scores)
     grad_inputs, g_wq, g_wk, g_wv, g_b = project_back(rows, dq, dk, dv, w_query, w_key, w_value, dz1)
-    pad = lambda a, to: jnp.pad(a, ((0, to - a.shape[0]), (0, 0)))
-    mine = jnp.concatenate([g_bi.reshape(-1, width), g_b.reshape(-1, width)])
-    tiny = jnp.concatenate([pad(small, 8), pad(mine, 8)])
     late = (g_wo, g_wq, g_wk, g_wv)
     shapes = [w_inner.shape, w_outer.shape] + [g.shape for g in late]
-    grads, tiny = reduce_gradients((keep, *taken), late, shapes, tiny, n_batch)
+    grads, tiny = reduce_gradients((keep, *taken), late, shapes, (small, g_bi, g_b), n_batch)
     g_wi, g_wf, g_wo, g_wq, g_wk, g_wv = [g.astype(F32) for g in grads]
     g_bi = tiny[8:8 + g_bi.size // width].reshape(-1)
-    g_b = tiny[8 + g_bi.size // width:8 + mine.shape[0]].reshape(g_b.shape)
+    g_b = tiny[8 + g_bi.size // width:][:g_b.size // width].reshape(g_b.shape)
     return (outputs, new_scores, grad_inputs, grad_prior, g_wq, g_wk, g_wv, g_b[0], g_b[1], g_wo,
             tiny[0], tiny[1], tiny[2], g_wi, g_bi, g_wf, tiny[3], tiny[4], tiny[5])
 

time: 339 us -> 314 us (0.926)
  local copies, waits for them, and re-layouts: 25.9 us -> 6.25 us
  Pallas kernels: 284 us -> 274 us
  waiting for transfers between devices: 0.01 us -> 9.63 us
  other arithmetic: 21.5 us -> 17.7 us
    unnamed x51 -> x20, local copies, waits for them, and re-layouts: 16.9 us -> 3.33 us
    ppermute x3 -> x2, waiting for transfers between devices: 0.01 us -> 9.63 us  [on_device(): lax.ppermute(give, 'batch', [(i, flip(i, first)) for i in range(n_batch)])]
    pallas_call x1, Pallas kernels: 159 us -> 150 us  [reduce_gradients(): pl.pallas_call(functools.partial(reduce_kernel, n, plans, ROWS, loads, sa...]
    another operation x9 -> x0, local copies, waits for them, and re-layouts: 5.53 us -> none  [the longest x7 4.16 us: on_device(): jnp.stack([b_output, gain_attn, shift_attn, b_outer, gain_ffn, shift_ffn])]
  transfers between devices with their start and end apart: 3 -> 2, of which waited for: 0 -> 2; matrix products, arithmetic and copies ran while one was open for 1% -> 0% of each run, Pallas kernels for 11% -> 12%
where the time goes in v4:
time: 314 us; the launch traced here: 313 us
  Pallas kernels  274 us (87%)
  other arithmetic  17.7 us (6%)
  waiting for transfers between devices  9.63 us (3%)
  local copies, waits for them, and re-layouts  6.25 us (2%)
  starting transfers between devices  4.4 us (1%)
    pallas_call x1, Pallas kernels, reduce_gradients(): pl.pallas_call(functools.partial(reduce_kernel, n, plans, ROWS, loads, sa...  150 us
    pallas_call x1, Pallas kernels, middle(): pl.pallas_call(functools.partial(middle_kernel, seqs, part, firsts), out_...  61.6 us
    pallas_call x1, Pallas kernels, attend_back(): pl.pallas_call(functools.partial(attend_back_kernel, 256, pair // 2), gri...  22.9 us
    pallas_call x1, Pallas kernels, attend(): pl.pallas_call(functools.partial(attend_kernel, 256, pair // 2), grid_spe...  18.2 us
    convert_element_type x6, other arithmetic, on_device(): g_wi, g_wf, g_wo, g_wq, g_wk, g_wv = [g.astype(F32) for g in grads]  17.7 us
    pallas_call x1, Pallas kernels, project_back(): pl.pallas_call(functools.partial(project_back_kernel, seqs, part), out_sh...  13.6 us
    ppermute x2, waiting for transfers between devices, on_device(): lax.ppermute(give, 'batch', [(i, flip(i, first)) for i in range(n_batch)])  9.63 us
    pallas_call x1, Pallas kernels, project_rows(): pl.pallas_call(functools.partial(project_kernel, seqs, part), out_shape=(...  8.55 us
  transfers between devices with their start and end apart: 2, of which 2 were waited for; matrix products, arithmetic and copies ran while one was open for 0% of the time, Pallas kernels for 12%

profile of v4, /device:TPU:0, one launch (start us, length us, event | category | flops | bytes accessed | tf_op | source)
XLA Modules:
  0.0 313.1 jit_solution(17186340530267548220)
XLA Ops:
  0.7 8.5 %project_rows.1 = (bf16[1024,1024]{1,0:T(8,128)(2,1)}, bf16[1024,512]{1,0:T(8,128)(2,1)}, bf16[1024,512]{1,0:T(8,128)(2,1)}, bf16[1024,512]{1,0:T(8,128)(2,1)}) custom-call(bf16[2,256,1024]{2,1,0:T(8,128)(2,1)} %x.3, bf16[1024,512]{1,0:T(8,128)(2,1)} %wq.3, bf16[1024,512]{1,0:T(8,128)(2,1)} %wk.3, bf16[1024,512]{1,0:T(8,128)(2,1)} %wv.3, ...), custom_call_target="tpu_custom_call" | custom-call | tf_op jit(solution)/shard_map/project_rows/pallas_call | solution.py:82
  9.2 18.2 %attend.1 = (bf16[2,8,512,512]{3,2,1,0:T(8,128)(2,1)}, bf16[1024,512]{1,0:T(8,128)(2,1)}, f32[2,4,512,128]{3,2,1,0:T(8,128)}) custom-call(s32[2]{0:T(128)} %lengths.3, bf16[1024,512]{1,0:T(8,128)(2,1)} %get-tuple-element.51.q, bf16[1024,512]{1,0:T(8,128)(2,1)} %get-tuple-element.52.k, bf16[1024,512]{1,0:T(8,128)(2,1)} %get-tuple-element.53.v, ...), custom_call_target="tpu_custom_call" | custom-call | tf_op jit(solution)/shard_map/attend/pallas_call | solution.py:122
  27.4 61.6 %middle.1 = (bf16[2,256,1024]{2,1,0:T(8,128)(2,1)}, f32[2,256,1024]{2,1,0:T(8,128)}, bf16[1024,512]{1,0:T(8,128)(2,1)}, bf16[512,1024]{1,0:T(8,128)(2,1)}, bf16[...) custom-call(bf16[1024,512]{1,0:T(8,128)(2,1)} %get-tuple-element.54., ...), custom_call_target="tpu_custom_call" | custom-call | flops 30064771072 | bytes 31457280 | tf_op jit(solution)/shard_map/middle/pallas_call | solution.py:406
  89.1 2.9 collective-permute-start
  92.0 1.5 collective-permute-start.1
  93.5 22.9 %attend_back.1 = (bf16[2,8,512,512]{3,2,1,0:T(8,128)(2,1)}, bf16[1024,512]{1,0:T(8,128)(2,1)}, bf16[1024,512]{1,0:T(8,128)(2,1)}, bf16[1024,512]{1,0:T(8,128)(2,1)}) custom-call(s32[2]{0:T(128)} %lengths.3, bf16[1024,512]{1,0:T(8,128)(2,1)} %get-tuple-element.51.q, bf16[1024,512]{1,0:T(8,128)(2,1)} %get-tuple-element.52.k, ...), custom_call_target="tpu_custom_call" | custom-call | flops 10737418240 | bytes 25165824 | tf_op jit(solution)/shard_map/attend_back/pallas_call | solution.py:170
  116.4 13.6 %project_back.1 = (bf16[2,256,1024]{2,1,0:T(8,128)(2,1)}, bf16[1024,512]{1,0:T(8,128)(2,1)}, bf16[1024,512]{1,0:T(8,128)(2,1)}, bf16[1024,512]{1,0:T(8,128)(2,1)}, f32[2,512]{1,0:T(2,128)}) custom-call(bf16[1024,1024]{1,0:T(8,128)(2,1)} %get-tuple-element.57.rows, bf16[1024,512]{1,0:T(8,128)(2,1)} %get-tuple-element.60.dq, ...), custom_call_target="tpu_custom_call" | custom-call | flops 6442450944 | bytes 16777216 | tf_op jit(solution)/shard_map/project_back/pallas_call | solution.py:455
  130.0 8.1 %collective-permute-done.refs_1_ = bf16[8,128,1024]{2,1,0:T(8,128)(2,1)S(1)} collective-permute-done((bf16[8,128,1024]{2,1,0:T(8,128)(2,1)}, bf16[8,128,1024]{2,1,0:T(8,128)(2,1)S(1)}, u32[]{:S(2)}, u32[]{:S(2)}) %collective-permute-start) | collective-permute-done | bytes 2097184 | tf_op jit(solution)/shard_map/ppermute | solution.py:753
  138.1 0.0 copy-start.1
  138.1 1.6 collective-permute-done.1.refs_2_
  139.7 0.0 copy-done.1
  139.7 149.5 %reduce_gradients.1 = (bf16[1024,2048]{1,0:T(8,128)(2,1)}, bf16[2048,1024]{1,0:T(8,128)(2,1)}, bf16[512,1024]{1,0:T(8,128)(2,1)}, bf16[1024,512]{1,0:T(8,128)(2,...) custom-call(bf16[16,128,1024]{2,1,0:T(8,128)(2,1)} %get-tuple-element.66.refs_0_, ...), custom_call_target="tpu_custom_call" | custom-call | tf_op jit(solution)/shard_map/reduce_gradients/pallas_call | solution.py:724
  289.2 1.6 fusion
  290.8 0.8 slice_bitcast_fusion
  291.6 1.3 fusion.1
  292.9 0.0 copy-start
  292.9 6.8 %convert_element_type.22 = f32[1024,2048]{1,0:T(8,128)} convert(bf16[1024,2048]{1,0:T(8,128)(2,1)} %get-tuple-element.81) | non-fusion elementwise | flops 2097152 | bytes 12582912 | tf_op jit(solution)/shard_map/convert_element_type | solution.py:760
  299.7 0.0 copy-done
  299.7 4.5 %convert_element_type.23 = f32[2048,1024]{1,0:T(8,128)} convert(bf16[2048,1024]{1,0:T(8,128)(2,1)S(1)} %copy-done) | non-fusion elementwise | flops 2097152 | bytes 12582912 | tf_op jit(solution)/shard_map/convert_element_type | solution.py:760
  304.2 0.0 copy-done.5
  304.2 1.6 convert_element_type.18
  305.8 0.0 copy-done.4
  305.8 1.6 convert_element_type.19
  307.4 0.0 copy-done.3
  307.4 1.6 convert_element_type.20
  309.0 0.0 copy-done.2
  309.0 1.6 convert_element_type.21
  310.6 0.6 copy.41
  311.2 0.0 copy-done.6
  311.2 1.0 copy.44
  312.2 0.0 copy-done.7
  312.2 1.0 copy.45
  (6 shorter events, 0.0 us)
Async XLA Ops:
  89.1 49.0 %collective-permute-start = (bf16[8,128,1024]{2,1,0:T(8,128)(2,1)}, bf16[8,128,1024]{2,1,0:T(8,128)(2,1)S(1)}, u32[]{:S(2)}, u32[]{:S(2)}) collective-permute-start(bf16[8,128,1024]{2,1,0:T(8,128)(2,1)} %get-tuple-element.67), channel_id=1, source_target_pairs={{0,1},{1,0},{2,3},{3,2},{4,5},{5,4},{6,7},{7,6},{8,9},{9,8},{10,11... | collective-permute-start | bytes 6291464 | tf_op jit(solution)/shard_map/ppermute | solution.py:753
  92.0 47.7 %collective-permute-start.1 = (bf16[8,128,1024]{2,1,0:T(8,128)(2,1)}, bf16[8,128,1024]{2,1,0:T(8,128)(2,1)}, u32[]{:S(2)}, u32[]{:S(2)}) collective-permute-start(bf16[8,128,1024]{2,1,0:T(8,128)(2,1)} %get-tuple-element.68), channel_id=1, source_target_pairs={{0,2},{1,3},{2,0},{3,1},{4,6},{5,7},{6,4},{7,5},{8,10},{9,11},{10,... | collective-permute-start | bytes 6291464 | tf_op jit(solution)/shard_map/ppermute | solution.py:753
  138.1 1.6 copy-start.1
  292.9 6.8 %copy-start = (bf16[2048,1024]{1,0:T(8,128)(2,1)S(1)}, bf16[2048,1024]{1,0:T(8,128)(2,1)}, u32[]{:S(2)}) copy-start(bf16[2048,1024]{1,0:T(8,128)(2,1)} %get-tuple-element.82) | copy-start | bytes 12582916
  299.7 4.5 %copy-start.5 = (bf16[1024,512]{1,0:T(8,128)(2,1)S(1)}, bf16[1024,512]{1,0:T(8,128)(2,1)}, u32[]{:S(2)}) copy-start(bf16[1024,512]{1,0:T(8,128)(2,1)} %get-tuple-element.76) | copy-start | bytes 3145732
  299.7 6.1 %copy-start.4 = (bf16[1024,512]{1,0:T(8,128)(2,1)S(1)}, bf16[1024,512]{1,0:T(8,128)(2,1)}, u32[]{:S(2)}) copy-start(bf16[1024,512]{1,0:T(8,128)(2,1)} %get-tuple-element.77) | copy-start | bytes 3145732
  304.2 3.2 %copy-start.3 = (bf16[1024,512]{1,0:T(8,128)(2,1)S(1)}, bf16[1024,512]{1,0:T(8,128)(2,1)}, u32[]{:S(2)}) copy-start(bf16[1024,512]{1,0:T(8,128)(2,1)} %get-tuple-element.78) | copy-start | bytes 3145732
  304.2 4.8 %copy-start.2 = (bf16[512,1024]{1,0:T(8,128)(2,1)S(1)}, bf16[512,1024]{1,0:T(8,128)(2,1)}, u32[]{:S(2)}) copy-start(bf16[512,1024]{1,0:T(8,128)(2,1)} %get-tuple-element.80) | copy-start | bytes 3145732
  305.8 5.4 %copy-start.6 = (bf16[2,256,1024]{2,1,0:T(8,128)(2,1)S(1)}, bf16[2,256,1024]{2,1,0:T(8,128)(2,1)}, u32[]{:S(2)}) copy-start(bf16[2,256,1024]{2,1,0:T(8,128)(2,1)} %get-tuple-element.110) | copy-start | bytes 3145732
  307.4 4.8 %copy-start.7 = (bf16[2,256,1024]{2,1,0:T(8,128)(2,1)S(1)}, bf16[2,256,1024]{2,1,0:T(8,128)(2,1)}, u32[]{:S(2)}) copy-start(bf16[2,256,1024]{2,1,0:T(8,128)(2,1)} %get-tuple-element.112) | copy-start | bytes 3145732

commit v5 on v4

--- a/solution.py
+++ b/solution.py
@@ -96,11 +96,11 @@
     scale = head ** -0.5
     for r in range(0, full, block):
         rows = pl.ds(r, block)
-        queries = q[rows, :]
+        queries = q[rows, :] * jnp.asarray(scale, BF16)
         parts, norms = [], []
         for h in range(2):
             mine = jnp.where(first == (h == 0), queries, jnp.zeros_like(queries))
-            scores = dot_t(mine, k[...]) * scale + prior[0, h, rows, :].astype(F32)
+            scores = dot_t(mine, k[...]) + prior[0, h, rows, :].astype(F32)
             score[0, h, rows, :] = scores.astype(BF16)
             masked = jnp.where(live, scores, NEG)
             top = jnp.max(masked, axis=-1, keepdims=True)
@@ -140,11 +140,11 @@
     dk_t, dv_t = [0.0, 0.0], [0.0, 0.0]
     for r in range(0, full, block):
         rows = pl.ds(r, block)
-        queries, cots = q[rows, :], dc[rows, :]
+        queries, cots = q[rows, :] * jnp.asarray(scale, BF16), dc[rows, :]
         parts = []
         for h in range(2):
             mine = first == (h == 0)
-            scores = dot_t(jnp.where(mine, queries, jnp.zeros_like(queries)), k[...]) * scale
+            scores = dot_t(jnp.where(mine, queries, jnp.zeros_like(queries)), k[...])
             scores = scores + prior[0, h, rows, :].astype(F32)
             probs = jnp.exp(jnp.where(live, scores, NEG) - norm[0, 0, rows, h * head:h * head + 1])
             dp = dot_t(jnp.where(mine, cots, jnp.zeros_like(cots)), v[...])
@@ -739,6 +739,43 @@
     return done[:-1], done[-1]
 
 
+def results_kernel(count, plain, *refs):
+    ins, tiny, outs = refs[:count + plain], refs[count + plain], refs[count + plain + 1:]
+    for src, dst in zip(ins, outs):
+        dst[...] = src[...].astype(dst.dtype)
+
+    @pl.when(pl.program_id(0) == 0)
+    def _():
+        row = 0
+        for place, dst in zip((0, 1, 2, 3, 4, 5, 8), outs[count + plain:]):
+            width = tiny.shape[1]
+            for j in range(dst.shape[0] // width):
+                dst[pl.ds(j * width, width)] = tiny[place + j, :]
+                row = place + j + 1
+        for j, dst in enumerate(outs[count + plain + 7:]):
+            at = j * dst.shape[0]
+            dst[...] = tiny[row + at // tiny.shape[1], pl.ds(at % tiny.shape[1], dst.shape[0])]
+
+
+def results(grads, rows, tiny, hidden, cols, steps=8):
+    flat = [r.reshape(-1, r.shape[-1]) for r in rows]
+    blocks = [pl.BlockSpec((a.shape[0] // steps, a.shape[1]), lambda i: (i, 0)) for a in (*grads, *flat)]
+    vectors = [tiny.shape[1]] * 6 + [hidden, cols, cols]
+    done = pl.pallas_call(
+        functools.partial(results_kernel, len(grads), len(flat)),
+        grid=(steps,),
+        in_specs=blocks + [pl.BlockSpec(tiny.shape, lambda i: (0, 0))],
+        out_specs=tuple(blocks + [pl.BlockSpec((v,), lambda i: (0,)) for v in vectors]),
+        out_shape=tuple([jax.ShapeDtypeStruct(g.shape, F32) for g in grads]
+                        + [jax.ShapeDtypeStruct(f.shape, f.dtype) for f in flat]
+                        + [jax.ShapeDtypeStruct((v,), F32) for v in vectors]),
+        compiler_params=pltpu.CompilerParams(vmem_limit_bytes=LIMIT),
+        name="results",
+    )(*grads, *flat, tiny)
+    grads, flat, vectors = done[:len(grads)], done[len(grads):-len(vectors)], done[-len(vectors):]
+    return grads, [f.reshape(r.shape) for f, r in zip(flat, rows)], vectors
+
+
 def on_device(n_batch, inputs, prior_scores, lengths, w_query, w_key, w_value, b_query, b_value, w_output, b_output,
               gain_attn, shift_attn, w_inner, b_inner, w_outer, b_outer, gain_ffn, shift_ffn, grad_out, grad_scores):
     width = inputs.shape[2]
@@ -757,11 +794,12 @@
     late = (g_wo, g_wq, g_wk, g_wv)
     shapes = [w_inner.shape, w_outer.shape] + [g.shape for g in late]
     grads, tiny = reduce_gradients((keep, *taken), late, shapes, (small, g_bi, g_b), n_batch)
-    g_wi, g_wf, g_wo, g_wq, g_wk, g_wv = [g.astype(F32) for g in grads]
-    g_bi = tiny[8:8 + g_bi.size // width].reshape(-1)
-    g_b = tiny[8 + g_bi.size // width:][:g_b.size // width].reshape(g_b.shape)
-    return (outputs, new_scores, grad_inputs, grad_prior, g_wq, g_wk, g_wv, g_b[0], g_b[1], g_wo,
-            tiny[0], tiny[1], tiny[2], g_wi, g_bi, g_wf, tiny[3], tiny[4], tiny[5])
+    hidden, cols = g_bi.shape[1], g_b.shape[1]
+    grads, (outputs, grad_inputs), vectors = results(grads, (outputs, grad_inputs), tiny, hidden, cols)
+    g_wi, g_wf, g_wo, g_wq, g_wk, g_wv = grads
+    g_bo, g_g1, g_s1, g_bf, g_g2, g_s2, g_bi, g_bq, g_bv = vectors
+    return (outputs, new_scores, grad_inputs, grad_prior, g_wq, g_wk, g_wv, g_bq, g_bv, g_wo,
+            g_bo, g_g1, g_s1, g_wi, g_bi, g_wf, g_bf, g_g2, g_s2)
 
 
 def solution(mesh):

time: 314 us -> 306 us (0.975)
  other arithmetic: 17.7 us -> 0 us
  Pallas kernels: 274 us -> 289 us
  local copies, waits for them, and re-layouts: 6.25 us -> 0.01 us
    convert_element_type x6 -> x0, other arithmetic: 17.7 us -> none  [on_device(): g_wi, g_wf, g_wo, g_wq, g_wk, g_wv = [g.astype(F32) for g in grads]]
    pallas_call x0 -> x1, Pallas kernels: none -> 15.6 us  [results(): pl.pallas_call(functools.partial(results_kernel, len(grads), len(flat)),...]
    unnamed x20 -> x2, local copies, waits for them, and re-layouts: 3.33 us -> 0.01 us
where the time goes in v5:
time: 306 us; the launch traced here: 305 us
  Pallas kernels  289 us (94%)
  waiting for transfers between devices  10.3 us (3%)
  starting transfers between devices  4.39 us (1%)
    pallas_call x1, Pallas kernels, reduce_gradients(): pl.pallas_call(functools.partial(reduce_kernel, n, plans, ROWS, loads, sa...  150 us
    pallas_call x1, Pallas kernels, middle(): pl.pallas_call(functools.partial(middle_kernel, seqs, part, firsts), out_...  61.6 us
    pallas_call x1, Pallas kernels, attend_back(): pl.pallas_call(functools.partial(attend_back_kernel, 256, pair // 2), gri...  22.2 us
    pallas_call x1, Pallas kernels, attend(): pl.pallas_call(functools.partial(attend_kernel, 256, pair // 2), grid_spe...  18.4 us
    pallas_call x1, Pallas kernels, results(): pl.pallas_call(functools.partial(results_kernel, len(grads), len(flat)),...  15.6 us
    pallas_call x1, Pallas kernels, project_back(): pl.pallas_call(functools.partial(project_back_kernel, seqs, part), out_sh...  13.7 us
    ppermute x2, waiting for transfers between devices, on_device(): lax.ppermute(give, 'batch', [(i, flip(i, first)) for i in range(n_batch)])  10.3 us
    pallas_call x1, Pallas kernels, project_rows(): pl.pallas_call(functools.partial(project_kernel, seqs, part), out_shape=(...  8.52 us
  transfers between devices with their start and end apart: 2, of which 2 were waited for; matrix products, arithmetic and copies ran while one was open for 0% of the time, Pallas kernels for 12%

profile of v5, /device:TPU:0, one launch (start us, length us, event | category | flops | bytes accessed | tf_op | source)
XLA Modules:
  0.0 305.1 jit_solution(13719174868546084858)
XLA Ops:
  0.7 8.5 %project_rows.1 = (bf16[1024,1024]{1,0:T(8,128)(2,1)}, bf16[1024,512]{1,0:T(8,128)(2,1)}, bf16[1024,512]{1,0:T(8,128)(2,1)}, bf16[1024,512]{1,0:T(8,128)(2,1)}) custom-call(bf16[2,256,1024]{2,1,0:T(8,128)(2,1)} %x.3, bf16[1024,512]{1,0:T(8,128)(2,1)} %wq.3, bf16[1024,512]{1,0:T(8,128)(2,1)} %wk.3, bf16[1024,512]{1,0:T(8,128)(2,1)} %wv.3, ...), custom_call_target="tpu_custom_call" | custom-call | tf_op jit(solution)/shard_map/project_rows/pallas_call | solution.py:82
  9.2 18.4 %attend.1 = (bf16[2,8,512,512]{3,2,1,0:T(8,128)(2,1)}, bf16[1024,512]{1,0:T(8,128)(2,1)}, f32[2,4,512,128]{3,2,1,0:T(8,128)}) custom-call(s32[2]{0:T(128)} %lengths.3, bf16[1024,512]{1,0:T(8,128)(2,1)} %get-tuple-element.68.q, bf16[1024,512]{1,0:T(8,128)(2,1)} %get-tuple-element.69.k, bf16[1024,512]{1,0:T(8,128)(2,1)} %get-tuple-element.70.v, ...), custom_call_target="tpu_custom_call" | custom-call | tf_op jit(solution)/shard_map/attend/pallas_call | solution.py:122
  27.6 61.6 %middle.1 = (bf16[2,256,1024]{2,1,0:T(8,128)(2,1)}, f32[2,256,1024]{2,1,0:T(8,128)}, bf16[1024,512]{1,0:T(8,128)(2,1)}, bf16[512,1024]{1,0:T(8,128)(2,1)}, bf16[...) custom-call(bf16[1024,512]{1,0:T(8,128)(2,1)} %get-tuple-element.71., ...), custom_call_target="tpu_custom_call" | custom-call | flops 30064771072 | bytes 31457280 | tf_op jit(solution)/shard_map/middle/pallas_call | solution.py:406
  89.1 2.9 collective-permute-start
  92.0 1.5 collective-permute-start.1
  93.5 22.2 %attend_back.1 = (bf16[2,8,512,512]{3,2,1,0:T(8,128)(2,1)}, bf16[1024,512]{1,0:T(8,128)(2,1)}, bf16[1024,512]{1,0:T(8,128)(2,1)}, bf16[1024,512]{1,0:T(8,128)(2,1)}) custom-call(s32[2]{0:T(128)} %lengths.3, bf16[1024,512]{1,0:T(8,128)(2,1)} %get-tuple-element.68.q, bf16[1024,512]{1,0:T(8,128)(2,1)} %get-tuple-element.69.k, ...), custom_call_target="tpu_custom_call" | custom-call | flops 10737418240 | bytes 25165824 | tf_op jit(solution)/shard_map/attend_back/pallas_call | solution.py:170
  115.7 13.7 %project_back.1 = (bf16[2,256,1024]{2,1,0:T(8,128)(2,1)}, bf16[1024,512]{1,0:T(8,128)(2,1)}, bf16[1024,512]{1,0:T(8,128)(2,1)}, bf16[1024,512]{1,0:T(8,128)(2,1)}, f32[2,512]{1,0:T(2,128)}) custom-call(bf16[1024,1024]{1,0:T(8,128)(2,1)} %get-tuple-element.76.rows, bf16[1024,512]{1,0:T(8,128)(2,1)} %get-tuple-element.79.dq, ...), custom_call_target="tpu_custom_call" | custom-call | flops 6442450944 | bytes 16777216 | tf_op jit(solution)/shard_map/project_back/pallas_call | solution.py:455
  129.4 8.8 %collective-permute-done.refs_1_ = bf16[8,128,1024]{2,1,0:T(8,128)(2,1)S(1)} collective-permute-done((bf16[8,128,1024]{2,1,0:T(8,128)(2,1)}, bf16[8,128,1024]{2,1,0:T(8,128)(2,1)S(1)}, u32[]{:S(2)}, u32[]{:S(2)}) %collective-permute-start) | collective-permute-done | bytes 2097184 | tf_op jit(solution)/shard_map/ppermute | solution.py:790
  138.2 0.0 copy-start
  138.2 1.6 collective-permute-done.1.refs_2_
  139.7 0.0 copy-done
  139.7 149.6 %reduce_gradients.1 = (bf16[1024,2048]{1,0:T(8,128)(2,1)}, bf16[2048,1024]{1,0:T(8,128)(2,1)}, bf16[512,1024]{1,0:T(8,128)(2,1)}, bf16[1024,512]{1,0:T(8,128)(2,...) custom-call(bf16[16,128,1024]{2,1,0:T(8,128)(2,1)} %get-tuple-element.72.refs_0_, ...), custom_call_target="tpu_custom_call" | custom-call | tf_op jit(solution)/shard_map/reduce_gradients/pallas_call | solution.py:724
  289.3 15.6 %results.1 = (f32[1024,2048]{1,0:T(8,128)}, f32[2048,1024]{1,0:T(8,128)}, f32[512,1024]{1,0:T(8,128)}, f32[1024,512]{1,0:T(8,128)}, f32[1024,512]{1,0:T(8,128)},...) custom-call(bf16[1024,2048]{1,0:T(8,128)(2,1)} %get-tuple-element.89, ...), custom_call_target="tpu_custom_call" | custom-call | tf_op jit(solution)/shard_map/results/pallas_call | solution.py:764
Async XLA Ops:
  89.1 49.0 %collective-permute-start = (bf16[8,128,1024]{2,1,0:T(8,128)(2,1)}, bf16[8,128,1024]{2,1,0:T(8,128)(2,1)S(1)}, u32[]{:S(2)}, u32[]{:S(2)}) collective-permute-start(bf16[8,128,1024]{2,1,0:T(8,128)(2,1)} %get-tuple-element.73), channel_id=1, source_target_pairs={{0,1},{1,0},{2,3},{3,2},{4,5},{5,4},{6,7},{7,6},{8,9},{9,8},{10,11... | collective-permute-start | bytes 6291464 | tf_op jit(solution)/shard_map/ppermute | solution.py:790
  92.0 47.7 %collective-permute-start.1 = (bf16[8,128,1024]{2,1,0:T(8,128)(2,1)}, bf16[8,128,1024]{2,1,0:T(8,128)(2,1)}, u32[]{:S(2)}, u32[]{:S(2)}) collective-permute-start(bf16[8,128,1024]{2,1,0:T(8,128)(2,1)} %get-tuple-element.74), channel_id=1, source_target_pairs={{0,2},{1,3},{2,0},{3,1},{4,6},{5,7},{6,4},{7,5},{8,10},{9,11},{10,... | collective-permute-start | bytes 6291464 | tf_op jit(solution)/shard_map/ppermute | solution.py:790
  138.2 1.6 copy-start

commit v6 on v5

--- a/solution.py
+++ b/solution.py
@@ -197,15 +197,20 @@
 
 
 def middle_kernel(seqs, part, firsts, c, x, wo, wi, wf, b_output, gain1, shift1, b_outer, gain2, shift2, b_inner, gout,
-                  out, dz1, dc, g_wo, keep, give_x, give_y, small, g_bi,
-                  unit1, r1, dz2, hn, act, slope, df, du, da, give, got, own, sums, bsum, bi, sems):
+                  out, dz1, dc, keep, give_x, give_y, taken, small, g_bi,
+                  unit1, r1, dz2, hn, act, slope, df, du, da, give, got, own, sums, bsum, bi, give_f, sems, far_sems):
     me = lax.axis_index("head")
     other = 1 - me
     width = x.shape[2]
     hidden = wi.shape[1]
     tile = 512
     sub = 64
-    meet(other)
+    barrier = pltpu.get_barrier_semaphore()
+    pl.semaphore_signal(barrier, inc=1, device_id={"head": other}, device_id_type=MESH)
+    for first in firsts:
+        pl.semaphore_signal(barrier, inc=1, device_id={"batch": flip(lax.axis_index("batch"), first)},
+                            device_id_type=MESH)
+    pl.semaphore_wait(barrier, 3)
     b_output, gain1, shift1, b_outer, gain2, shift2 = map(as_row, (b_output, gain1, shift1, b_outer, gain2, shift2))
     sums[...] = jnp.zeros_like(sums)
     bsum[...] = jnp.zeros_like(bsum)
@@ -299,6 +304,40 @@
         block = df.at[rows_of(s, me)]
         to_partner(block, block, sems, 3 * seqs + s, other).start()
 
+    mine = lax.axis_index("batch")
+    gives = (give_x, give_y)
+    half = keep.shape[1]
+    per = hidden // width
+    side = give_f.shape[0] // 2
+    edge = give_x.shape[0] - side
+
+    def put(value, kept, axis, given, given_at):
+        bit = (mine // (1 << firsts[axis])) % 2
+
+        @pl.when(bit == 0)
+        def _():
+            keep[kept] = value[:half].astype(BF16)
+            given[given_at] = value[half:].astype(BF16)
+
+        @pl.when(bit == 1)
+        def _():
+            keep[kept] = value[half:].astype(BF16)
+            given[given_at] = value[:half].astype(BF16)
+
+    def far_copy(i, axis):
+        return pltpu.make_async_remote_copy(
+            src_ref=give_f.at[i], dst_ref=taken.at[i], send_sem=far_sems.at[0, i], recv_sem=far_sems.at[1, i],
+            device_id={"batch": flip(mine, firsts[axis])}, device_id_type=MESH)
+
+    def grads_outer():
+        for axis in range(2):
+            def give_outer(i, _, axis=axis):
+                chunk = axis * side + i
+                put(t_dot(act[:, at(chunk * 2 * half, 2 * half)], df[...]), 2 * side + chunk, axis, give_f, chunk)
+                far_copy(chunk, axis).start()
+                return 0
+            lax.fori_loop(0, side, give_outer, 0)
+
     def inner_back(s, p):
         rows = rows_of(s, p)
 
@@ -325,6 +364,7 @@
             for q in range(seqs):
                 block = df.at[rows_of(q, me)]
                 to_partner(block, block, sems, 3 * seqs + q, other).wait()
+            grads_outer()
         inner_back(s, p)
         if p is other:
             outer_back(s, p, give.at[pl.ds(2 * seqs, seqs)])
@@ -350,64 +390,45 @@
         block = da.at[rows_of(s, me)]
         to_partner(block, block, sems, 5 * seqs + s, other).start()
 
-    mine = lax.axis_index("batch")
-    gives = (give_x, give_y)
-    half = keep.shape[1]
-    per = hidden // width
-
-    def put(value, kept, axis, given):
-        bit = (mine // (1 << firsts[axis])) % 2
-
-        @pl.when(bit == 0)
-        def _():
-            keep[kept] = value[:half].astype(BF16)
-            gives[axis][given] = value[half:].astype(BF16)
-
-        @pl.when(bit == 1)
-        def _():
-            keep[kept] = value[half:].astype(BF16)
-            gives[axis][given] = value[:half].astype(BF16)
-
-    def grads_of(axis, start, count):
-        def grad_outer(i, _):
-            at_act = at((start + i) * 2 * half, 2 * half)
-            put(t_dot(act[:, at_act], df[...]), early + start + i, axis, count + i)
-            return 0
-
-        def grad_inner(i, _):
-            at_hn, at_du = at((start + i) // per * 2 * half, 2 * half), at((start + i) % per * width, width)
-            put(t_dot(hn[:, at_hn], du[:, at_du]), start + i, axis, i)
-            return 0
-
-        lax.fori_loop(0, count, grad_inner, 0)
-        lax.fori_loop(0, count, grad_outer, 0)
-
-    early = keep.shape[0] // 2
-    begin = 0
     for axis in range(2):
-        grads_of(axis, begin, gives[axis].shape[0] // 2)
-        begin += gives[axis].shape[0] // 2
+        def give_inner(i, _, axis=axis):
+            at_hn, at_du = at((axis * side + i) // per * 2 * half, 2 * half), at((axis * side + i) % per * width, width)
+            put(t_dot(hn[:, at_hn], du[:, at_du]), axis * side + i, axis, gives[axis], i)
+            return 0
+        lax.fori_loop(0, side, give_inner, 0)
 
     for s in range(seqs):
         block = da.at[rows_of(s, me)]
         to_partner(block, block, sems, 5 * seqs + s, other).wait()
     dc[...] = dot_t(da[...], wo[...]).astype(BF16)
-    g_wo[...] = t_dot(c[...], da[...]).astype(BF16)
+    for axis in range(2):
+        def give_output(i, _, axis=axis):
+            cols = at((axis * edge + i) * 2 * half, 2 * half)
+            put(t_dot(c[:, cols], da[...]), 4 * side + axis * edge + i, axis, gives[axis], side + i)
+            return 0
+        lax.fori_loop(0, edge, give_output, 0)
     small[...] = jnp.sum(sums[...], axis=1)
     g_bi[...] = jnp.sum(bsum[...], axis=0, keepdims=True)
-
-
-def middle(c, x, wo, wi, wf, vectors, gout, firsts, counts, rows):
+    for axis in range(2):
+        def far_done(i, _, axis=axis):
+            far_copy(axis * side + i, axis).wait()
+            return 0
+        lax.fori_loop(0, side, far_done, 0)
+
+
+def middle(c, x, wo, wi, wf, vectors, gout, firsts, rows):
     seqs, part, width = x.shape
     total, cols = c.shape
     hidden = wi.shape[1]
     sds = jax.ShapeDtypeStruct
-    halves = [sds((2 * count, rows // 2, width), BF16) for count in (sum(counts), *counts)]
+    side, edge = hidden // rows // 2, cols // rows // 2
+    halves = [sds((count, rows // 2, width), BF16)
+              for count in (4 * side + 2 * edge, side + edge, side + edge, 2 * side)]
     return pl.pallas_call(
         functools.partial(middle_kernel, seqs, part, firsts),
-        out_shape=(sds(x.shape, BF16), sds(x.shape, F32), sds(c.shape, BF16), sds(wo.shape, BF16),
+        out_shape=(sds(x.shape, BF16), sds(x.shape, F32), sds(c.shape, BF16),
                    *halves, sds((6, width), F32), sds((1, hidden), F32)),
-        in_specs=vmem(6 + len(vectors)), out_specs=tuple(vmem(9)),
+        in_specs=vmem(6 + len(vectors)), out_specs=(*vmem(6), pl.BlockSpec(memory_space=pl.ANY), *vmem(2)),
         scratch_shapes=[
             pltpu.VMEM(x.shape, F32), pltpu.VMEM((seqs, part, 128), F32), pltpu.VMEM(x.shape, F32),
             pltpu.VMEM((total, width), BF16), pltpu.VMEM((total, hidden), BF16), pltpu.VMEM((total, hidden), F32),
@@ -415,7 +436,8 @@
             pltpu.VMEM((3 * seqs, part, width), BF16), pltpu.VMEM((3, seqs, part, width), BF16),
             pltpu.VMEM(x.shape, BF16), pltpu.VMEM((6, 8, width), F32), pltpu.VMEM((8, hidden), F32),
             pltpu.VMEM((1, hidden), F32),
-            pltpu.SemaphoreType.DMA((2, 6 * seqs)),
+            pltpu.VMEM((2 * side, rows // 2, width), BF16),
+            pltpu.SemaphoreType.DMA((2, 6 * seqs)), pltpu.SemaphoreType.DMA((2, 2 * side)),
         ],
         compiler_params=pltpu.CompilerParams(collective_id=2, has_side_effects=True, vmem_limit_bytes=LIMIT),
         cost_estimate=pl.CostEstimate(flops=14 * total * width * hidden, transcendentals=total * hidden,
@@ -463,8 +485,8 @@
     )(rows, dq, dk, dv, wq, wk, wv, dz1)
 LINE = 16
 ROWS = 256
-LATE_COLORS = (0, 1, 2, 3, 0, 1, 2, 3)
-PRECEDENCE = (29, 13, 18, 0, 6, 13, 11, 17, 6, 9, 1, 15, 15, 6, 22, 21, 13, 2, 9, 12, 8, 7, 35, 19)
+LATE_COLORS = (0, 1, 2, 3, 2, 3)
+PRECEDENCE = (4, 18, 28, 24, 6, 31, 14, 24, 33, 31, 35, 17, 18, 35, 27, 25, 9, 35, 23, 15, 35, 21, 35, 19)
 LANDS = ("gather", "out", "back_in", "back_mid", "back_out")
 
 
@@ -704,15 +726,17 @@
     width = tiny[0].shape[1]
     tiny_shape = (16, width)
     saves = chunk_pieces(shapes, ROWS, width)
-    count = early[0].shape[0] // 2
+    outer = early[3].shape[0]
+    edge = early[0].shape[0] - 2 * outer
     slots, plans, loads = [0, 0], [], []
-    for which in range(2):
+    for which, count in enumerate((outer, outer, edge)):
         for c in range(count):
             color = c * 2 // count
-            loads.append((0, which * count + c, 1 + color, slots[color]))
-            slots[color] += 1
+            kept = which * outer + c
+            loads.append((0, kept, 3, c) if which == 1 else (0, kept, 1 + color, slots[color]))
+            slots[color] += which != 1
             plans.append(chunk_plan(n, color, ROWS))
-    for c in range(len(saves) - 2 * count):
+    for c in range(len(saves) - len(plans)):
         plans.append(chunk_plan(n, LATE_COLORS[c % len(LATE_COLORS)], ROWS))
         loads.append(None)
     nc = len(saves)
@@ -783,17 +807,15 @@
     rows, q, k, v = project_rows(inputs, w_query, w_key, w_value, b_query, b_value)
     new_scores, context, norm = attend(lengths, q, k, v, prior_scores)
     firsts = grid_bits(n_batch)[0][:2]
-    chunks = w_inner.size // (ROWS * width)
-    counts = [chunks // 2] * 2
-    outputs, dz1, dc, g_wo, keep, *gives, small, g_bi = middle(
-        context, inputs, w_output, w_inner, w_outer, vectors, grad_out, firsts, counts, ROWS)
+    outputs, dz1, dc, keep, *gives, far, small, g_bi = middle(
+        context, inputs, w_output, w_inner, w_outer, vectors, grad_out, firsts, ROWS)
     taken = [lax.ppermute(give, "batch", [(i, flip(i, first)) for i in range(n_batch)])
              for give, first in zip(gives, firsts)]
     grad_prior, dq, dk, dv = attend_back(lengths, q, k, v, dc, prior_scores, norm, grad_scores)
     grad_inputs, g_wq, g_wk, g_wv, g_b = project_back(rows, dq, dk, dv, w_query, w_key, w_value, dz1)
-    late = (g_wo, g_wq, g_wk, g_wv)
-    shapes = [w_inner.shape, w_outer.shape] + [g.shape for g in late]
-    grads, tiny = reduce_gradients((keep, *taken), late, shapes, (small, g_bi, g_b), n_batch)
+    late = (g_wq, g_wk, g_wv)
+    shapes = [w_inner.shape, w_outer.shape, w_output.shape] + [g.shape for g in late]
+    grads, tiny = reduce_gradients((keep, *taken, far), late, shapes, (small, g_bi, g_b), n_batch)
     hidden, cols = g_bi.shape[1], g_b.shape[1]
     grads, (outputs, grad_inputs), vectors = results(grads, (outputs, grad_inputs), tiny, hidden, cols)
     g_wi, g_wf, g_wo, g_wq, g_wk, g_wv = grads

time: 306 us -> 302 us (0.987)
  waiting for transfers between devices: 10.3 us -> 0.01 us
  Pallas kernels: 289 us -> 297 us
    ppermute x2, waiting for transfers between devices: 10.3 us -> 0.01 us  [on_device(): lax.ppermute(give, 'batch', [(i, flip(i, first)) for i in range(n_batch)])]
    pallas_call x1, Pallas kernels: 61.6 us -> 67.5 us  [middle(): pl.pallas_call(functools.partial(middle_kernel, seqs, part, firsts), out_...]
  transfers between devices with their start and end apart: 2 -> 2, of which waited for: 2 -> 0; matrix products, arithmetic and copies ran while one was open for 0% -> 0% of each run, Pallas kernels for 12% -> 12%
where the time goes in v6:
time: 302 us; the launch traced here: 301 us
  Pallas kernels  297 us (98%)
    pallas_call x1, Pallas kernels, reduce_gradients(): pl.pallas_call(functools.partial(reduce_kernel, n, plans, ROWS, loads, sa...  151 us
    pallas_call x1, Pallas kernels, middle(): pl.pallas_call(functools.partial(middle_kernel, seqs, part, firsts), out_...  67.5 us
    pallas_call x1, Pallas kernels, attend_back(): pl.pallas_call(functools.partial(attend_back_kernel, 256, pair // 2), gri...  22.2 us
    pallas_call x1, Pallas kernels, attend(): pl.pallas_call(functools.partial(attend_kernel, 256, pair // 2), grid_spe...  18.4 us
    pallas_call x1, Pallas kernels, results(): pl.pallas_call(functools.partial(results_kernel, len(grads), len(flat)),...  15.6 us
    pallas_call x1, Pallas kernels, project_back(): pl.pallas_call(functools.partial(project_back_kernel, seqs, part), out_sh...  13.6 us
    pallas_call x1, Pallas kernels, project_rows(): pl.pallas_call(functools.partial(project_kernel, seqs, part), out_shape=(...  8.61 us
  transfers between devices with their start and end apart: 2, of which 0 were waited for; matrix products, arithmetic and copies ran while one was open for 0% of the time, Pallas kernels for 12%

profile of v6, /device:TPU:0, one launch (start us, length us, event | category | flops | bytes accessed | tf_op | source)
XLA Modules:
  0.0 301.1 jit_solution(9662629966215586185)
XLA Ops:
  0.7 8.6 %project_rows.1 = (bf16[1024,1024]{1,0:T(8,128)(2,1)}, bf16[1024,512]{1,0:T(8,128)(2,1)}, bf16[1024,512]{1,0:T(8,128)(2,1)}, bf16[1024,512]{1,0:T(8,128)(2,1)}) custom-call(bf16[2,256,1024]{2,1,0:T(8,128)(2,1)} %x.3, bf16[1024,512]{1,0:T(8,128)(2,1)} %wq.3, bf16[1024,512]{1,0:T(8,128)(2,1)} %wk.3, bf16[1024,512]{1,0:T(8,128)(2,1)} %wv.3, ...), custom_call_target="tpu_custom_call" | custom-call | tf_op jit(solution)/shard_map/project_rows/pallas_call | solution.py:82
  9.3 18.4 %attend.1 = (bf16[2,8,512,512]{3,2,1,0:T(8,128)(2,1)}, bf16[1024,512]{1,0:T(8,128)(2,1)}, f32[2,4,512,128]{3,2,1,0:T(8,128)}) custom-call(s32[2]{0:T(128)} %lengths.3, bf16[1024,512]{1,0:T(8,128)(2,1)} %get-tuple-element.68.q, bf16[1024,512]{1,0:T(8,128)(2,1)} %get-tuple-element.69.k, bf16[1024,512]{1,0:T(8,128)(2,1)} %get-tuple-element.70.v, ...), custom_call_target="tpu_custom_call" | custom-call | tf_op jit(solution)/shard_map/attend/pallas_call | solution.py:122
  27.7 67.5 %middle.1 = (bf16[2,256,1024]{2,1,0:T(8,128)(2,1)}, f32[2,256,1024]{2,1,0:T(8,128)}, bf16[1024,512]{1,0:T(8,128)(2,1)}, bf16[18,128,1024]{2,1,0:T(8,128)(2,1)}, ...) custom-call(bf16[1024,512]{1,0:T(8,128)(2,1)} %get-tuple-element.71., ...), custom_call_target="tpu_custom_call" | custom-call | flops 30064771072 | bytes 31457280 | tf_op jit(solution)/shard_map/middle/pallas_call | solution.py:427
  95.1 0.6 collective-permute-start
  95.8 1.5 collective-permute-start.1
  97.2 22.2 %attend_back.1 = (bf16[2,8,512,512]{3,2,1,0:T(8,128)(2,1)}, bf16[1024,512]{1,0:T(8,128)(2,1)}, bf16[1024,512]{1,0:T(8,128)(2,1)}, bf16[1024,512]{1,0:T(8,128)(2,1)}) custom-call(s32[2]{0:T(128)} %lengths.3, bf16[1024,512]{1,0:T(8,128)(2,1)} %get-tuple-element.68.q, bf16[1024,512]{1,0:T(8,128)(2,1)} %get-tuple-element.69.k, ...), custom_call_target="tpu_custom_call" | custom-call | flops 10737418240 | bytes 25165824 | tf_op jit(solution)/shard_map/attend_back/pallas_call | solution.py:170
  119.4 13.6 %project_back.1 = (bf16[2,256,1024]{2,1,0:T(8,128)(2,1)}, bf16[1024,512]{1,0:T(8,128)(2,1)}, bf16[1024,512]{1,0:T(8,128)(2,1)}, bf16[1024,512]{1,0:T(8,128)(2,1)}, f32[2,512]{1,0:T(2,128)}) custom-call(bf16[1024,1024]{1,0:T(8,128)(2,1)} %get-tuple-element.76.rows, bf16[1024,512]{1,0:T(8,128)(2,1)} %get-tuple-element.79.dq, ...), custom_call_target="tpu_custom_call" | custom-call | flops 6442450944 | bytes 16777216 | tf_op jit(solution)/shard_map/project_back/pallas_call | solution.py:477
  133.0 0.0 collective-permute-done.refs_1_
  133.0 0.0 copy-start
  133.1 0.0 collective-permute-done.1.refs_2_
  133.1 0.0 copy-start.1
  133.1 1.0 copy-done
  134.1 0.4 copy-done.1
  134.5 150.8 %reduce_gradients.1 = (bf16[1024,2048]{1,0:T(8,128)(2,1)}, bf16[2048,1024]{1,0:T(8,128)(2,1)}, bf16[512,1024]{1,0:T(8,128)(2,1)}, bf16[1024,512]{1,0:T(8,128)(2,...) custom-call(bf16[18,128,1024]{2,1,0:T(8,128)(2,1)} %get-tuple-element.72.refs_0_, ...), custom_call_target="tpu_custom_call" | custom-call | tf_op jit(solution)/shard_map/reduce_gradients/pallas_call | solution.py:748
  285.3 15.6 %results.1 = (f32[1024,2048]{1,0:T(8,128)}, f32[2048,1024]{1,0:T(8,128)}, f32[512,1024]{1,0:T(8,128)}, f32[1024,512]{1,0:T(8,128)}, f32[1024,512]{1,0:T(8,128)},...) custom-call(bf16[1024,2048]{1,0:T(8,128)(2,1)} %get-tuple-element.89, ...), custom_call_target="tpu_custom_call" | custom-call | tf_op jit(solution)/shard_map/results/pallas_call | solution.py:788
Async XLA Ops:
  95.1 37.9 %collective-permute-start = (bf16[5,128,1024]{2,1,0:T(8,128)(2,1)}, bf16[5,128,1024]{2,1,0:T(8,128)(2,1)S(1)}, u32[]{:S(2)}, u32[]{:S(2)}) collective-permute-start(bf16[5,128,1024]{2,1,0:T(8,128)(2,1)} %get-tuple-element.73), channel_id=1, source_target_pairs={{0,1},{1,0},{2,3},{3,2},{4,5},{5,4},{6,7},{7,6},{8,9},{9,8},{10,11... | collective-permute-start | bytes 3932168 | tf_op jit(solution)/shard_map/ppermute | solution.py:812
  95.8 37.3 %collective-permute-start.1 = (bf16[5,128,1024]{2,1,0:T(8,128)(2,1)}, bf16[5,128,1024]{2,1,0:T(8,128)(2,1)S(1)}, u32[]{:S(2)}, u32[]{:S(2)}) collective-permute-start(bf16[5,128,1024]{2,1,0:T(8,128)(2,1)} %get-tuple-element.74), channel_id=1, source_target_pairs={{0,2},{1,3},{2,0},{3,1},{4,6},{5,7},{6,4},{7,5},{8,10},{9,11},{10,... | collective-permute-start | bytes 3932168 | tf_op jit(solution)/shard_map/ppermute | solution.py:812
  133.0 1.1 copy-start
  133.1 1.5 copy-start.1

commit v7 on v6

--- a/solution.py
+++ b/solution.py
@@ -197,8 +197,8 @@
 
 
 def middle_kernel(seqs, part, firsts, c, x, wo, wi, wf, b_output, gain1, shift1, b_outer, gain2, shift2, b_inner, gout,
-                  out, dz1, dc, keep, give_x, give_y, taken, small, g_bi,
-                  unit1, r1, dz2, hn, act, slope, df, du, da, give, got, own, sums, bsum, bi, give_f, sems, far_sems):
+                  out, dz1, dc, keep, give_x, give_y, quarter, small, g_bi,
+                  unit1, r1, hn, act, slope, df, du, da, give, got, own, sums, bsum, bi, keep_f, give_f, taken, sems, far_sems):
     me = lax.axis_index("head")
     other = 1 - me
     width = x.shape[2]
@@ -294,7 +294,7 @@
             out[s, rows, :] = (unit * gain2 + shift2).astype(BF16)
             g = gout[s, rows, :].astype(F32)
             d = norm_back(g, gain2, unit, r)
-            dz2[s, rows, :] = d
+            dz1[s, rows, :] = d
             df[at((2 * s + me) * part + i * sub, sub), :] = d.astype(BF16)
             sums[3] += fold(d)
             sums[4] += fold(g * unit)
@@ -309,20 +309,21 @@
     half = keep.shape[1]
     per = hidden // width
     side = give_f.shape[0] // 2
-    edge = give_x.shape[0] - side
-
-    def put(value, kept, axis, given, given_at):
+    edge = give_x.shape[0] - side - side // 2
+
+    def put(value, kept, axis, given):
         bit = (mine // (1 << firsts[axis])) % 2
+        size = value.shape[0] // 2
 
         @pl.when(bit == 0)
         def _():
-            keep[kept] = value[:half].astype(BF16)
-            given[given_at] = value[half:].astype(BF16)
+            kept[...] = value[:size].astype(BF16)
+            given[...] = value[size:].astype(BF16)
 
         @pl.when(bit == 1)
         def _():
-            keep[kept] = value[half:].astype(BF16)
-            given[given_at] = value[:half].astype(BF16)
+            kept[...] = value[size:].astype(BF16)
+            given[...] = value[:size].astype(BF16)
 
     def far_copy(i, axis):
         return pltpu.make_async_remote_copy(
@@ -330,13 +331,13 @@
             device_id={"batch": flip(mine, firsts[axis])}, device_id_type=MESH)
 
     def grads_outer():
-        for axis in range(2):
-            def give_outer(i, _, axis=axis):
+        def give_outer(i, _):
+            for axis in range(2):
                 chunk = axis * side + i
-                put(t_dot(act[:, at(chunk * 2 * half, 2 * half)], df[...]), 2 * side + chunk, axis, give_f, chunk)
+                put(t_dot(act[:, at(chunk * 2 * half, 2 * half)], df[...]), keep_f.at[chunk], axis, give_f.at[chunk])
                 far_copy(chunk, axis).start()
-                return 0
-            lax.fori_loop(0, side, give_outer, 0)
+            return 0
+        lax.fori_loop(0, side, give_outer, 0)
 
     def inner_back(s, p):
         rows = rows_of(s, p)
@@ -377,7 +378,7 @@
 
         def first_back(i, _):
             rows = at(i * sub, sub)
-            cot = dz2[s, rows, :] + (own[s, rows, :].astype(F32) + got[2, s, rows, :].astype(F32))
+            cot = dz1[s, rows, :] + (own[s, rows, :].astype(F32) + got[2, s, rows, :].astype(F32))
             unit = unit1[s, rows, :]
             d = norm_back(cot, gain1, unit, r1[s, rows, 0:1])
             dz1[s, rows, :] = d
@@ -393,7 +394,7 @@
     for axis in range(2):
         def give_inner(i, _, axis=axis):
             at_hn, at_du = at((axis * side + i) // per * 2 * half, 2 * half), at((axis * side + i) % per * width, width)
-            put(t_dot(hn[:, at_hn], du[:, at_du]), axis * side + i, axis, gives[axis], i)
+            put(t_dot(hn[:, at_hn], du[:, at_du]), keep.at[axis * side + i], axis, gives[axis].at[i])
             return 0
         lax.fori_loop(0, side, give_inner, 0)
 
@@ -404,14 +405,17 @@
     for axis in range(2):
         def give_output(i, _, axis=axis):
             cols = at((axis * edge + i) * 2 * half, 2 * half)
-            put(t_dot(c[:, cols], da[...]), 4 * side + axis * edge + i, axis, gives[axis], side + i)
+            put(t_dot(c[:, cols], da[...]), keep.at[2 * side + axis * edge + i], axis, gives[axis].at[side + i])
             return 0
         lax.fori_loop(0, edge, give_output, 0)
     small[...] = jnp.sum(sums[...], axis=1)
     g_bi[...] = jnp.sum(bsum[...], axis=0, keepdims=True)
     for axis in range(2):
         def far_done(i, _, axis=axis):
-            far_copy(axis * side + i, axis).wait()
+            chunk = axis * side + i
+            far_copy(chunk, axis).wait()
+            place = gives[1 - axis].at[side + edge + i // 2, at(i % 2 * (half // 2), half // 2)]
+            put(keep_f[chunk].astype(F32) + taken[chunk].astype(F32), quarter.at[chunk], 1 - axis, place)
             return 0
         lax.fori_loop(0, side, far_done, 0)
 
@@ -423,23 +427,24 @@
     sds = jax.ShapeDtypeStruct
     side, edge = hidden // rows // 2, cols // rows // 2
     halves = [sds((count, rows // 2, width), BF16)
-              for count in (4 * side + 2 * edge, side + edge, side + edge, 2 * side)]
+              for count in (2 * side + 2 * edge, side + edge + side // 2, side + edge + side // 2)]
+    halves.append(sds((2 * side, rows // 4, width), BF16))
     return pl.pallas_call(
         functools.partial(middle_kernel, seqs, part, firsts),
         out_shape=(sds(x.shape, BF16), sds(x.shape, F32), sds(c.shape, BF16),
                    *halves, sds((6, width), F32), sds((1, hidden), F32)),
-        in_specs=vmem(6 + len(vectors)), out_specs=(*vmem(6), pl.BlockSpec(memory_space=pl.ANY), *vmem(2)),
+        in_specs=vmem(6 + len(vectors)), out_specs=tuple(vmem(9)),
         scratch_shapes=[
-            pltpu.VMEM(x.shape, F32), pltpu.VMEM((seqs, part, 128), F32), pltpu.VMEM(x.shape, F32),
+            pltpu.VMEM(x.shape, F32), pltpu.VMEM((seqs, part, 128), F32),
             pltpu.VMEM((total, width), BF16), pltpu.VMEM((total, hidden), BF16), pltpu.VMEM((total, hidden), F32),
             pltpu.VMEM((total, width), BF16), pltpu.VMEM((total, hidden), BF16), pltpu.VMEM((total, width), BF16),
             pltpu.VMEM((3 * seqs, part, width), BF16), pltpu.VMEM((3, seqs, part, width), BF16),
             pltpu.VMEM(x.shape, BF16), pltpu.VMEM((6, 8, width), F32), pltpu.VMEM((8, hidden), F32),
             pltpu.VMEM((1, hidden), F32),
-            pltpu.VMEM((2 * side, rows // 2, width), BF16),
+            *[pltpu.VMEM((2 * side, rows // 2, width), BF16)] * 3,
             pltpu.SemaphoreType.DMA((2, 6 * seqs)), pltpu.SemaphoreType.DMA((2, 2 * side)),
         ],
-        compiler_params=pltpu.CompilerParams(collective_id=2, has_side_effects=True, vmem_limit_bytes=LIMIT),
+        compiler_params=pltpu.CompilerParams(collective_id=2, has_side_effects=True, vmem_limit_bytes=66 * 1000 * 1000),
         cost_estimate=pl.CostEstimate(flops=14 * total * width * hidden, transcendentals=total * hidden,
                                       bytes_accessed=30 << 20),
         name="middle",
@@ -485,8 +490,9 @@
     )(rows, dq, dk, dv, wq, wk, wv, dz1)
 LINE = 16
 ROWS = 256
-LATE_COLORS = (0, 1, 2, 3, 2, 3)
-PRECEDENCE = (4, 18, 28, 24, 6, 31, 14, 24, 33, 31, 35, 17, 18, 35, 27, 25, 9, 35, 23, 15, 35, 21, 35, 19)
+LATE_COLORS = (2, 3, 0, 1, 2, 0)
+LAG = 0.16
+PRECEDENCE = (22, 6, 15, 2, 35, 0, 7, 26, 35, 20, 25, 7, 20, 21, 9, 24, 29, 3, 10, 29, 34, 14, 14, 6)
 LANDS = ("gather", "out", "back_in", "back_mid", "back_out")
 
 
@@ -522,7 +528,6 @@
 
 def event_order(n, plans, rows):
     first, _ = grid_bits(n)
-    lag = 0.16
 
     def path(kind, b):
         place = kind.split("_")[-1]
@@ -537,7 +542,7 @@
                           for c, row in enumerate(work) if step[c] < len(row))
         link, span = work[c][step[c]]
         free[link] = start + span
-        ready[c] = free[link] + lag
+        ready[c] = free[link] + LAG
         events.append((start, c, step[c]))
         step[c] += 1
     events += [(r, c, len(work[c])) for c, r in enumerate(ready)]
@@ -574,6 +579,7 @@
     nc = len(plans)
     me, head = lax.axis_index("batch"), lax.axis_index("head")
     first, bits = grid_bits(n)
+    done = [0 if load is None else load[0] for load in loads]
     bit_of = [(me // (1 << b)) % 2 for b in range(bits)]
     z = me // (1 << first[2])
     side = z // 2
@@ -621,15 +627,18 @@
                 outside = grads[i + count - results].at[pl.ds(r, rows), pl.ds(col, span)]
                 yield pltpu.make_async_copy(outside, work.at[c, :, pl.ds(at, span)], load_sem.at[c, k])
         else:
-            kept, kept_at, given, given_at = loads[c]
-            keep, _, length, at = spans[c][0]
+            _, kept, kept_at, given, given_at, given_row = loads[c]
+            keep, _, length, at = spans[c][done[c] - 1]
             inside = work.at[c, pl.ds(pl.multiple_of(keep, 16), length)]
             yield pltpu.make_async_copy(grads[kept].at[kept_at], inside, load_sem.at[c, 0])
-            yield pltpu.make_async_copy(grads[given].at[given_at], got.at[c, pl.ds(at, length)], load_sem.at[c, 1])
-
-    for c in range(nc):
-        for move in moves(c, False):
-            move.start()
+            outside = grads[given].at[given_at, pl.ds(given_row, length)]
+            yield pltpu.make_async_copy(outside, got.at[c, pl.ds(at, length)], load_sem.at[c, 1])
+
+    events = [(c, s + done[c]) for c, s in event_order(n, [p[d:] for p, d in zip(plans, done)], rows)]
+    for c, s in events:
+        if s == done[c]:
+            for move in moves(c, False):
+                move.start()
     hold[...] = jnp.zeros_like(hold)
     hold[0:6, :] = small[...]
     width, row = hold.shape[1], 8
@@ -660,14 +669,14 @@
         kind = plans[c][s][0]
         keep, _, length, at = spans[c][s]
         sender, receiver = roles(kind)
-        if s == 0 and loads[c] is not None:
+        if s == done[c] - 1:
             for move in moves(c, False):
                 move.wait()
         else:
             only(sender, lambda: copy_of(c, s).wait_send())
 
         def take():
-            if s > 0 or loads[c] is None:
+            if s != done[c] - 1:
                 copy_of(c, s).wait_recv()
             if kind in LANDS:
                 return
@@ -696,8 +705,6 @@
         else:
             hold[...] += tiny_got[k]
 
-    done = [load is not None for load in loads]
-    events = [(c, s + done[c]) for c, s in event_order(n, [p[d:] for p, d in zip(plans, done)], rows)]
     gap = len(events) // (bits + 2)
     for e, (c, s) in enumerate(events):
         if s == 0:
@@ -727,14 +734,17 @@
     tiny_shape = (16, width)
     saves = chunk_pieces(shapes, ROWS, width)
     outer = early[3].shape[0]
-    edge = early[0].shape[0] - 2 * outer
-    slots, plans, loads = [0, 0], [], []
+    edge = early[0].shape[0] - outer
+    side = (outer + edge) // 2
+    plans, loads = [], []
     for which, count in enumerate((outer, outer, edge)):
         for c in range(count):
-            color = c * 2 // count
-            kept = which * outer + c
-            loads.append((0, kept, 3, c) if which == 1 else (0, kept, 1 + color, slots[color]))
-            slots[color] += which != 1
+            color, slot = c * 2 // count, c % (count // 2)
+            if which == 1:
+                loads.append((2, 3, c, 2 - color, side + slot // 2, slot % 2 * (ROWS // 4)))
+            else:
+                base = outer if which == 2 else 0
+                loads.append((1, 0, base + c, 1 + color, base // 2 + slot, 0))
             plans.append(chunk_plan(n, color, ROWS))
     for c in range(len(saves) - len(plans)):
         plans.append(chunk_plan(n, LATE_COLORS[c % len(LATE_COLORS)], ROWS))
@@ -807,7 +817,7 @@
     rows, q, k, v = project_rows(inputs, w_query, w_key, w_value, b_query, b_value)
     new_scores, context, norm = attend(lengths, q, k, v, prior_scores)
     firsts = grid_bits(n_batch)[0][:2]
-    outputs, dz1, dc, keep, *gives, far, small, g_bi = middle(
+    outputs, dz1, dc, keep, *gives, quarter, small, g_bi = middle(
         context, inputs, w_output, w_inner, w_outer, vectors, grad_out, firsts, ROWS)
     taken = [lax.ppermute(give, "batch", [(i, flip(i, first)) for i in range(n_batch)])
              for give, first in zip(gives, firsts)]
@@ -815,7 +825,7 @@
     grad_inputs, g_wq, g_wk, g_wv, g_b = project_back(rows, dq, dk, dv, w_query, w_key, w_value, dz1)
     late = (g_wq, g_wk, g_wv)
     shapes = [w_inner.shape, w_outer.shape, w_output.shape] + [g.shape for g in late]
-    grads, tiny = reduce_gradients((keep, *taken, far), late, shapes, (small, g_bi, g_b), n_batch)
+    grads, tiny = reduce_gradients((keep, *taken, quarter), late, shapes, (small, g_bi, g_b), n_batch)
     hidden, cols = g_bi.shape[1], g_b.shape[1]
     grads, (outputs, grad_inputs), vectors = results(grads, (outputs, grad_inputs), tiny, hidden, cols)
     g_wi, g_wf, g_wo, g_wq, g_wk, g_wv = grads

time: 302 us -> 294 us (0.974)
  Pallas kernels: 297 us -> 285 us
  waiting for transfers between devices: 0.01 us -> 5.99 us
    pallas_call x1, Pallas kernels: 151 us -> 139 us  [reduce_gradients(): pl.pallas_call(functools.partial(reduce_kernel, n, plans, ROWS, loads, sa...]
    ppermute x2, waiting for transfers between devices: 0.01 us -> 5.99 us  [on_device(): lax.ppermute(give, 'batch', [(i, flip(i, first)) for i in range(n_batch)])]
  transfers between devices with their start and end apart: 2 -> 2, of which waited for: 0 -> 2; matrix products, arithmetic and copies ran while one was open for 0% -> 0% of each run, Pallas kernels for 12% -> 12%
where the time goes in v7:
time: 294 us
  Pallas kernels  285 us (97%)
  waiting for transfers between devices  5.99 us (2%)
    pallas_call x1, Pallas kernels, reduce_gradients(): pl.pallas_call(functools.partial(reduce_kernel, n, plans, ROWS, loads, sa...  139 us
    pallas_call x1, Pallas kernels, middle(): pl.pallas_call(functools.partial(middle_kernel, seqs, part, firsts), out_...  67.4 us
    pallas_call x1, Pallas kernels, attend_back(): pl.pallas_call(functools.partial(attend_back_kernel, 256, pair // 2), gri...  22.2 us
    pallas_call x1, Pallas kernels, attend(): pl.pallas_call(functools.partial(attend_kernel, 256, pair // 2), grid_spe...  18.4 us
    pallas_call x1, Pallas kernels, results(): pl.pallas_call(functools.partial(results_kernel, len(grads), len(flat)),...  15.6 us
    pallas_call x1, Pallas kernels, project_back(): pl.pallas_call(functools.partial(project_back_kernel, seqs, part), out_sh...  13.6 us
    pallas_call x1, Pallas kernels, project_rows(): pl.pallas_call(functools.partial(project_kernel, seqs, part), out_shape=(...  8.54 us
    ppermute x2, waiting for transfers between devices, on_device(): lax.ppermute(give, 'batch', [(i, flip(i, first)) for i in range(n_batch)])  5.99 us
  transfers between devices with their start and end apart: 2, of which 2 were waited for; matrix products, arithmetic and copies ran while one was open for 0% of the time, Pallas kernels for 12%

profile of v7, /device:TPU:0, one launch (start us, length us, event | category | flops | bytes accessed | tf_op | source)
XLA Modules:
  0.0 294.0 jit_solution(11018112653230552816)
XLA Ops:
  0.7 8.5 %project_rows.1 = (bf16[1024,1024]{1,0:T(8,128)(2,1)}, bf16[1024,512]{1,0:T(8,128)(2,1)}, bf16[1024,512]{1,0:T(8,128)(2,1)}, bf16[1024,512]{1,0:T(8,128)(2,1)}) custom-call(bf16[2,256,1024]{2,1,0:T(8,128)(2,1)} %x.3, bf16[1024,512]{1,0:T(8,128)(2,1)} %wq.3, bf16[1024,512]{1,0:T(8,128)(2,1)} %wk.3, bf16[1024,512]{1,0:T(8,128)(2,1)} %wv.3, ...), custom_call_target="tpu_custom_call" | custom-call | tf_op jit(solution)/shard_map/project_rows/pallas_call | solution.py:82
  9.2 18.4 %attend.1 = (bf16[2,8,512,512]{3,2,1,0:T(8,128)(2,1)}, bf16[1024,512]{1,0:T(8,128)(2,1)}, f32[2,4,512,128]{3,2,1,0:T(8,128)}) custom-call(s32[2]{0:T(128)} %lengths.3, bf16[1024,512]{1,0:T(8,128)(2,1)} %get-tuple-element.68.q, bf16[1024,512]{1,0:T(8,128)(2,1)} %get-tuple-element.69.k, bf16[1024,512]{1,0:T(8,128)(2,1)} %get-tuple-element.70.v, ...), custom_call_target="tpu_custom_call" | custom-call | tf_op jit(solution)/shard_map/attend/pallas_call | solution.py:122
  27.6 67.4 %middle.1 = (bf16[2,256,1024]{2,1,0:T(8,128)(2,1)}, f32[2,256,1024]{2,1,0:T(8,128)}, bf16[1024,512]{1,0:T(8,128)(2,1)}, bf16[10,128,1024]{2,1,0:T(8,128)(2,1)}, ...) custom-call(bf16[1024,512]{1,0:T(8,128)(2,1)} %get-tuple-element.71., ...), custom_call_target="tpu_custom_call" | custom-call | flops 30064771072 | bytes 31457280 | tf_op jit(solution)/shard_map/middle/pallas_call | solution.py:432
  95.0 1.5 collective-permute-start
  96.5 0.5 collective-permute-start.1
  97.0 22.2 %attend_back.1 = (bf16[2,8,512,512]{3,2,1,0:T(8,128)(2,1)}, bf16[1024,512]{1,0:T(8,128)(2,1)}, bf16[1024,512]{1,0:T(8,128)(2,1)}, bf16[1024,512]{1,0:T(8,128)(2,1)}) custom-call(s32[2]{0:T(128)} %lengths.3, bf16[1024,512]{1,0:T(8,128)(2,1)} %get-tuple-element.68.q, bf16[1024,512]{1,0:T(8,128)(2,1)} %get-tuple-element.69.k, ...), custom_call_target="tpu_custom_call" | custom-call | flops 10737418240 | bytes 25165824 | tf_op jit(solution)/shard_map/attend_back/pallas_call | solution.py:170
  119.2 13.6 %project_back.1 = (bf16[2,256,1024]{2,1,0:T(8,128)(2,1)}, bf16[1024,512]{1,0:T(8,128)(2,1)}, bf16[1024,512]{1,0:T(8,128)(2,1)}, bf16[1024,512]{1,0:T(8,128)(2,1)}, f32[2,512]{1,0:T(2,128)}) custom-call(bf16[1024,1024]{1,0:T(8,128)(2,1)} %get-tuple-element.76.rows, bf16[1024,512]{1,0:T(8,128)(2,1)} %get-tuple-element.79.dq, ...), custom_call_target="tpu_custom_call" | custom-call | flops 6442450944 | bytes 16777216 | tf_op jit(solution)/shard_map/project_back/pallas_call | solution.py:482
  132.9 4.7 %collective-permute-done.refs_1_ = bf16[7,128,1024]{2,1,0:T(8,128)(2,1)S(1)} collective-permute-done((bf16[7,128,1024]{2,1,0:T(8,128)(2,1)}, bf16[7,128,1024]{2,1,0:T(8,128)(2,1)S(1)}, u32[]{:S(2)}, u32[]{:S(2)}) %collective-permute-start) | collective-permute-done | bytes 1835040 | tf_op jit(solution)/shard_map/ppermute | solution.py:822
  137.6 0.0 copy-start
  137.6 1.3 collective-permute-done.1.refs_2_
  138.9 0.0 copy-done
  138.9 139.3 %reduce_gradients.1 = (bf16[1024,2048]{1,0:T(8,128)(2,1)}, bf16[2048,1024]{1,0:T(8,128)(2,1)}, bf16[512,1024]{1,0:T(8,128)(2,1)}, bf16[1024,512]{1,0:T(8,128)(2,...) custom-call(bf16[10,128,1024]{2,1,0:T(8,128)(2,1)} %get-tuple-element.72.refs_0_, ...), custom_call_target="tpu_custom_call" | custom-call | tf_op jit(solution)/shard_map/reduce_gradients/pallas_call | solution.py:758
  278.2 15.6 %results.1 = (f32[1024,2048]{1,0:T(8,128)}, f32[2048,1024]{1,0:T(8,128)}, f32[512,1024]{1,0:T(8,128)}, f32[1024,512]{1,0:T(8,128)}, f32[1024,512]{1,0:T(8,128)},...) custom-call(bf16[1024,2048]{1,0:T(8,128)(2,1)} %get-tuple-element.89, ...), custom_call_target="tpu_custom_call" | custom-call | tf_op jit(solution)/shard_map/results/pallas_call | solution.py:798
Async XLA Ops:
  95.0 42.6 %collective-permute-start = (bf16[7,128,1024]{2,1,0:T(8,128)(2,1)}, bf16[7,128,1024]{2,1,0:T(8,128)(2,1)S(1)}, u32[]{:S(2)}, u32[]{:S(2)}) collective-permute-start(bf16[7,128,1024]{2,1,0:T(8,128)(2,1)} %get-tuple-element.73), channel_id=1, source_target_pairs={{0,1},{1,0},{2,3},{3,2},{4,5},{5,4},{6,7},{7,6},{8,9},{9,8},{10,11... | collective-permute-start | bytes 5505032 | tf_op jit(solution)/shard_map/ppermute | solution.py:822
  96.5 42.3 %collective-permute-start.1 = (bf16[7,128,1024]{2,1,0:T(8,128)(2,1)}, bf16[7,128,1024]{2,1,0:T(8,128)(2,1)}, u32[]{:S(2)}, u32[]{:S(2)}) collective-permute-start(bf16[7,128,1024]{2,1,0:T(8,128)(2,1)} %get-tuple-element.74), channel_id=1, source_target_pairs={{0,2},{1,3},{2,0},{3,1},{4,6},{5,7},{6,4},{7,5},{8,10},{9,11},{10,... | collective-permute-start | bytes 5505032 | tf_op jit(solution)/shard_map/ppermute | solution.py:822
  137.6 1.3 copy-start

commit v8 on v7

--- a/solution.py
+++ b/solution.py
@@ -38,6 +38,10 @@
 
 def vmem(count):
     return [pl.BlockSpec(memory_space=pltpu.VMEM)] * count
+
+
+def hbm(count):
+    return [pl.BlockSpec(memory_space=pl.ANY)] * count
 
 
 def as_row(vector):
@@ -106,8 +110,7 @@
             top = jnp.max(masked, axis=-1, keepdims=True)
             terms = jnp.exp(masked - top)
             total = jnp.sum(terms, axis=-1, keepdims=True)
-            probs = (terms * (1.0 / total)).astype(BF16)
-            parts.append(dot(probs, v[...]))
+            parts.append(dot(terms.astype(BF16), v[...]) * (1.0 / total))
             norms.append(top + jnp.log(total))
         c[rows, :] = jnp.where(first, parts[0], parts[1]).astype(BF16)
         norm[0, 0, rows, :] = jnp.where(first, norms[0], norms[1])
@@ -120,7 +123,7 @@
     big = pl.BlockSpec((1, 2, full, full), lambda s, h, n: (s, h, 0, 0))
     norm = pl.BlockSpec((1, 1, full, pair), lambda s, h, n: (s, h, 0, 0))
     return pl.pallas_call(
-        functools.partial(attend_kernel, 256, pair // 2),
+        functools.partial(attend_kernel, full, pair // 2),
         grid_spec=pltpu.PrefetchScalarGridSpec(
             num_scalar_prefetch=1, grid=(seqs, heads // 2),
             in_specs=[rows, rows, rows, big], out_specs=(big, rows, norm)),
@@ -168,7 +171,7 @@
     norms = pl.BlockSpec((1, 1, full, pair), lambda s, h, n: (s, h, 0, 0))
     flat = jax.ShapeDtypeStruct(q.shape, BF16)
     return pl.pallas_call(
-        functools.partial(attend_back_kernel, 256, pair // 2),
+        functools.partial(attend_back_kernel, full, pair // 2),
         grid_spec=pltpu.PrefetchScalarGridSpec(
             num_scalar_prefetch=1, grid=(seqs, heads // 2),
             in_specs=[rows, rows, rows, rows, big, norms, big], out_specs=(big, rows, rows, rows)),
@@ -196,15 +199,21 @@
     return r * (e - jnp.mean(e, axis=-1, keepdims=True) - unit * jnp.mean(e * unit, axis=-1, keepdims=True))
 
 
-def middle_kernel(seqs, part, firsts, c, x, wo, wi, wf, b_output, gain1, shift1, b_outer, gain2, shift2, b_inner, gout,
-                  out, dz1, dc, keep, give_x, give_y, quarter, small, g_bi,
-                  unit1, r1, hn, act, slope, df, du, da, give, got, own, sums, bsum, bi, keep_f, give_f, taken, sems, far_sems):
+def middle_kernel(seqs, part, firsts, c, x, wo, wi_far, wf_far, b_output, gain1, shift1, b_outer, gain2, shift2, b_inner, gout_far,
+                  out_far, dz1_far, dc, keep, give_x, give_y, quarter, small, g_bi,
+                  unit1, r1, hn, act, slope, df, du, da, give, got, own, sums, bsum, bi, keep_f, give_f, taken, wi, wf, gout, out, dz1, sems, far_sems, own_sems):
     me = lax.axis_index("head")
     other = 1 - me
     width = x.shape[2]
     hidden = wi.shape[1]
     tile = 512
     sub = 64
+    fetch_wi, fetch_wf, fetch_gout, store_out, store_dz1 = [
+        pltpu.make_async_copy(src, dst, own_sems.at[i]) for i, (src, dst) in enumerate(
+            ((wi_far, wi), (wf_far, wf), (gout_far, gout), (out, out_far), (dz1, dz1_far)))]
+    fetch_wi.start()
+    fetch_wf.start()
+    fetch_gout.start()
     barrier = pltpu.get_barrier_semaphore()
     pl.semaphore_signal(barrier, inc=1, device_id={"head": other}, device_id_type=MESH)
     for first in firsts:
@@ -276,13 +285,18 @@
             for q in range(seqs):
                 block = hn.at[rows_of(q, me)]
                 to_partner(block, block, sems, seqs + q, other).wait()
+        if n == 0:
+            fetch_wi.wait()
         inner(s, p)
+        if n == 0:
+            fetch_wf.wait()
         if p is other:
             outer(s, p, give.at[pl.ds(seqs, seqs)])
             to_partner(give.at[seqs + s], got.at[1, s], sems, 2 * seqs + s, other).start()
         else:
             outer(s, p, own)
 
+    fetch_gout.wait()
     for s in range(seqs):
         to_partner(give.at[seqs + s], got.at[1, s], sems, 2 * seqs + s, other).wait()
 
@@ -304,6 +318,8 @@
         block = df.at[rows_of(s, me)]
         to_partner(block, block, sems, 3 * seqs + s, other).start()
 
+    store_out.start()
+
     mine = lax.axis_index("batch")
     gives = (give_x, give_y)
     half = keep.shape[1]
@@ -391,6 +407,7 @@
         block = da.at[rows_of(s, me)]
         to_partner(block, block, sems, 5 * seqs + s, other).start()
 
+    store_dz1.start()
     for axis in range(2):
         def give_inner(i, _, axis=axis):
             at_hn, at_du = at((axis * side + i) // per * 2 * half, 2 * half), at((axis * side + i) % per * width, width)
@@ -418,6 +435,8 @@
             put(keep_f[chunk].astype(F32) + taken[chunk].astype(F32), quarter.at[chunk], 1 - axis, place)
             return 0
         lax.fori_loop(0, side, far_done, 0)
+    store_out.wait()
+    store_dz1.wait()
 
 
 def middle(c, x, wo, wi, wf, vectors, gout, firsts, rows):
@@ -433,7 +452,7 @@
         functools.partial(middle_kernel, seqs, part, firsts),
         out_shape=(sds(x.shape, BF16), sds(x.shape, F32), sds(c.shape, BF16),
                    *halves, sds((6, width), F32), sds((1, hidden), F32)),
-        in_specs=vmem(6 + len(vectors)), out_specs=tuple(vmem(9)),
+        in_specs=vmem(3) + hbm(2) + vmem(len(vectors)) + hbm(1), out_specs=tuple(hbm(2) + vmem(7)),
         scratch_shapes=[
             pltpu.VMEM(x.shape, F32), pltpu.VMEM((seqs, part, 128), F32),
             pltpu.VMEM((total, width), BF16), pltpu.VMEM((total, hidden), BF16), pltpu.VMEM((total, hidden), F32),
@@ -442,7 +461,9 @@
             pltpu.VMEM(x.shape, BF16), pltpu.VMEM((6, 8, width), F32), pltpu.VMEM((8, hidden), F32),
             pltpu.VMEM((1, hidden), F32),
             *[pltpu.VMEM((2 * side, rows // 2, width), BF16)] * 3,
-            pltpu.SemaphoreType.DMA((2, 6 * seqs)), pltpu.SemaphoreType.DMA((2, 2 * side)),
+            pltpu.VMEM(wi.shape, BF16), pltpu.VMEM(wf.shape, BF16), pltpu.VMEM(x.shape, BF16),
+            pltpu.VMEM(x.shape, BF16), pltpu.VMEM(x.shape, F32),
+            pltpu.SemaphoreType.DMA((2, 6 * seqs)), pltpu.SemaphoreType.DMA((2, 2 * side)), pltpu.SemaphoreType.DMA((5,)),
         ],
         compiler_params=pltpu.CompilerParams(collective_id=2, has_side_effects=True, vmem_limit_bytes=66 * 1000 * 1000),
         cost_estimate=pl.CostEstimate(flops=14 * total * width * hidden, transcendentals=total * hidden,
@@ -754,7 +775,6 @@
     _, bits = grid_bits(n)
     got_rows = max(sum(size for kind, _, size in plan if kind not in LANDS) for plan in plans)
     grads = (*early, *late)
-    hbm = lambda k: [pl.BlockSpec(memory_space=pl.ANY)] * k
     done = pl.pallas_call(
         functools.partial(reduce_kernel, n, plans, ROWS, loads, saves, len(grads), len(shapes)),
         out_shape=(*(jax.ShapeDtypeStruct(shape, BF16) for shape in shapes), jax.ShapeDtypeStruct(tiny_shape, F32)),
@@ -791,7 +811,7 @@
             dst[...] = tiny[row + at // tiny.shape[1], pl.ds(at % tiny.shape[1], dst.shape[0])]
 
 
-def results(grads, rows, tiny, hidden, cols, steps=8):
+def results(grads, rows, tiny, hidden, cols, steps=4):
     flat = [r.reshape(-1, r.shape[-1]) for r in rows]
     blocks = [pl.BlockSpec((a.shape[0] // steps, a.shape[1]), lambda i: (i, 0)) for a in (*grads, *flat)]
     vectors = [tiny.shape[1]] * 6 + [hidden, cols, cols]

time: 294 us -> 285 us (0.969)
  Pallas kernels: 285 us -> 273 us
  waiting for transfers between devices: 5.99 us -> 9.16 us
    pallas_call x2, Pallas kernels: 40.6 us -> 32.3 us  [the longest x1 19 us: attend_back(): pl.pallas_call(functools.partial(attend_back_kernel, full, pair // 2), gr...]
    pallas_call x1, Pallas kernels: 67.4 us -> 63.9 us  [middle(): pl.pallas_call(functools.partial(middle_kernel, seqs, part, firsts), out_...]
    ppermute x2, waiting for transfers between devices: 5.99 us -> 9.16 us  [on_device(): lax.ppermute(give, 'batch', [(i, flip(i, first)) for i in range(n_batch)])]
  transfers between devices with their start and end apart: 2 -> 2, of which waited for: 2 -> 2; matrix products, arithmetic and copies ran while one was open for 0% -> 0% of each run, Pallas kernels for 12% -> 11%
where the time goes in v8:
time: 285 us
  Pallas kernels  273 us (96%)
  waiting for transfers between devices  9.16 us (3%)
    pallas_call x1, Pallas kernels, reduce_gradients(): pl.pallas_call(functools.partial(reduce_kernel, n, plans, ROWS, loads, sa...  139 us
    pallas_call x1, Pallas kernels, middle(): pl.pallas_call(functools.partial(middle_kernel, seqs, part, firsts), out_...  63.9 us
    pallas_call x1, Pallas kernels, attend_back(): pl.pallas_call(functools.partial(attend_back_kernel, full, pair // 2), gr...  19 us
    pallas_call x1, Pallas kernels, results(): pl.pallas_call(functools.partial(results_kernel, len(grads), len(flat)),...  14.9 us
    pallas_call x1, Pallas kernels, project_back(): pl.pallas_call(functools.partial(project_back_kernel, seqs, part), out_sh...  13.6 us
    pallas_call x1, Pallas kernels, attend(): pl.pallas_call(functools.partial(attend_kernel, full, pair // 2), grid_sp...  13.3 us
    ppermute x2, waiting for transfers between devices, on_device(): lax.ppermute(give, 'batch', [(i, flip(i, first)) for i in range(n_batch)])  9.16 us
    pallas_call x1, Pallas kernels, project_rows(): pl.pallas_call(functools.partial(project_kernel, seqs, part), out_shape=(...  8.54 us
  transfers between devices with their start and end apart: 2, of which 2 were waited for; matrix products, arithmetic and copies ran while one was open for 0% of the time, Pallas kernels for 11%

profile of v8, /device:TPU:0, one launch (start us, length us, event | category | flops | bytes accessed | tf_op | source)
XLA Modules:
  0.0 284.6 jit_solution(9621517286993921341)
XLA Ops:
  0.7 8.5 %project_rows.1 = (bf16[1024,1024]{1,0:T(8,128)(2,1)}, bf16[1024,512]{1,0:T(8,128)(2,1)}, bf16[1024,512]{1,0:T(8,128)(2,1)}, bf16[1024,512]{1,0:T(8,128)(2,1)}) custom-call(bf16[2,256,1024]{2,1,0:T(8,128)(2,1)} %x.3, bf16[1024,512]{1,0:T(8,128)(2,1)} %wq.3, bf16[1024,512]{1,0:T(8,128)(2,1)} %wk.3, bf16[1024,512]{1,0:T(8,128)(2,1)} %wv.3, ...), custom_call_target="tpu_custom_call" | custom-call | tf_op jit(solution)/shard_map/project_rows/pallas_call | solution.py:86
  9.2 13.3 %attend.1 = (bf16[2,8,512,512]{3,2,1,0:T(8,128)(2,1)}, bf16[1024,512]{1,0:T(8,128)(2,1)}, f32[2,4,512,128]{3,2,1,0:T(8,128)}) custom-call(s32[2]{0:T(128)} %lengths.3, bf16[1024,512]{1,0:T(8,128)(2,1)} %get-tuple-element.68.q, bf16[1024,512]{1,0:T(8,128)(2,1)} %get-tuple-element.69.k, bf16[1024,512]{1,0:T(8,128)(2,1)} %get-tuple-element.70.v, ...), custom_call_target="tpu_custom_call" | custom-call | tf_op jit(solution)/shard_map/attend/pallas_call | solution.py:125
  22.5 63.9 %middle.1 = (bf16[2,256,1024]{2,1,0:T(8,128)(2,1)}, f32[2,256,1024]{2,1,0:T(8,128)}, bf16[1024,512]{1,0:T(8,128)(2,1)}, bf16[10,128,1024]{2,1,0:T(8,128)(2,1)}, ...) custom-call(bf16[1024,512]{1,0:T(8,128)(2,1)} %get-tuple-element.71., ...), custom_call_target="tpu_custom_call" | custom-call | flops 30064771072 | bytes 31457280 | tf_op jit(solution)/shard_map/middle/pallas_call | solution.py:451
  86.4 1.5 collective-permute-start
  87.9 0.5 collective-permute-start.1
  88.4 19.0 %attend_back.1 = (bf16[2,8,512,512]{3,2,1,0:T(8,128)(2,1)}, bf16[1024,512]{1,0:T(8,128)(2,1)}, bf16[1024,512]{1,0:T(8,128)(2,1)}, bf16[1024,512]{1,0:T(8,128)(2,1)}) custom-call(s32[2]{0:T(128)} %lengths.3, bf16[1024,512]{1,0:T(8,128)(2,1)} %get-tuple-element.68.q, bf16[1024,512]{1,0:T(8,128)(2,1)} %get-tuple-element.69.k, ...), custom_call_target="tpu_custom_call" | custom-call | flops 10737418240 | bytes 25165824 | tf_op jit(solution)/shard_map/attend_back/pallas_call | solution.py:173
  107.4 13.6 %project_back.1 = (bf16[2,256,1024]{2,1,0:T(8,128)(2,1)}, bf16[1024,512]{1,0:T(8,128)(2,1)}, bf16[1024,512]{1,0:T(8,128)(2,1)}, bf16[1024,512]{1,0:T(8,128)(2,1)}, f32[2,512]{1,0:T(2,128)}) custom-call(bf16[1024,1024]{1,0:T(8,128)(2,1)} %get-tuple-element.76.rows, bf16[1024,512]{1,0:T(8,128)(2,1)} %get-tuple-element.79.dq, ...), custom_call_target="tpu_custom_call" | custom-call | flops 6442450944 | bytes 16777216 | tf_op jit(solution)/shard_map/project_back/pallas_call | solution.py:503
  121.0 7.9 %collective-permute-done.refs_1_ = bf16[7,128,1024]{2,1,0:T(8,128)(2,1)S(1)} collective-permute-done((bf16[7,128,1024]{2,1,0:T(8,128)(2,1)}, bf16[7,128,1024]{2,1,0:T(8,128)(2,1)S(1)}, u32[]{:S(2)}, u32[]{:S(2)}) %collective-permute-start) | collective-permute-done | bytes 1835040 | tf_op jit(solution)/shard_map/ppermute | solution.py:842
  128.9 0.0 copy-start
  128.9 1.3 collective-permute-done.1.refs_2_
  130.2 0.0 copy-done
  130.2 139.4 %reduce_gradients.1 = (bf16[1024,2048]{1,0:T(8,128)(2,1)}, bf16[2048,1024]{1,0:T(8,128)(2,1)}, bf16[512,1024]{1,0:T(8,128)(2,1)}, bf16[1024,512]{1,0:T(8,128)(2,...) custom-call(bf16[10,128,1024]{2,1,0:T(8,128)(2,1)} %get-tuple-element.72.refs_0_, ...), custom_call_target="tpu_custom_call" | custom-call | tf_op jit(solution)/shard_map/reduce_gradients/pallas_call | solution.py:778
  269.6 14.9 %results.1 = (f32[1024,2048]{1,0:T(8,128)}, f32[2048,1024]{1,0:T(8,128)}, f32[512,1024]{1,0:T(8,128)}, f32[1024,512]{1,0:T(8,128)}, f32[1024,512]{1,0:T(8,128)},...) custom-call(bf16[1024,2048]{1,0:T(8,128)(2,1)} %get-tuple-element.89, ...), custom_call_target="tpu_custom_call" | custom-call | tf_op jit(solution)/shard_map/results/pallas_call | solution.py:818
Async XLA Ops:
  86.4 42.6 %collective-permute-start = (bf16[7,128,1024]{2,1,0:T(8,128)(2,1)}, bf16[7,128,1024]{2,1,0:T(8,128)(2,1)S(1)}, u32[]{:S(2)}, u32[]{:S(2)}) collective-permute-start(bf16[7,128,1024]{2,1,0:T(8,128)(2,1)} %get-tuple-element.73), channel_id=1, source_target_pairs={{0,1},{1,0},{2,3},{3,2},{4,5},{5,4},{6,7},{7,6},{8,9},{9,8},{10,11... | collective-permute-start | bytes 5505032 | tf_op jit(solution)/shard_map/ppermute | solution.py:842
  87.9 42.3 %collective-permute-start.1 = (bf16[7,128,1024]{2,1,0:T(8,128)(2,1)}, bf16[7,128,1024]{2,1,0:T(8,128)(2,1)}, u32[]{:S(2)}, u32[]{:S(2)}) collective-permute-start(bf16[7,128,1024]{2,1,0:T(8,128)(2,1)} %get-tuple-element.74), channel_id=1, source_target_pairs={{0,2},{1,3},{2,0},{3,1},{4,6},{5,7},{6,4},{7,5},{8,10},{9,11},{10,... | collective-permute-start | bytes 5505032 | tf_op jit(solution)/shard_map/ppermute | solution.py:842
  128.9 1.3 copy-start
